TPU v7x, 32 devices: a whole 2x2x4 slice. The times are simulated.
32 devices in a mesh: shard: 4 (over y, x), ctx: 8 (over z, core).
Axes of the slice: x: 2, y: 2, z: 4, core: 2. Of those that a mesh axis runs over, the one named last changes fastest.
Arguments:
- tokens: bfloat16 [16, 1024, 1152], P('shard', 'ctx'), may hold values from -6 to 6
- cotangent: bfloat16 [16, 1024, 1152], P('shard', 'ctx'), may hold values from -6 to 6
- pictures: int32 [16, 2], P('shard'), may hold values from 0 to 768, as said below
- w_query: bfloat16 [1152, 1024], P('shard'), may hold values from -0.1875 to 0.1875
- w_key: bfloat16 [1152, 256], P('shard'), may hold values from -0.1875 to 0.1875
- w_value: bfloat16 [1152, 256], P('shard'), may hold values from -0.1875 to 0.1875
- w_out: bfloat16 [1024, 1152], P('shard'), may hold values from -0.1875 to 0.1875
- w_gate: bfloat16 [1152, 6912], P('shard'), may hold values from -0.1875 to 0.1875
- w_up: bfloat16 [1152, 6912], P('shard'), may hold values from -0.1875 to 0.1875
- w_down: bfloat16 [6912, 1152], P('shard'), may hold values from -0.078125 to 0.078125
- g_attn_in: float32 [1152], P('shard'), may hold values from 0.5 to 1.5
- g_attn_out: float32 [1152], P('shard'), may hold values from 0.5 to 1.5
- g_ffn_in: float32 [1152], P('shard'), may hold values from 0.5 to 1.5
- g_ffn_out: float32 [1152], P('shard'), may hold values from 0.5 to 1.5
- g_query: float32 [256], P('shard'), may hold values from 0.5 to 1.5
- g_key: float32 [256], P('shard'), may hold values from 0.5 to 1.5
Outputs:
- output: bfloat16 [16, 1024, 1152], P('shard', 'ctx')
- input_grad: bfloat16 [16, 1024, 1152], P('shard', 'ctx')
- grad_w_query: float32 [1152, 1024], P('shard')
- grad_w_key: float32 [1152, 256], P('shard')
- grad_w_value: float32 [1152, 256], P('shard')
- grad_w_out: float32 [1024, 1152], P('shard')
- grad_w_gate: float32 [1152, 6912], P('shard')
- grad_w_up: float32 [1152, 6912], P('shard')
- grad_w_down: float32 [6912, 1152], P('shard')
- grad_g_attn_in: float32 [1152], P('shard')
- grad_g_attn_out: float32 [1152], P('shard')
- grad_g_ffn_in: float32 [1152], P('shard')
- grad_g_ffn_out: float32 [1152], P('shard')
- grad_g_query: float32 [256], P('shard')
- grad_g_key: float32 [256], P('shard')
Inputs may be any that keep to these rules, and one draw needn't show every extreme that they name: `pictures`: piece j of a sequence lies wholly within the j-th of its 2 equal parts of 512 tokens, so pieces never meet.
All inputs are finite; a program needn't handle non-finite values.
Results may differ from a plain program's by a relative error of at most 0.04.
Values may be sent and summed in bfloat16 or wider, within the bound.
No kernel may reach another device: no remote copies, remote signals or barrier semaphores. Data moves between devices by JAX's collectives and lax.ppermute only.
A program may use at most 320 MiB of HBM per device.

v0:
```python
import jax
import jax.numpy as jnp
from jax import lax
from jax.sharding import PartitionSpec as P

HEADS = 4
HD = 256
PIECE = 256


epsilon = 1e-06
rope_base = 1000000.0
score_scale = 0.0625


def normed(values_in, gain_vec):
    return (
        values_in
        * lax.rsqrt(jnp.mean(values_in * values_in, axis=-1, keepdims=True) + epsilon)
        * gain_vec
    )


def angles(positions, head_width):
    half_width = head_width // 2
    inverse = jnp.exp(
        -(jnp.arange(half_width).astype(jnp.float32) * 2.0 / head_width)
        * jnp.log(jnp.float32(rope_base))
    )
    return positions[:, None] * inverse[None, :]


def rotated(values_in, angle_table):
    half_width = values_in.shape[-1] // 2
    cosine = jnp.cos(angle_table)
    sine_part = jnp.sin(angle_table)
    front_half = values_in[..., :half_width]
    back_half = values_in[..., half_width:]
    return jnp.concatenate(
        [front_half * cosine - back_half * sine_part, back_half * cosine + front_half * sine_part],
        axis=-1,
    )


def allowed(query_pos, key_pos, starts):
    causal = key_pos[None, :] <= query_pos[:, None]
    inside_query = (query_pos[:, None] >= starts[None, :]) & (
        query_pos[:, None] < starts[None, :] + PIECE
    )
    inside_key = (key_pos[:, None] >= starts[None, :]) & (
        key_pos[:, None] < starts[None, :] + PIECE
    )
    shared = jnp.any(inside_query[:, None, :] & inside_key[None, :, :], axis=-1)
    return causal | shared


def geglu(gate_act, up_act):
    return jax.nn.gelu(gate_act, approximate=True) * up_act


def norm_rope(raw_rows, gain_vec, angle_table):
    return rotated(normed(raw_rows, gain_vec), angle_table)


def norm_back(values_in, gain_vec, grad_rows):
    return jax.vjp(normed, values_in, gain_vec)[1](grad_rows)


def body(
    tokens,
    cotangent,
    pictures,
    w_query,
    w_key,
    w_value,
    w_out,
    w_gate,
    w_up,
    w_down,
    g_attn_in,
    g_attn_out,
    g_ffn_in,
    g_ffn_out,
    g_query,
    g_key,
):
    (
        w_query,
        w_key,
        w_value,
        w_out,
        w_gate,
        w_up,
        w_down,
        g_attn_in,
        g_attn_out,
        g_ffn_in,
        g_ffn_out,
        g_query,
        g_key,
    ) = (
        lax.all_gather(w_query, "shard", axis=0, tiled=True),
        lax.all_gather(w_key, "shard", axis=0, tiled=True),
        lax.all_gather(w_value, "shard", axis=0, tiled=True),
        lax.all_gather(w_out, "shard", axis=0, tiled=True),
        lax.all_gather(w_gate, "shard", axis=0, tiled=True),
        lax.all_gather(w_up, "shard", axis=0, tiled=True),
        lax.all_gather(w_down, "shard", axis=0, tiled=True),
        lax.all_gather(g_attn_in.astype(jnp.bfloat16), "shard", axis=0, tiled=True).astype(
            g_attn_in.dtype
        ),
        lax.all_gather(g_attn_out.astype(jnp.bfloat16), "shard", axis=0, tiled=True).astype(
            g_attn_out.dtype
        ),
        lax.all_gather(g_ffn_in.astype(jnp.bfloat16), "shard", axis=0, tiled=True).astype(
            g_ffn_in.dtype
        ),
        lax.all_gather(g_ffn_out.astype(jnp.bfloat16), "shard", axis=0, tiled=True).astype(
            g_ffn_out.dtype
        ),
        lax.all_gather(g_query.astype(jnp.bfloat16), "shard", axis=0, tiled=True).astype(
            g_query.dtype
        ),
        lax.all_gather(g_key.astype(jnp.bfloat16), "shard", axis=0, tiled=True).astype(g_key.dtype),
    )
    local_seqs, local_len, model_width = tokens.shape
    row_count = local_seqs * local_len
    seq_len = local_len * lax.axis_size("ctx")
    query_pos = lax.axis_index("ctx") * local_len + jnp.arange(local_len, dtype=jnp.int32)
    key_pos = jnp.arange(seq_len, dtype=jnp.int32)
    angle_rows = jnp.tile(angles(query_pos.astype(jnp.float32), HD), (local_seqs, 1))
    x_rows = tokens.reshape(row_count, model_width).astype(jnp.float32)
    normal_in = normed(x_rows, g_attn_in).astype(jnp.bfloat16)
    query_raw = jnp.dot(normal_in, w_query, preferred_element_type=jnp.float32).reshape(
        row_count, HEADS, HD
    )
    key_raw = jnp.dot(normal_in, w_key, preferred_element_type=jnp.float32)
    value_raw = jnp.dot(normal_in, w_value, preferred_element_type=jnp.float32)
    queries = norm_rope(query_raw, g_query, angle_rows[:, None, :]).astype(jnp.bfloat16)
    key_local = norm_rope(key_raw, g_key, angle_rows).astype(jnp.bfloat16)
    value_local = value_raw.astype(jnp.bfloat16)
    key_all, value_all = (
        lax.all_gather(key_local.reshape(local_seqs, local_len, HD), "ctx", axis=1, tiled=True),
        lax.all_gather(value_local.reshape(local_seqs, local_len, HD), "ctx", axis=1, tiled=True),
    )
    query_seq = queries.reshape(local_seqs, local_len, HEADS, HD)

    def attend_forward(sequence_item):
        query_block, key_block, value_block, starts = sequence_item
        permitted = allowed(query_pos, key_pos, starts)
        scores = (
            jnp.einsum("chd,kd->hck", query_block, key_block, preferred_element_type=jnp.float32)
            * score_scale
        )
        scores = jnp.where(permitted[None], scores, -1e30)
        peak_score = jnp.max(scores, axis=-1, keepdims=True)
        exponent = jnp.exp(scores - peak_score)
        totals = jnp.sum(exponent, axis=-1, keepdims=True)
        softmaxed = (exponent / totals).astype(jnp.bfloat16)
        mixed_block = jnp.einsum(
            "hck,kd->chd", softmaxed, value_block, preferred_element_type=jnp.float32
        )
        return (mixed_block, (peak_score + jnp.log(totals))[..., 0])

    mixed_heads, log_totals = lax.map(attend_forward, (query_seq, key_all, value_all, pictures))
    mixed_flat = mixed_heads.reshape(row_count, HEADS * HD).astype(jnp.bfloat16)
    attn_out = jnp.dot(mixed_flat, w_out, preferred_element_type=jnp.float32)
    residual = x_rows + normed(attn_out, g_attn_out)
    normal_ffn = normed(residual, g_ffn_in).astype(jnp.bfloat16)
    gate_act = jnp.dot(normal_ffn, w_gate, preferred_element_type=jnp.float32)
    up_act = jnp.dot(normal_ffn, w_up, preferred_element_type=jnp.float32)
    hidden = geglu(gate_act, up_act).astype(jnp.bfloat16)
    branch = jnp.dot(hidden, w_down, preferred_element_type=jnp.float32)
    output = (
        (residual + normed(branch, g_ffn_out))
        .astype(jnp.bfloat16)
        .reshape(local_seqs, local_len, model_width)
    )
    grad_rows = cotangent.reshape(row_count, model_width).astype(jnp.float32)
    branch_grad, grad_g_ffn_out = norm_back(branch, g_ffn_out, grad_rows)
    branch_low = branch_grad.astype(jnp.bfloat16)
    grad_w_down = jnp.einsum("nf,nd->fd", hidden, branch_low, preferred_element_type=jnp.float32)
    hidden_grad = jnp.einsum("nd,fd->nf", branch_low, w_down, preferred_element_type=jnp.float32)
    gate_grad, up_grad = jax.vjp(geglu, gate_act, up_act)[1](hidden_grad)
    gate_grad = gate_grad.astype(jnp.bfloat16)
    up_grad = up_grad.astype(jnp.bfloat16)
    grad_w_gate = jnp.einsum("nd,nf->df", normal_ffn, gate_grad, preferred_element_type=jnp.float32)
    grad_w_up = jnp.einsum("nd,nf->df", normal_ffn, up_grad, preferred_element_type=jnp.float32)
    normal_ffn_grad = jnp.einsum(
        "nf,df->nd", gate_grad, w_gate, preferred_element_type=jnp.float32
    ) + jnp.einsum("nf,df->nd", up_grad, w_up, preferred_element_type=jnp.float32)
    residual_part, grad_g_ffn_in = norm_back(residual, g_ffn_in, normal_ffn_grad)
    residual_grad = grad_rows + residual_part
    attn_grad, grad_g_attn_out = norm_back(attn_out, g_attn_out, residual_grad)
    attn_grad = attn_grad.astype(jnp.bfloat16)
    grad_w_out = jnp.einsum("nf,nd->fd", mixed_flat, attn_grad, preferred_element_type=jnp.float32)
    mixed_grad = (
        jnp.einsum("nd,fd->nf", attn_grad, w_out, preferred_element_type=jnp.float32)
        .astype(jnp.bfloat16)
        .reshape(local_seqs, local_len, HEADS, HD)
    )

    def attend_backward(sequence_item):
        query_block, key_block, value_block, starts, log_total, mixed_block_grad = sequence_item
        permitted = allowed(query_pos, key_pos, starts)
        scores = (
            jnp.einsum("chd,kd->hck", query_block, key_block, preferred_element_type=jnp.float32)
            * score_scale
        )
        scores = jnp.where(permitted[None], scores, -1e30)
        weights_back = jnp.exp(scores - log_total[..., None])
        prob_grad = jnp.einsum(
            "chd,kd->hck", mixed_block_grad, value_block, preferred_element_type=jnp.float32
        )
        row_inner = jnp.sum(weights_back * prob_grad, axis=-1, keepdims=True)
        score_grad = (weights_back * (prob_grad - row_inner)).astype(jnp.bfloat16)
        query_part = (
            jnp.einsum("hck,kd->chd", score_grad, key_block, preferred_element_type=jnp.float32)
            * score_scale
        )
        key_part = (
            jnp.einsum("hck,chd->kd", score_grad, query_block, preferred_element_type=jnp.float32)
            * score_scale
        )
        value_part = jnp.einsum(
            "hck,chd->kd",
            weights_back.astype(jnp.bfloat16),
            mixed_block_grad,
            preferred_element_type=jnp.float32,
        )
        return (query_part, key_part, value_part)

    query_grad, key_partial, value_partial = lax.map(
        attend_backward, (query_seq, key_all, value_all, pictures, log_totals, mixed_grad)
    )
    key_grad, value_grad = (
        lax.psum_scatter(
            key_partial.astype(jnp.bfloat16), "ctx", scatter_dimension=1, tiled=True
        ).astype(jnp.float32),
        lax.psum_scatter(
            value_partial.astype(jnp.bfloat16), "ctx", scatter_dimension=1, tiled=True
        ).astype(jnp.float32),
    )
    query_raw_grad, grad_g_query = jax.vjp(
        lambda raw_rows, gain_vec: norm_rope(raw_rows, gain_vec, angle_rows[:, None, :]),
        query_raw,
        g_query,
    )[1](query_grad.reshape(row_count, HEADS, HD))
    key_raw_grad, grad_g_key = jax.vjp(
        lambda raw_rows, gain_vec: norm_rope(raw_rows, gain_vec, angle_rows), key_raw, g_key
    )[1](key_grad.reshape(row_count, HD))
    query_raw_grad = query_raw_grad.reshape(row_count, HEADS * HD).astype(jnp.bfloat16)
    key_raw_grad = key_raw_grad.astype(jnp.bfloat16)
    value_raw_grad = value_grad.reshape(row_count, HD).astype(jnp.bfloat16)
    grad_w_query = jnp.einsum(
        "nd,nf->df", normal_in, query_raw_grad, preferred_element_type=jnp.float32
    )
    grad_w_key = jnp.einsum(
        "nd,nf->df", normal_in, key_raw_grad, preferred_element_type=jnp.float32
    )
    grad_w_value = jnp.einsum(
        "nd,nf->df", normal_in, value_raw_grad, preferred_element_type=jnp.float32
    )
    normal_in_grad = jnp.einsum(
        "nf,df->nd", query_raw_grad, w_query, preferred_element_type=jnp.float32
    )
    normal_in_grad = normal_in_grad + jnp.einsum(
        "nf,df->nd", key_raw_grad, w_key, preferred_element_type=jnp.float32
    )
    normal_in_grad = normal_in_grad + jnp.einsum(
        "nf,df->nd", value_raw_grad, w_value, preferred_element_type=jnp.float32
    )
    input_part, grad_g_attn_in = norm_back(x_rows, g_attn_in, normal_in_grad)
    input_grad = (
        (residual_grad + input_part)
        .astype(jnp.bfloat16)
        .reshape(local_seqs, local_len, model_width)
    )
    (
        grad_w_query,
        grad_w_key,
        grad_w_value,
        grad_w_out,
        grad_w_gate,
        grad_w_up,
        grad_w_down,
        grad_g_attn_in,
        grad_g_attn_out,
        grad_g_ffn_in,
        grad_g_ffn_out,
        grad_g_query,
        grad_g_key,
    ) = (
        lax.psum_scatter(
            grad_w_query.astype(jnp.bfloat16), "shard", scatter_dimension=0, tiled=True
        ).astype(jnp.float32),
        lax.psum_scatter(
            grad_w_key.astype(jnp.bfloat16), "shard", scatter_dimension=0, tiled=True
        ).astype(jnp.float32),
        lax.psum_scatter(
            grad_w_value.astype(jnp.bfloat16), "shard", scatter_dimension=0, tiled=True
        ).astype(jnp.float32),
        lax.psum_scatter(
            grad_w_out.astype(jnp.bfloat16), "shard", scatter_dimension=0, tiled=True
        ).astype(jnp.float32),
        lax.psum_scatter(
            grad_w_gate.astype(jnp.bfloat16), "shard", scatter_dimension=0, tiled=True
        ).astype(jnp.float32),
        lax.psum_scatter(
            grad_w_up.astype(jnp.bfloat16), "shard", scatter_dimension=0, tiled=True
        ).astype(jnp.float32),
        lax.psum_scatter(
            grad_w_down.astype(jnp.bfloat16), "shard", scatter_dimension=0, tiled=True
        ).astype(jnp.float32),
        lax.psum_scatter(
            grad_g_attn_in.astype(jnp.bfloat16), "shard", scatter_dimension=0, tiled=True
        ).astype(jnp.float32),
        lax.psum_scatter(
            grad_g_attn_out.astype(jnp.bfloat16), "shard", scatter_dimension=0, tiled=True
        ).astype(jnp.float32),
        lax.psum_scatter(
            grad_g_ffn_in.astype(jnp.bfloat16), "shard", scatter_dimension=0, tiled=True
        ).astype(jnp.float32),
        lax.psum_scatter(
            grad_g_ffn_out.astype(jnp.bfloat16), "shard", scatter_dimension=0, tiled=True
        ).astype(jnp.float32),
        lax.psum_scatter(
            grad_g_query.astype(jnp.bfloat16), "shard", scatter_dimension=0, tiled=True
        ).astype(jnp.float32),
        lax.psum_scatter(
            grad_g_key.astype(jnp.bfloat16), "shard", scatter_dimension=0, tiled=True
        ).astype(jnp.float32),
    )
    (
        grad_w_query,
        grad_w_key,
        grad_w_value,
        grad_w_out,
        grad_w_gate,
        grad_w_up,
        grad_w_down,
        grad_g_attn_in,
        grad_g_attn_out,
        grad_g_ffn_in,
        grad_g_ffn_out,
        grad_g_query,
        grad_g_key,
    ) = (
        lax.psum(grad_w_query.astype(jnp.bfloat16), "ctx").astype(jnp.float32),
        lax.psum(grad_w_key.astype(jnp.bfloat16), "ctx").astype(jnp.float32),
        lax.psum(grad_w_value.astype(jnp.bfloat16), "ctx").astype(jnp.float32),
        lax.psum(grad_w_out.astype(jnp.bfloat16), "ctx").astype(jnp.float32),
        lax.psum(grad_w_gate.astype(jnp.bfloat16), "ctx").astype(jnp.float32),
        lax.psum(grad_w_up.astype(jnp.bfloat16), "ctx").astype(jnp.float32),
        lax.psum(grad_w_down.astype(jnp.bfloat16), "ctx").astype(jnp.float32),
        lax.psum(grad_g_attn_in.astype(jnp.bfloat16), "ctx").astype(jnp.float32),
        lax.psum(grad_g_attn_out.astype(jnp.bfloat16), "ctx").astype(jnp.float32),
        lax.psum(grad_g_ffn_in.astype(jnp.bfloat16), "ctx").astype(jnp.float32),
        lax.psum(grad_g_ffn_out.astype(jnp.bfloat16), "ctx").astype(jnp.float32),
        lax.psum(grad_g_query.astype(jnp.bfloat16), "ctx").astype(jnp.float32),
        lax.psum(grad_g_key.astype(jnp.bfloat16), "ctx").astype(jnp.float32),
    )
    return (
        output,
        input_grad,
        grad_w_query,
        grad_w_key,
        grad_w_value,
        grad_w_out,
        grad_w_gate,
        grad_w_up,
        grad_w_down,
        grad_g_attn_in,
        grad_g_attn_out,
        grad_g_ffn_in,
        grad_g_ffn_out,
        grad_g_query,
        grad_g_key,
    )


def solution(mesh):
    return jax.shard_map(
        body,
        mesh=mesh,
        in_specs=(
            P("shard", "ctx", None),
            P("shard", "ctx", None),
            P("shard", None),
            P("shard", None),
            P("shard", None),
            P("shard", None),
            P("shard", None),
            P("shard", None),
            P("shard", None),
            P("shard", None),
            P("shard"),
            P("shard"),
            P("shard"),
            P("shard"),
            P("shard"),
            P("shard"),
        ),
        out_specs=(
            P("shard", "ctx", None),
            P("shard", "ctx", None),
            P("shard", None),
            P("shard", None),
            P("shard", None),
            P("shard", None),
            P("shard", None),
            P("shard", None),
            P("shard", None),
            P("shard"),
            P("shard"),
            P("shard"),
            P("shard"),
            P("shard"),
            P("shard"),
        ),
        check_vma=False,
    )
```

profile of v0, /device:TPU:0, one launch (start us, length us, event | category | flops | bytes accessed | tf_op | source)
XLA Modules:
  0.0 1735.5 jit_solution(17152365747530546222)
XLA Ops:
  16.0 18.1 %all-reduce.19 = (bf16[1152]{0:T(1024)(128)(2,1)S(1)}, bf16[256]{0:T(256)(128)(2,1)S(1)}, bf16[256]{0:T(256)(128)(2,1)S(1)}, bf16[1152]{0:T(1024)(128)(2,1)S(1)}...) all-reduce(bf16[1152]{0:T(1024)(128)(2,1)S(1)} %dynamic-update-slic, ...), channel_id=1, replica_groups=mesh['shard'=4,'ctx'=8] {'shard'}, use_global_device_ids=true, to_apply=%add.4 | all-reduce | flops 5120 | bytes 20480
  34.1 15.1 all_gather.46
  53.3 9.5 all_gather.48
  71.3 3.0 copy.76
  74.3 3.0 multiply_reduce_fusion.9
  79.4 6.8 all-gather.8.cloned.1.call-done
  86.2 30.8 %all-gather.10.cloned.1.call-done = bf16[4,1024,256]{2,1,0:T(8,128)(2,1)} async-done(((bf16[4,128,256]{2,1,0:T(8,128)(2,1)}), bf16[4,1024,256]{2,1,0:T(8,128)(2,1)}) %all-gather.10.cloned.1.call-update) | async-done | bytes 2097168 | tf_op jit(solution)/shard_map/all_gather | solution.py:143
  117.1 22.0 %while.30 = (s32[]{:T(128)}, bf16[4,128,4,256]{1,3,2,0:T(8,128)(2,1)S(1)}, f32[4,4,128]{2,1,0:T(4,128)}, bf16[4,1024,256]{2,1,0:T(8,128)(2,1)}, s32[4,2]{1,0:T(4...) while((s32[]{:T(128)}, ...), condition=%wide.region_7.8_spmd.clone.clone, body=%wide.region_3.7_spmd.clone.clone.sunk | while | flops 541727104 | bytes 8937641 | solution.py:165
  143.3 12.4 all-gather.14.cloned.1.call-done
  155.8 3.7 multiply_reduce_fusion.6
  161.7 146.1 %all-gather.16.cloned.1.call-done = bf16[1152,6912]{1,0:T(8,128)(2,1)} async-done(((bf16[288,6912]{1,0:T(8,128)(2,1)}), bf16[1152,6912]{1,0:T(8,128)(2,1)}) %all-gather.16.cloned.1.call-update) | async-done | bytes 15925264 | tf_op jit(solution)/shard_map/all_gather | solution.py:106
  307.8 16.7 fusion.88
  324.5 135.4 %all-gather.18.cloned.1.call-done = bf16[1152,6912]{1,0:T(8,128)(2,1)} async-done(((bf16[288,6912]{1,0:T(8,128)(2,1)}), bf16[1152,6912]{1,0:T(8,128)(2,1)}) %all-gather.18.cloned.1.call-update) | async-done | bytes 15925264 | tf_op jit(solution)/shard_map/all_gather | solution.py:107
  459.9 21.6 %multiply_convert_fusion.1 = (bf16[512,6912]{1,0:T(8,128)(2,1)}, f32[512,6912]{1,0:T(8,128)}) fusion(f32[512,6912]{1,0:T(8,128)} %fusion.88, bf16[512,1152]{1,0:T(8,128)(2,1)S(1)} %multiply_convert_fusion.2, bf16[1152,6912]{1,0:T(8,128)(2,1)} %all-gather.18.cloned.1.call-done), kind=kOutput, calls=%fused_computation.88 | convolution fusion | flops 8189116416 | bytes 52494336 | tf_op jit(solution)/shard_map/dot_general | solution.py:171
  481.4 130.6 %all-gather.20.cloned.1.call-done = bf16[6912,1152]{1,0:T(8,128)(2,1)} async-done(((bf16[1728,1152]{1,0:T(8,128)(2,1)}), bf16[6912,1152]{1,0:T(8,128)(2,1)}) %all-gather.20.cloned.1.call-update) | async-done | bytes 15925264 | tf_op jit(solution)/shard_map/all_gather | solution.py:108
  612.1 14.5 multiply_reduce_fusion.4
  628.0 2.3 fusion.61
  630.3 28.3 %multiply_convert_fusion = (bf16[512,6912]{1,0:T(8,128)(2,1)}, bf16[512,6912]{1,0:T(8,128)(2,1)}) fusion(f32[512,6912]{1,0:T(8,128)} %fusion.88, f32[512,6912]{1,0:T(8,128)} %get-tuple-element.431, bf16[512,1152]{1,0:T(8,128)(2,1)} %get-tuple-element.410, bf16[6912,1152]{1,0:T(8,128)(2,1)} %all-gather.20.cloned.1.call-done), kind=kOutput, calls=%fused_computation.87 | convolution fusion | flops 8238661632 | bytes 59572224 | tf_op jit(solution)/shard_map/nd,fd->nf/dot_general | solution.py:183
  658.6 14.4 fusion.89
  673.1 17.0 multiply_reduce_fusion
  698.3 73.9 %while.31 = (s32[]{:T(128)}, f32[4,128,4,256]{3,1,0,2:T(8,128)}, bf16[4,1024,256]{2,1,0:T(8,128)(2,1)}, bf16[4,1024,256]{2,1,0:T(8,128)(2,1)}, bf16[4,1024,256]{...) while((s32[]{:T(128)}, f32[4,128,4,256]{3,1,0,2:T(8,128)}, ...), condition=%wide.region_17.18_spmd.clone.clone, body=%wide.region_14.17_spmd.clone.clone.sunk | while | flops 1347950976 | bytes 57952580 | solution.py:233
  706.2 2.3 fusion.174
  724.7 2.3 fusion.174
  743.2 2.3 fusion.174
  761.6 2.3 fusion.174
  779.0 2.8 convolution_convert_fusion.4
  783.5 3.0 convolution_convert_fusion.3
  786.8 21.4 %reduce-scatter.10.cloned.1.call-done = bf16[4,128,256]{2,1,0:T(8,128)(2,1)} async-done(((bf16[4,1024,256]{2,1,0:T(8,128)(2,1)}), bf16[4,128,256]{2,1,0:T(8,128)(2,1)}) %reduce-scatter.10.cloned.1.call-update) | async-done | bytes 262160 | tf_op jit(solution)/shard_map/reduce_scatter | solution.py:237
  812.4 32.5 %reduce-scatter.12.cloned.1.call-done = bf16[4,128,256]{2,1,0:T(8,128)(2,1)} async-done(((bf16[4,1024,256]{2,1,0:T(8,128)(2,1)}), bf16[4,128,256]{2,1,0:T(8,128)(2,1)}) %reduce-scatter.12.cloned.1.call-update) | async-done | bytes 262160 | tf_op jit(solution)/shard_map/reduce_scatter | solution.py:240
  844.9 2.3 fusion.59
  847.3 14.2 convolution_convert_fusion.2
  861.6 14.5 convolution_convert_fusion.1
  877.4 17.1 convolution_convert_fusion
  894.8 29.5 %reduce-scatter.20.cloned.1.call-done = bf16[256,1152]{1,0:T(8,128)(2,1)} async-done(((bf16[1024,1152]{1,0:T(8,128)(2,1)}), bf16[256,1152]{1,0:T(8,128)(2,1)}) %reduce-scatter.20.cloned.1.call-update) | async-done | bytes 589840 | tf_op jit(solution)/shard_map/reduce_scatter | solution.py:303
  924.4 28.4 %reduce-scatter.16.cloned.1.call-done = bf16[288,256]{1,0:T(8,128)(2,1)} async-done(((bf16[1152,256]{1,0:T(8,128)(2,1)}), bf16[288,256]{1,0:T(8,128)(2,1)}) %reduce-scatter.16.cloned.1.call-update) | async-done | bytes 147472 | tf_op jit(solution)/shard_map/reduce_scatter | solution.py:297
  952.8 28.8 %reduce-scatter.18.cloned.1.call-done = bf16[288,256]{1,0:T(8,128)(2,1)} async-done(((bf16[1152,256]{1,0:T(8,128)(2,1)}), bf16[288,256]{1,0:T(8,128)(2,1)}) %reduce-scatter.18.cloned.1.call-update) | async-done | bytes 147472 | tf_op jit(solution)/shard_map/reduce_scatter | solution.py:300
  981.6 150.3 %reduce-scatter.22.cloned.1.call-done = bf16[288,6912]{1,0:T(8,128)(2,1)} async-done(((bf16[1152,6912]{1,0:T(8,128)(2,1)}), bf16[288,6912]{1,0:T(8,128)(2,1)}) %reduce-scatter.22.cloned.1.call-update) | async-done | bytes 3981328 | tf_op jit(solution)/shard_map/reduce_scatter | solution.py:306
  1131.9 150.6 %reduce-scatter.24.cloned.1.call-done = bf16[288,6912]{1,0:T(8,128)(2,1)} async-done(((bf16[1152,6912]{1,0:T(8,128)(2,1)}), bf16[288,6912]{1,0:T(8,128)(2,1)}) %reduce-scatter.24.cloned.1.call-update) | async-done | bytes 3981328 | tf_op jit(solution)/shard_map/reduce_scatter | solution.py:309
  1282.4 150.3 %reduce-scatter.26.cloned.1.call-done = bf16[1728,1152]{1,0:T(8,128)(2,1)} async-done(((bf16[6912,1152]{1,0:T(8,128)(2,1)}), bf16[1728,1152]{1,0:T(8,128)(2,1)}) %reduce-scatter.26.cloned.1.call-update) | async-done | bytes 3981328 | tf_op jit(solution)/shard_map/reduce_scatter | solution.py:312
  1437.8 2.9 fusion.69
  1440.7 16.5 all-reduce.18
  1464.9 15.7 all-reduce.16
  1488.7 3.3 fusion.64
  1492.1 217.1 %all-reduce.22.cloned.1.call-done = (bf16[288,1024]{1,0:T(8,128)(2,1)}, bf16[288,256]{1,0:T(8,128)(2,1)}, bf16[288,256]{1,0:T(8,128)(2,1)}, bf16[256,1152]{1,0:T...) async-done(((bf16[288,1024]{1,0:T(8,128)(2,1)}, bf16[288,256]{1,0:T(8,128)(2,1)}, bf16[288,256]{1,0:T(8,128)(2,1)}, ...) | async-done | bytes 13418512 | tf_op jit(solution)/shard_map/psum | solution.py:349
  1709.2 2.4 convert_element_type.295
  1717.0 4.0 convert_element_type.303
  1720.9 4.0 convert_element_type.305
  1724.9 3.8 convert_element_type.307
  (434 shorter events, 163.0 us)
Async XLA Ops:
  7.2 44.4 %copy-start.2 = (bf16[4,128,1152]{2,1,0:T(8,128)(2,1)S(1)}, bf16[4,128,1152]{2,1,0:T(8,128)(2,1)}, u32[]{:S(2)}) copy-start(bf16[4,128,1152]{2,1,0:T(8,128)(2,1)} %param.20) | copy-start | bytes 3538948
  7.2 64.1 %all-gather.12.cloned.1.call-start = ((), (), s32[]{:S(2)}) async-start(), calls=%async_computation.11 | async-start | bytes 2949120 | tf_op jit(solution)/shard_map/all_gather | solution.py:102
  7.9 78.3 %all-gather.8.cloned.1.call-start = ((), (), s32[]{:S(2)}) async-start(), calls=%async_computation.9 | async-start | bytes 2359296 | tf_op jit(solution)/shard_map/all_gather | solution.py:144
  34.1 35.8 %copy-start.51 = (f32[1152]{0:T(1024)}, f32[1152]{0:T(1024)S(1)}, u32[]{:S(2)}) copy-start(f32[1152]{0:T(1024)S(1)} %convert_element_type.258) | copy-start | bytes 13828
  51.0 18.9 %copy-start.63 = (f32[4,128]{1,0:T(4,128)}, f32[4,128]{1,0:T(4,128)S(1)}, u32[]{:S(2)}) copy-start(f32[4,128]{1,0:T(4,128)S(1)} %fusion.70) | copy-start | bytes 6148
  51.9 11.4 copy-start.34
  53.2 63.9 %all-gather.10.cloned.1.call-start = ((), (), s32[]{:S(2)}) async-start(), calls=%async_computation.10 | async-start | bytes 2359296 | tf_op jit(solution)/shard_map/all_gather | solution.py:143
  53.2 11.2 copy-start.73
  65.2 90.6 %all-gather.14.cloned.1.call-start = ((), (), s32[]{:S(2)}) async-start(), calls=%async_computation.12 | async-start | bytes 2949120 | tf_op jit(solution)/shard_map/all_gather | solution.py:105
  65.8 242.0 %all-gather.16.cloned.1.call-start = ((), (), s32[]{:S(2)}) async-start(), calls=%async_computation.13 | async-start | bytes 19906560 | tf_op jit(solution)/shard_map/all_gather | solution.py:106
  66.4 393.5 %all-gather.18.cloned.1.call-start = ((), (), s32[]{:S(2)}) async-start(), calls=%async_computation.14 | async-start | bytes 19906560 | tf_op jit(solution)/shard_map/all_gather | solution.py:107
  67.0 545.1 %all-gather.20.cloned.1.call-start = ((), (), s32[]{:S(2)}) async-start(), calls=%async_computation.15 | async-start | bytes 19906560 | tf_op jit(solution)/shard_map/all_gather | solution.py:108
  67.7 740.5 %reduce-scatter.10.cloned.1.call-start = ((), (), s32[]{:S(2)}) async-start(), calls=%async_computation.16 | async-start | bytes 2359296 | tf_op jit(solution)/shard_map/reduce_scatter | solution.py:237
  68.0 92.0 %copy-start.56 = (f32[1152]{0:T(1024)}, f32[1152]{0:T(1024)S(1)}, u32[]{:S(2)}) copy-start(f32[1152]{0:T(1024)S(1)} %convert_element_type.272) | copy-start | bytes 13828
  78.9 38.2 %copy-start.40 = (bf16[4,128,4,256]{1,3,2,0:T(8,128)(2,1)S(1)}, bf16[4,128,4,256]{1,3,2,0:T(8,128)(2,1)}, u32[]{:S(2)}) copy-start(bf16[4,128,4,256]{1,3,2,0:T(8,128)(2,1)} %custom-call) | copy-start | bytes 3145732
  140.0 19.4 %copy-start.10 = (bf16[4,128,4,256]{3,1,2,0:T(8,128)(2,1)}, bf16[4,128,4,256]{3,1,2,0:T(8,128)(2,1)S(1)}, u32[]{:S(2)}) copy-start(bf16[4,128,4,256]{3,1,2,0:T(8,128)(2,1)S(1)} %get-tuple-element.667) | copy-start | bytes 3145732
  161.4 163.1 %copy-start.71 = (f32[512]{0:T(512)}, f32[512]{0:T(512)S(1)}, u32[]{:S(2)}) copy-start(f32[512]{0:T(512)S(1)} %fusion.83) | copy-start | bytes 6148
  161.7 298.2 %copy-start.30 = (bf16[512,1152]{1,0:T(8,128)(2,1)}, bf16[512,1152]{1,0:T(8,128)(2,1)S(1)}, u32[]{:S(2)}) copy-start(bf16[512,1152]{1,0:T(8,128)(2,1)S(1)} %multiply_convert_fusion.2) | copy-start | bytes 3538948
  612.1 14.5 copy-start.11
  612.1 14.5 copy-start.58
  658.6 14.4 copy-start.72
  658.6 14.4 copy-start.83
  673.0 17.0 copy-start.70
  673.1 17.0 copy-start.5
  673.1 17.0 copy-start.57
  673.1 17.0 copy-start.62
  708.5 6.4 copy-start.1
  727.0 6.4 copy-start.1
  745.5 6.4 copy-start.1
  764.0 6.4 copy-start.1
  772.2 72.7 %reduce-scatter.12.cloned.1.call-start = ((), (), s32[]{:S(2)}) async-start(), calls=%async_computation.17 | async-start | bytes 2359296 | tf_op jit(solution)/shard_map/reduce_scatter | solution.py:240
  773.0 121.9 %reduce-scatter.14.cloned.1.call-start = ((), (), s32[]{:S(2)}) async-start(), calls=%async_computation.18 | async-start | bytes 2949120 | tf_op jit(solution)/shard_map/reduce_scatter | solution.py:294
  781.9 142.5 %reduce-scatter.20.cloned.1.call-start = ((), (), s32[]{:S(2)}) async-start(), calls=%async_computation.21 | async-start | bytes 2949120 | tf_op jit(solution)/shard_map/reduce_scatter | solution.py:303
  786.4 22.7 %copy-start.46 = (f32[128,128]{1,0:T(8,128)S(1)}, f32[128,128]{1,0:T(8,128)}, u32[]{:S(2)}) copy-start(f32[128,128]{1,0:T(8,128)} %copy-done.44) | copy-start | bytes 196612
  786.4 22.8 %copy-start.49 = (f32[128,128]{1,0:T(8,128)S(1)}, f32[128,128]{1,0:T(8,128)}, u32[]{:S(2)}) copy-start(f32[128,128]{1,0:T(8,128)} %copy-done.47) | copy-start | bytes 196612
  786.5 22.9 %copy-start.13 = (f32[512,256]{1,0:T(8,128)S(1)}, f32[512,256]{1,0:T(8,128)}, u32[]{:S(2)}) copy-start(f32[512,256]{1,0:T(8,128)} %copy-done.12) | copy-start | bytes 1572868
  786.5 22.9 %copy-start.60 = (f32[512]{0:T(512)S(1)}, f32[512]{0:T(512)}, u32[]{:S(2)}) copy-start(f32[512]{0:T(512)} %copy-done.59) | copy-start | bytes 6148
  786.5 22.9 %copy-start.74 = (f32[256]{0:T(256)S(1)}, f32[256]{0:T(256)}, u32[]{:S(2)}) copy-start(f32[256]{0:T(256)} %copy-done.73) | copy-start | bytes 3076
  786.5 166.3 %reduce-scatter.16.cloned.1.call-start = ((), (), s32[]{:S(2)}) async-start(), calls=%async_computation.19 | async-start | bytes 737280 | tf_op jit(solution)/shard_map/reduce_scatter | solution.py:297
  812.3 34.9 %copy-start.31 = (bf16[512,1152]{1,0:T(8,128)(2,1)S(1)}, bf16[512,1152]{1,0:T(8,128)(2,1)}, u32[]{:S(2)}) copy-start(bf16[512,1152]{1,0:T(8,128)(2,1)} %copy-done.30) | copy-start | bytes 3538948
  812.4 169.2 %reduce-scatter.18.cloned.1.call-start = ((), (), s32[]{:S(2)}) async-start(), calls=%async_computation.20 | async-start | bytes 737280 | tf_op jit(solution)/shard_map/reduce_scatter | solution.py:300
  847.2 284.6 %reduce-scatter.22.cloned.1.call-start = ((), (), s32[]{:S(2)}) async-start(), calls=%async_computation.22 | async-start | bytes 19906560 | tf_op jit(solution)/shard_map/reduce_scatter | solution.py:306
  861.6 420.9 %reduce-scatter.24.cloned.1.call-start = ((), (), s32[]{:S(2)}) async-start(), calls=%async_computation.23 | async-start | bytes 19906560 | tf_op jit(solution)/shard_map/reduce_scatter | solution.py:309
  876.1 556.6 %reduce-scatter.26.cloned.1.call-start = ((), (), s32[]{:S(2)}) async-start(), calls=%async_computation.24 | async-start | bytes 19906560 | tf_op jit(solution)/shard_map/reduce_scatter | solution.py:312
  894.5 814.6 %all-reduce.22.cloned.1.call-start = ((), (), s32[]{:S(2)}) async-start(), calls=%async_computation.25 | async-start | bytes 26836992 | tf_op jit(solution)/shard_map/psum | solution.py:349
  1437.8 50.3 %copy-start.64 = (f32[4,128]{1,0:T(4,128)S(1)}, f32[4,128]{1,0:T(4,128)}, u32[]{:S(2)}) copy-start(f32[4,128]{1,0:T(4,128)} %copy-done.63) | copy-start | bytes 6148
  1437.8 51.0 %copy-start.7 = (f32[512,1152]{1,0:T(8,128)S(1)}, f32[512,1152]{1,0:T(8,128)}, u32[]{:S(2)}) copy-start(f32[512,1152]{1,0:T(8,128)} %copy-done.6) | copy-start | bytes 7077892
  1709.2 7.8 copy-start.16
  (65 other events, 110.3 us)
Sparse Core Ops, SparseCore 0:
  9.9 44.6 all-gather.11
  56.7 29.5 all-gather.7
  88.4 28.5 all-gather.9
  118.7 36.9 all-gather.13
  157.4 150.3 all-gather.15
  309.5 150.3 all-gather.17
  461.7 150.3 all-gather.19
  772.4 35.7 reduce-scatter.9
  810.5 34.3 reduce-scatter.11
  847.8 36.0 reduce-scatter.13
  886.9 37.3 reduce-scatter.19
  927.7 25.0 reduce-scatter.15
  956.5 25.0 reduce-scatter.17
  984.6 147.2 reduce-scatter.21
  1135.1 147.2 reduce-scatter.23
  1285.4 147.2 reduce-scatter.25
  1435.8 273.3 all-reduce.21
where the time goes:
time: 1740 us
  waiting for transfers between devices  1270 us (73%)
  matrix products  229 us (13%)
  blocking collectives  74.9 us (4%)
  local copies, waits for them, and re-layouts  70.1 us (4%)
  other arithmetic  67 us (4%)
  between operations  18.2 us (1%)
    psum x1, waiting for transfers between devices, body(): lax.psum(grad_w_query.astype(jnp.bfloat16), 'ctx').astype(jnp.float32)  217 us
    reduce_scatter x1, waiting for transfers between devices, body(): lax.psum_scatter(grad_w_up.astype(jnp.bfloat16), 'shard', scatter_dimensi...  151 us
    reduce_scatter x1, waiting for transfers between devices, body(): lax.psum_scatter(grad_w_down.astype(jnp.bfloat16), 'shard', scatter_dimen...  150 us
    reduce_scatter x1, waiting for transfers between devices, body(): lax.psum_scatter(grad_w_gate.astype(jnp.bfloat16), 'shard', scatter_dimen...  150 us
    all_gather x1, waiting for transfers between devices, body(): lax.all_gather(w_gate, 'shard', axis=0, tiled=True)  146 us
    all_gather x1, waiting for transfers between devices, body(): lax.all_gather(w_up, 'shard', axis=0, tiled=True)  135 us
    all_gather x1, waiting for transfers between devices, body(): lax.all_gather(w_down, 'shard', axis=0, tiled=True)  131 us
  transfers between devices with their start and end apart: 17, of which 15 were waited for; matrix products, arithmetic and copies ran while one was open for 10% of the time, Pallas kernels for 0%

commit v1 on v0

v1 whole, which is shorter than its diff:
```python
import jax
import jax.numpy as jnp
from jax import lax
from jax.sharding import Mesh
from jax.sharding import PartitionSpec as P

HEADS = 4
HD = 256
PIECE = 256
EPS = 1e-06
ROPE_BASE = 1000000.0
SCALE = 0.0625
BF = jnp.bfloat16
F32 = jnp.float32


def dot(a, b):
    return lax.dot_general(a, b, (((1,), (0,)), ((), ())), preferred_element_type=F32)


def dot_t(a, b):
    return lax.dot_general(a, b, (((1,), (1,)), ((), ())), preferred_element_type=F32)


def dot_rows(a, b):
    return lax.dot_general(a, b, (((0,), (0,)), ((), ())), preferred_element_type=F32)


def inv_rms(v):
    return lax.rsqrt(jnp.mean(v * v, axis=-1, keepdims=True) + EPS)


def rms_back(v, r, gain, z):
    gz = gain * z
    return r * gz - v * (r * r * r * jnp.mean(gz * v, axis=-1, keepdims=True))


def rope(v, cos, sin):
    half = v.shape[-1] // 2
    a, b = v[..., :half], v[..., half:]
    return jnp.concatenate([a * cos - b * sin, b * cos + a * sin], axis=-1)


def gelu_and_slope(u):
    k = 0.7978845608028654
    u2 = u * u
    t = jnp.tanh(k * (u + 0.044715 * u2 * u))
    half = 0.5 * (1.0 + t)
    slope = half + 0.5 * u * (1.0 - t * t) * (k * (1.0 + 3.0 * 0.044715 * u2))
    return u * half, slope


def allowed(query_pos, key_pos, starts):
    causal = key_pos[None, :] <= query_pos[:, None]
    inside_query = (query_pos[:, None] >= starts[None, :]) & (
        query_pos[:, None] < starts[None, :] + PIECE
    )
    inside_key = (key_pos[:, None] >= starts[None, :]) & (
        key_pos[:, None] < starts[None, :] + PIECE
    )
    shared = jnp.any(inside_query[:, None, :] & inside_key[None, :, :], axis=-1)
    return causal | shared


def body(
    tokens,
    cotangent,
    pictures,
    w_query,
    w_key,
    w_value,
    w_out,
    w_gate,
    w_up,
    w_down,
    g_attn_in,
    g_attn_out,
    g_ffn_in,
    g_ffn_out,
    g_query,
    g_key,
):
    seqs, piece_len, width = tokens.shape
    n_s = lax.axis_size("shard")
    n_r = lax.axis_size("r")
    n_z = lax.axis_size("z")
    s, z, c = lax.axis_index("shard"), lax.axis_index("z"), lax.axis_index("c")
    own = seqs * piece_len
    both = 2 * own
    d_own = width // n_s
    ff = w_gate.shape[1]
    ff_own = ff // (2 * n_s)

    def px(v, k):
        return lax.ppermute(v, "shard", [(i, i ^ k) for i in range(n_s)])

    def pz(v, k):
        return lax.ppermute(v, "z", [(i, i ^ k) for i in range(n_z)])

    def pc(v):
        return lax.ppermute(v, "c", [(0, 1), (1, 0)])

    def natural(pieces, index):
        stacked = jnp.stack(pieces)
        n = len(pieces)
        return jnp.stack(
            [lax.dynamic_index_in_dim(stacked, index ^ j, 0, keepdims=False) for j in range(n)]
        )

    def pick(v, index, axis=0):
        return lax.dynamic_index_in_dim(v, index, axis, keepdims=False)

    def by_core(mine, other, axis):
        first = jnp.where(c == 0, mine, other)
        second = jnp.where(c == 0, other, mine)
        return jnp.stack([first, second], axis=axis)

    def gather4(v):
        h = v.shape[0] // 2
        f1, f2 = px(v, 1), px(v, 2)
        f3 = jnp.concatenate([px(f1[:h], 2), px(f2[h:], 1)])
        return [v, f1, f2, f3]

    def scatter4(p):
        h = p[0].shape[0] // 2
        a = px(p[3][:h].astype(BF), 2)
        b = px(p[3][h:].astype(BF), 1)
        q1 = jnp.concatenate([(p[1][:h] + a).astype(BF), p[1][h:].astype(BF)])
        q2 = jnp.concatenate([p[2][:h].astype(BF), (p[2][h:] + b).astype(BF)])
        return p[0] + px(q1, 1).astype(F32) + px(q2, 2).astype(F32)

    def sum_z(v):
        if n_z == 4:
            t = lax.ppermute(v, "z", [(0, 1), (3, 2)])
            part = v + t
            u = lax.ppermute(part, "z", [(1, 2), (2, 1)])
            total = part + u
            back = lax.ppermute(total, "z", [(1, 0), (2, 3)])
            v = jnp.where((z == 0) | (z == 3), back, total)
        else:
            v = lax.psum(v, "z")
        return lax.psum(v, "r") if n_r > 1 else v

    def to_sequence(v):
        got = [pick(v, z)] + [pz(pick(v, z ^ k), k) for k in range(1, n_z)]
        return natural(got, z)

    def from_sequence(v):
        got = [pick(v, z)] + [pz(pick(v, z ^ k), k) for k in range(1, n_z)]
        return natural(got, z)

    wq_half = lax.dynamic_slice_in_dim(w_query, c * (HEADS // 2 * HD), HEADS // 2 * HD, 1)
    wkv_half = jnp.where(c == 0, w_key, w_value)
    qkv_mine = jnp.concatenate([wq_half, wkv_half], axis=1)
    half_head = w_out.shape[0] // 2
    out_mine = lax.dynamic_slice_in_dim(w_out, c * half_head, half_head, 0)
    gains = jnp.concatenate([g_attn_in, g_attn_out, g_ffn_in, g_ffn_out, g_query, g_key])
    gains = natural([gains] + [px(gains, k) for k in range(1, n_s)], s)
    w_qkv = natural([qkv_mine] + [px(qkv_mine, k) for k in range(1, n_s)], s)
    w_qkv = w_qkv.reshape(width, qkv_mine.shape[1])
    w_qkv_other = pc(w_qkv)
    out_half = natural([out_mine] + [px(out_mine, k) for k in range(1, n_s)], s)
    w_out_all = by_core(out_half, pc(out_half), 1).reshape(HEADS * HD, width)
    x = to_sequence(tokens).reshape(own, width).astype(F32)
    zc = to_sequence(cotangent).reshape(own, width)

    def gain(first, size):
        return gains[:, first : first + size].reshape(1, n_s * size)

    hd_own = HD // n_s
    ga_in, ga_out, gf_in, gf_out = (gain(i * d_own, d_own) for i in range(4))
    gq, gk = gain(4 * d_own, hd_own), gain(4 * d_own + hd_own, hd_own)

    def col_piece(w, k):
        first = (s ^ k) * (2 * ff_own) + c * ff_own
        return lax.dynamic_slice_in_dim(w, first, ff_own, 1)

    gu = [jnp.stack([col_piece(w_gate, k), col_piece(w_up, k)]) for k in range(n_s)]
    gu = natural([gu[0]] + [px(gu[k], k) for k in range(1, n_s)], s)
    wg = gu[:, 0].reshape(width, ff_own)
    wu = gu[:, 1].reshape(width, ff_own)
    wd = lax.dynamic_slice_in_dim(w_down, c * ff_own, ff_own, 0)

    def whole(mine):
        n = mine.shape[1]
        mine = mine.reshape(seqs, piece_len, n)
        return by_core(mine, pc(mine), 1).reshape(both, n)

    def mine_of(v):
        n = v.shape[1]
        return pick(v.reshape(seqs, 2, piece_len, n), c, 1).reshape(own, n)

    r_x = inv_rms(x)
    nin = whole((x * r_x * ga_in).astype(BF))
    heads = HEADS // 2
    raw = dot(nin, w_qkv)
    raw_other = dot(nin, w_qkv_other[:, heads * HD :])
    q_raw = raw[:, : heads * HD].reshape(both, heads, HD)
    k_raw = jnp.where(c == 0, raw[:, heads * HD :], raw_other)
    v_raw = jnp.where(c == 0, raw_other, raw[:, heads * HD :])
    base = lax.axis_index("r") * both
    q_pos = base + jnp.arange(both, dtype=jnp.int32)
    half = HD // 2
    inverse = jnp.exp(
        -(jnp.arange(half).astype(F32) * 2.0 / HD) * jnp.log(jnp.float32(ROPE_BASE))
    )
    angle = q_pos.astype(F32)[:, None] * inverse[None, :]
    cos, sin = jnp.cos(angle), jnp.sin(angle)
    rq, rk = inv_rms(q_raw), inv_rms(k_raw)
    queries = rope(q_raw * rq * gq, cos[:, None, :], sin[:, None, :]).astype(BF)
    keys = rope(k_raw * rk * gk, cos, sin).astype(BF)
    values = v_raw.astype(BF)
    if n_r > 1:
        keys = lax.all_gather(keys, "r", axis=0, tiled=True)
        values = lax.all_gather(values, "r", axis=0, tiled=True)
    starts = pick(pictures, z)
    permitted = allowed(q_pos, jnp.arange(keys.shape[0], dtype=jnp.int32), starts)
    scores = jnp.einsum("qhd,kd->hqk", queries, keys, preferred_element_type=F32) * SCALE
    scores = jnp.where(permitted[None], scores, -1e30)
    peak = jnp.max(scores, axis=-1, keepdims=True)
    expo = jnp.exp(scores - peak)
    total = jnp.sum(expo, axis=-1, keepdims=True)
    soft = (expo / total).astype(BF)
    lse = peak + jnp.log(total)
    mixed = jnp.einsum("hqk,kd->qhd", soft, values, preferred_element_type=F32)
    mixed = mixed.astype(BF).reshape(both, heads * HD)
    mixed_other = pc(mixed)
    mixed_all = by_core(mixed, mixed_other, 1).reshape(both, HEADS * HD)
    attn_out = dot(mine_of(mixed_all), w_out_all)
    r_ao = inv_rms(attn_out)
    residual = x + attn_out * r_ao * ga_out
    r_res = inv_rms(residual)
    nffn = (residual * r_res * gf_in).astype(BF)

    rows = []
    acts = []
    branch_parts = []
    for v in gather4(nffn):
        rk_rows = jnp.concatenate([v, pc(v)])
        g_act, u_act = dot(rk_rows, wg), dot(rk_rows, wu)
        gel, _ = gelu_and_slope(g_act)
        hid = (gel * u_act).astype(BF)
        part = dot(hid, wd)
        branch_parts.append(part[:own] + pc(part[own:].astype(BF)))
        rows.append(rk_rows)
        acts.append((g_act, u_act, hid))
    branch = scatter4(branch_parts)
    r_b = inv_rms(branch)
    output = (residual + branch * r_b * gf_out).astype(BF)
    output = from_sequence(output.reshape(tokens.shape))

    zf = zc.astype(F32)
    gg_ffn_out = jnp.sum(zf * branch * r_b, axis=0)
    low = rms_back(branch, r_b, gf_out, zf).astype(BF)
    back_parts, gates, ups, lows = [], [], [], []
    for k, v in enumerate(gather4(low)):
        g_act, u_act, hid = acts[k]
        rk_low = jnp.concatenate([v, pc(v)])
        hid_grad = dot_t(rk_low, wd)
        gel, slope = gelu_and_slope(g_act)
        gate_grad = (hid_grad * u_act * slope).astype(BF)
        up_grad = (hid_grad * gel).astype(BF)
        part = dot_t(gate_grad, wg) + dot_t(up_grad, wu)
        back_parts.append(part[:own] + pc(part[own:].astype(BF)))
        gates.append(gate_grad)
        ups.append(up_grad)
        lows.append(rk_low)
    nffn_grad = scatter4(back_parts)
    all_rows = jnp.concatenate(rows)
    gw_down = dot_rows(jnp.concatenate([a[2] for a in acts]), jnp.concatenate(lows)).astype(BF)
    gw_gate = dot_rows(all_rows, jnp.concatenate(gates)).astype(BF)
    gw_up = dot_rows(all_rows, jnp.concatenate(ups)).astype(BF)

    hp = ff_own // 2
    gw_down = jnp.concatenate([sum_z(gw_down[:hp]), sum_z(gw_down[hp:])])
    gw_gu = jnp.stack([gw_gate.reshape(n_s, d_own, ff_own), gw_up.reshape(n_s, d_own, ff_own)], 1)
    gw_gu = [sum_z(pick(gw_gu, s))] + [sum_z(px(pick(gw_gu, s ^ k), k)) for k in range(1, n_s)]

    res_grad = zf + rms_back(residual, r_res, gf_in, nffn_grad)
    gg_ffn_in = jnp.sum(nffn_grad * residual * r_res, axis=0)
    gg_attn_out = jnp.sum(res_grad * attn_out * r_ao, axis=0)
    attn_grad = whole(rms_back(attn_out, r_ao, ga_out, res_grad).astype(BF))
    w_out_heads = lax.dynamic_slice_in_dim(w_out_all, c * heads * HD, heads * HD, 0)
    mixed_grad = dot_t(attn_grad, w_out_heads).astype(BF).reshape(both, heads, HD)
    scores = jnp.einsum("qhd,kd->hqk", queries, keys, preferred_element_type=F32) * SCALE
    scores = jnp.where(permitted[None], scores, -1e30)
    back = jnp.exp(scores - lse)
    prob_grad = jnp.einsum("qhd,kd->hqk", mixed_grad, values, preferred_element_type=F32)
    inner = jnp.sum(back * prob_grad, axis=-1, keepdims=True)
    score_grad = (back * (prob_grad - inner)).astype(BF)
    q_grad = jnp.einsum("hqk,kd->qhd", score_grad, keys, preferred_element_type=F32) * SCALE
    k_grad = jnp.einsum("hqk,qhd->kd", score_grad, queries, preferred_element_type=F32) * SCALE
    v_grad = jnp.einsum("hqk,qhd->kd", back.astype(BF), mixed_grad, preferred_element_type=F32)
    k_grad = k_grad + pc(k_grad.astype(BF)).astype(F32)
    v_grad = v_grad + pc(v_grad.astype(BF)).astype(F32)
    if n_r > 1:
        k_grad = lax.psum_scatter(k_grad.astype(BF), "r", scatter_dimension=0, tiled=True).astype(F32)
        v_grad = lax.psum_scatter(v_grad.astype(BF), "r", scatter_dimension=0, tiled=True).astype(F32)
    q_un = rope(q_grad, cos[:, None, :], -sin[:, None, :])
    k_un = rope(k_grad, cos, -sin)
    gg_query = jnp.sum(q_un * q_raw * rq, axis=(0, 1))
    gg_key = jnp.sum(mine_of(k_un * k_raw * rk), axis=0)
    q_low = rms_back(q_raw, rq, gq, q_un).astype(BF).reshape(both, heads * HD)
    k_low = rms_back(k_raw, rk, gk, k_un).astype(BF)
    v_low = v_grad.astype(BF)
    kv_mine = jnp.where(c == 0, k_low, v_low)
    kv_other = jnp.where(c == 0, v_low, k_low)
    low_mine = jnp.concatenate([q_low, kv_mine], axis=1)
    low_other = jnp.concatenate([pc(q_low), kv_other], axis=1)
    nin_grad = dot_t(mine_of(low_mine), w_qkv) + dot_t(mine_of(low_other), w_qkv_other)
    gg_attn_in = jnp.sum(nin_grad * x * r_x, axis=0)
    input_grad = (res_grad + rms_back(x, r_x, ga_in, nin_grad)).astype(BF)
    input_grad = from_sequence(input_grad.reshape(tokens.shape))

    gw_qkv = dot_rows(nin, low_mine)
    mixed_cols = mixed_all.reshape(both, HEADS, 2, HD // 2)
    mixed_cols = pick(mixed_cols, c, 2).reshape(both, HEADS * HD // 2)
    gw_out = dot_rows(mixed_cols, attn_grad)

    def to_shards(v):
        v = v.reshape(n_s, v.shape[0] // n_s, v.shape[1])
        return scatter4([pick(v, s ^ k) for k in range(n_s)]).astype(BF)

    gw_qkv = sum_z(to_shards(gw_qkv))
    gw_out = sum_z(to_shards(gw_out))

    parts = [gg_attn_in, gg_attn_out, gg_ffn_in, gg_ffn_out, gg_query, gg_key]
    small = jnp.concatenate([p.reshape(n_s, -1) for p in parts], axis=1)
    small = small + pc(small)
    for k in (1, 2) if n_z == 4 else ():
        small = small + pz(small, k)
    if n_z != 4:
        small = lax.psum(small, "z")
    if n_r > 1:
        small = lax.psum(small, "r")
    for k in (1, 2):
        small = small + px(small, k)
    small = pick(small, s)
    sizes = [d_own] * 4 + [hd_own] * 2
    small_out = []
    first = 0
    for size in sizes:
        small_out.append(small[first : first + size])
        first += size

    hw = heads * HD
    qkv_pair = by_core(gw_qkv, pc(gw_qkv), 0).astype(F32)
    gw_query = jnp.concatenate([qkv_pair[0][:, :hw], qkv_pair[1][:, :hw]], axis=1)
    gw_key, gw_value = qkv_pair[0][:, hw:], qkv_pair[1][:, hw:]
    gw_out = by_core(gw_out, pc(gw_out), 0).reshape(w_out.shape).astype(F32)
    gw_down = by_core(gw_down, pc(gw_down), 0).reshape(w_down.shape).astype(F32)
    pieces = natural([by_core(p, pc(p), 0) for p in gw_gu], s)
    gw_gate = jnp.concatenate(
        [pieces[j, i, 0] for j in range(n_s) for i in range(2)], axis=1
    ).astype(F32)
    gw_up = jnp.concatenate(
        [pieces[j, i, 1] for j in range(n_s) for i in range(2)], axis=1
    ).astype(F32)
    return (
        output,
        input_grad,
        gw_query,
        gw_key,
        gw_value,
        gw_out,
        gw_gate,
        gw_up,
        gw_down,
        *small_out,
    )


def solution(mesh):
    n_s, n_c = mesh.shape["shard"], mesh.shape["ctx"]

    def run(*args):
        seqs = args[0].shape[0] // n_s
        groups = n_c // (2 * seqs)
        fine = Mesh(mesh.devices.reshape(n_s, groups, seqs, 2), ("shard", "r", "z", "c"))
        ctx = ("r", "z", "c")
        rows, mat, vec = P("shard", ctx, None), P("shard", None), P("shard")
        return jax.shard_map(
            body,
            mesh=fine,
            in_specs=(rows, rows, mat) + (mat,) * 7 + (vec,) * 6,
            out_specs=(rows, rows) + (mat,) * 7 + (vec,) * 6,
            check_vma=False,
        )(*args)

    return run
```

time: 1740 us -> 1010 us (0.58)
  waiting for transfers between devices: 1270 us -> 402 us
  starting transfers between devices: 1.32 us -> 112 us
  other arithmetic: 67 us -> 153 us
  blocking collectives: 74.9 us -> 0 us
  local copies, waits for them, and re-layouts: 70.1 us -> 144 us
  matrix products: 229 us -> 187 us
    reduce_scatter x9 -> x0, waiting for transfers between devices: 592 us -> none  [the longest x1 151 us: body(): lax.psum_scatter(grad_w_up.astype(jnp.bfloat16), 'shard', scatter_dimensi...]
    all_gather x7 -> x0, waiting for transfers between devices: 462 us -> none  [the longest x1 146 us: body(): lax.all_gather(w_gate, 'shard', axis=0, tiled=True)]
    ppermute x0 -> x111, waiting for transfers between devices: none -> 402 us  [the longest x8 144 us: sum_z(): back = lax.ppermute(total, 'z', [(1, 0), (2, 3)])]
    psum x1 -> x0, waiting for transfers between devices: 217 us -> none  [body(): lax.psum(grad_w_query.astype(jnp.bfloat16), 'ctx').astype(jnp.float32)]
    ppermute x0 -> x111, starting transfers between devices: none -> 112 us  [the longest x41 46.5 us: px(): return lax.ppermute(v, 'shard', [(i, i ^ k) for i in range(n_s)])]
    dot_general x49 -> x41, matrix products: 229 us -> 187 us  [the longest x15 76.7 us: dot_t(): lax.dot_general(a, b, (((1,), (1,)), ((), ())), preferred_element_type=F32)]
    another operation x6 -> x46, other arithmetic: 0.36 us -> 40.7 us  [the longest x15 14.3 us: natural(): stacked = jnp.stack(pieces)]
    unnamed x2 -> x0, blocking collectives: 34.6 us -> none
  transfers between devices with their start and end apart: 17 -> 111, of which waited for: 15 -> 36; matrix products, arithmetic and copies ran while one was open for 10% -> 44% of each run, Pallas kernels for 0% -> 0%
where the time goes in v1:
time: 1010 us; the launch traced here: 1000 us
  waiting for transfers between devices  402 us (40%)
  matrix products  187 us (19%)
  other arithmetic  153 us (15%)
  local copies, waits for them, and re-layouts  144 us (14%)
  starting transfers between devices  112 us (11%)
    ppermute x8, waiting for transfers between devices, sum_z(): back = lax.ppermute(total, 'z', [(1, 0), (2, 3)])  144 us
    ppermute x41, waiting for transfers between devices, px(): return lax.ppermute(v, 'shard', [(i, i ^ k) for i in range(n_s)])  114 us
    ppermute x8, waiting for transfers between devices, sum_z(): t = lax.ppermute(v, 'z', [(0, 1), (3, 2)])  89.9 us
    dot_general x15, matrix products, dot_t(): lax.dot_general(a, b, (((1,), (1,)), ((), ())), preferred_element_type=F32)  76.7 us
    dot_general x15, matrix products, dot(): lax.dot_general(a, b, (((1,), (0,)), ((), ())), preferred_element_type=F32)  54.1 us
    ppermute x14, waiting for transfers between devices, pz(): return lax.ppermute(v, 'z', [(i, i ^ k) for i in range(n_z)])  53 us
    unnamed x372, local copies, waits for them, and re-layouts  50.1 us
    ppermute x41, starting transfers between devices, px(): return lax.ppermute(v, 'shard', [(i, i ^ k) for i in range(n_s)])  46.5 us
  transfers between devices with their start and end apart: 111, of which 36 were waited for; matrix products, arithmetic and copies ran while one was open for 44% of the time, Pallas kernels for 0%

profile of v1, /device:TPU:0, one launch (start us, length us, event | category | flops | bytes accessed | tf_op | source)
XLA Modules:
  0.0 1001.6 jit_solution(9384445260145544774)
XLA Ops:
  20.0 5.7 dynamic-slice_bitcast_fusion.22
  46.6 14.0 %collective-permute-done.1 = bf16[128,1152]{1,0:T(8,128)(2,1)S(1)} collective-permute-done((bf16[128,1152]{1,0:T(8,128)(2,1)S(1)}, bf16[128,1152]{1,0:T(8,128)(2,1)S(1)}, u32[]{:S(2)}, u32[]{:S(2)}) %collective-permute-start.1) | collective-permute-done | bytes 294944 | tf_op jit(solution)/shard_map/ppermute | solution.py:98
  75.1 6.7 collective-permute-done.7
  86.2 4.5 fusion.212
  148.6 23.4 %collective-permute-done.21 = bf16[512,1152]{1,0:T(8,128)(2,1)S(1)} collective-permute-done((bf16[512,1152]{1,0:T(8,128)(2,1)S(1)}, bf16[512,1152]{1,0:T(8,128)(2,1)S(1)}, u32[]{:S(2)}, u32[]{:S(2)}) %collective-permute-start.21) | collective-permute-done | bytes 1179680 | tf_op jit(solution)/shard_map/ppermute | solution.py:95
  176.5 6.0 multiply_convert_fusion.11
  196.6 5.2 multiply_convert_fusion.8
  210.4 5.2 multiply_convert_fusion.10
  219.5 5.4 multiply_convert_fusion.9
  235.4 12.3 %collective-permute-done.33 = bf16[256,1152]{1,0:T(8,128)(2,1)S(1)} collective-permute-done((bf16[256,1152]{1,0:T(8,128)(2,1)S(1)}, bf16[256,1152]{1,0:T(8,128)(2,1)S(1)}, u32[]{:S(2)}, u32[]{:S(2)}) %collective-permute-start.33) | collective-permute-done | bytes 589856 | tf_op jit(solution)/shard_map/ppermute | solution.py:95
  254.5 13.3 %collective-permute-done.39 = bf16[128,1152]{1,0:T(8,128)(2,1)S(1)} collective-permute-done((bf16[128,1152]{1,0:T(8,128)(2,1)}, bf16[128,1152]{1,0:T(8,128)(2,1)S(1)}, u32[]{:S(2)}, u32[]{:S(2)}) %collective-permute-start.39) | collective-permute-done | bytes 294944 | tf_op jit(solution)/shard_map/ppermute | solution.py:98
  269.2 7.0 collective-permute-done.34
  301.8 11.1 %collective-permute-done.47 = bf16[512,1152]{1,0:T(8,128)(2,1)} collective-permute-done((bf16[512,1152]{1,0:T(8,128)(2,1)}, bf16[512,1152]{1,0:T(8,128)(2,1)}, u32[]{:S(2)}, u32[]{:S(2)}) %collective-permute-start.47) | collective-permute-done | bytes 1179680 | tf_op jit(solution)/shard_map/ppermute | solution.py:95
  317.7 8.2 multiply_convert_fusion.6
  325.9 5.1 fusion.216
  340.4 7.7 multiply_convert_fusion
  348.2 4.5 fusion.219
  359.2 8.2 multiply_convert_fusion.4
  367.5 4.5 fusion.217
  380.5 8.4 multiply_convert_fusion.2
  388.9 4.6 fusion.218
  393.5 15.8 %fusion.52 = bf16[1152,864]{0,1:T(8,128)(2,1)} fusion(bf16[4096,1152]{1,0:T(8,128)(2,1)} %get-tuple-element.131, bf16[1024,864]{0,1:T(8,128)(2,1)} %copy-done.166, bf16[1024,864]{0,1:T(8,128)(2,1)} %get-tuple-element.66, bf16[1024,864]{0,1:T(8,128)(2,1)} %get-tuple-element.62, bf16[1024,864]{0,1:T(8,128)(2,1)} %get-tuple-element.60), kind=kOutput, calls=%fused_computation.95 | convolution fusion | flops 8183033856 | bytes 18505728 | tf_op jit(solution)/shard_map/dot_general | solution.py:26
  409.3 14.7 %fusion.49 = bf16[1152,864]{0,1:T(8,128)(2,1)} fusion(bf16[4096,1152]{1,0:T(8,128)(2,1)} %get-tuple-element.131, bf16[1024,864]{0,1:T(8,128)(2,1)} %get-tuple-element.63, bf16[1024,864]{0,1:T(8,128)(2,1)S(1)} %copy-done.164, bf16[1024,864]{0,1:T(8,128)(2,1)} %get-tuple-element.61, bf16[1024,864]{0,1:T(8,128)(2,1)S(1)} %copy-done.162), kind=kOutput, calls=%fused_computation.94 | convolution fusion | flops 8183033856 | bytes 18505728 | tf_op jit(solution)/shard_map/dot_general | solution.py:26
  424.0 6.0 convolution_add_fusion.1
  434.6 10.7 %fusion.46 = bf16[864,1152]{1,0:T(8,128)(2,1)} fusion(bf16[4096,1152]{1,0:T(8,128)(2,1)S(1)} %constant_dynamic-update-slice_fusion.16, bf16[1024,864]{0,1:T(8,128)(2,1)S(1)} %copy-done.81, bf16[1024,864]{0,1:T(8,128)(2,1)S(1)} %copy-done.77, bf16[1024,864]{0,1:T(8,128)(2,1)S(1)} %copy-done.79, bf16[1024,864]{0,1:T(8,128)(2,1)S(1)} %copy-done.75), kind=kOutput, calls=%fused_computation.93 | convolution fusion | flops 8183033856 | bytes 18505728 | tf_op jit(solution)/shard_map/dot_general | solution.py:26
  448.1 4.1 copy.265
  467.8 17.1 %collective-permute-done.80 = bf16[2,288,864]{2,1,0:T(8,128)(2,1)S(1)} collective-permute-done((bf16[2,288,864]{2,1,0:T(8,128)(2,1)S(1)}, bf16[2,288,864]{2,1,0:T(8,128)(2,1)S(1)}, u32[]{:S(2)}, u32[]{:S(2)}) %collective-permute-start.80) | collective-permute-done | bytes 995360 | tf_op jit(solution)/shard_map/ppermute | solution.py:134
  487.2 15.2 %collective-permute-done.55 = bf16[256,1152]{1,0:T(8,128)(2,1)S(1)} collective-permute-done((bf16[256,1152]{1,0:T(8,128)(2,1)S(1)}, bf16[256,1152]{1,0:T(8,128)(2,1)S(1)}, u32[]{:S(2)}, u32[]{:S(2)}) %collective-permute-start.55) | collective-permute-done | bytes 589856 | tf_op jit(solution)/shard_map/ppermute | solution.py:95
  505.2 6.8 collective-permute-done.89
  513.6 10.9 %collective-permute-done.51 = bf16[256,1152]{1,0:T(8,128)(2,1)S(1)} collective-permute-done((bf16[256,1152]{1,0:T(8,128)(2,1)S(1)}, bf16[256,1152]{1,0:T(8,128)(2,1)S(1)}, u32[]{:S(2)}, u32[]{:S(2)}) %collective-permute-start.51) | collective-permute-done | bytes 589856 | tf_op jit(solution)/shard_map/ppermute | solution.py:95
  532.8 14.7 %collective-permute-done.102 = bf16[432,1152]{1,0:T(8,128)(2,1)S(1)} collective-permute-done((bf16[432,1152]{1,0:T(8,128)(2,1)S(1)}, bf16[432,1152]{1,0:T(8,128)(2,1)S(1)}, u32[]{:S(2)}, u32[]{:S(2)}) %collective-permute-start.102) | collective-permute-done | bytes 995360 | tf_op jit(solution)/shard_map/ppermute | solution.py:134
  547.4 22.1 %collective-permute-done.95 = bf16[2,288,864]{2,1,0:T(8,128)(2,1)S(1)} collective-permute-done((bf16[2,288,864]{2,1,0:T(8,128)(2,1)S(1)}, bf16[2,288,864]{2,1,0:T(8,128)(2,1)S(1)}, u32[]{:S(2)}, u32[]{:S(2)}) %collective-permute-start.95) | collective-permute-done | bytes 995360 | tf_op jit(solution)/shard_map/ppermute | solution.py:134
  571.2 20.4 %collective-permute-done.90 = bf16[2,288,864]{2,1,0:T(8,128)(2,1)S(1)} collective-permute-done((bf16[2,288,864]{2,1,0:T(8,128)(2,1)S(1)}, bf16[2,288,864]{2,1,0:T(8,128)(2,1)S(1)}, u32[]{:S(2)}, u32[]{:S(2)}) %collective-permute-start.90) | collective-permute-done | bytes 995360 | tf_op jit(solution)/shard_map/ppermute | solution.py:134
  595.7 15.6 %collective-permute-done.85 = bf16[2,288,864]{2,1,0:T(8,128)(2,1)S(1)} collective-permute-done((bf16[2,288,864]{2,1,0:T(8,128)(2,1)S(1)}, bf16[2,288,864]{2,1,0:T(8,128)(2,1)S(1)}, u32[]{:S(2)}, u32[]{:S(2)}) %collective-permute-start.85) | collective-permute-done | bytes 995360 | tf_op jit(solution)/shard_map/ppermute | solution.py:134
  654.6 63.6 %collective-permute-done.104 = bf16[432,1152]{1,0:T(8,128)(2,1)} collective-permute-done((bf16[432,1152]{1,0:T(8,128)(2,1)}, bf16[432,1152]{1,0:T(8,128)(2,1)}, u32[]{:S(2)}, u32[]{:S(2)}) %collective-permute-start.104) | collective-permute-done | bytes 995360 | tf_op jit(solution)/shard_map/ppermute | solution.py:138
  723.4 15.4 %collective-permute-done.101 = bf16[432,1152]{1,0:T(8,128)(2,1)} collective-permute-done((bf16[432,1152]{1,0:T(8,128)(2,1)}, bf16[432,1152]{1,0:T(8,128)(2,1)}, u32[]{:S(2)}, u32[]{:S(2)}) %collective-permute-start.101) | collective-permute-done | bytes 995360 | tf_op jit(solution)/shard_map/ppermute | solution.py:138
  741.7 19.1 %collective-permute-done.97 = bf16[2,288,864]{2,1,0:T(8,128)(2,1)S(1)} collective-permute-done((bf16[2,288,864]{2,1,0:T(8,128)(2,1)S(1)}, bf16[2,288,864]{2,1,0:T(8,128)(2,1)S(1)}, u32[]{:S(2)}, u32[]{:S(2)}) %collective-permute-start.97) | collective-permute-done | bytes 995360 | tf_op jit(solution)/shard_map/ppermute | solution.py:138
  764.2 18.7 %collective-permute-done.92 = bf16[2,288,864]{2,1,0:T(8,128)(2,1)S(1)} collective-permute-done((bf16[2,288,864]{2,1,0:T(8,128)(2,1)S(1)}, bf16[2,288,864]{2,1,0:T(8,128)(2,1)S(1)}, u32[]{:S(2)}, u32[]{:S(2)}) %collective-permute-start.92) | collective-permute-done | bytes 995360 | tf_op jit(solution)/shard_map/ppermute | solution.py:138
  784.1 13.7 %collective-permute-done.87 = bf16[2,288,864]{2,1,0:T(8,128)(2,1)S(1)} collective-permute-done((bf16[2,288,864]{2,1,0:T(8,128)(2,1)S(1)}, bf16[2,288,864]{2,1,0:T(8,128)(2,1)S(1)}, u32[]{:S(2)}, u32[]{:S(2)}) %collective-permute-start.87) | collective-permute-done | bytes 995360 | tf_op jit(solution)/shard_map/ppermute | solution.py:138
  825.1 4.6 collective-permute-done.75
  891.5 7.9 concatenate.157
  899.4 5.9 convert_element_type.456
  905.2 7.6 concatenate.158
  912.9 5.9 convert_element_type.457
  921.2 6.1 collective-permute-start.68
  931.4 4.9 fusion.94
  949.3 23.3 %collective-permute-done.108 = f32[4,1280]{1,0:T(4,128)S(1)} collective-permute-done((f32[4,1280]{1,0:T(4,128)S(1)}, f32[4,1280]{1,0:T(4,128)S(1)}, u32[]{:S(2)}, u32[]{:S(2)}) %collective-permute-start.108) | collective-permute-done | bytes 20512 | tf_op jit(solution)/shard_map/ppermute | solution.py:98
  983.2 13.2 %collective-permute-done.70 = bf16[288,768]{1,0:T(8,128)(2,1)S(1)} collective-permute-done((bf16[288,768]{1,0:T(8,128)(2,1)S(1)}, bf16[288,768]{1,0:T(8,128)(2,1)S(1)}, u32[]{:S(2)}, u32[]{:S(2)}) %collective-permute-start.70) | collective-permute-done | bytes 442400 | tf_op jit(solution)/shard_map/ppermute | solution.py:138
  (838 shorter events, 442.6 us)
Async XLA Ops:
  2.1 31.2 %collective-permute-start.5 = (f32[1280]{0:T(1024)}, f32[1280]{0:T(1024)}, u32[]{:S(2)}, u32[]{:S(2)}) collective-permute-start(f32[1280]{0:T(1024)} %concatenate.123), channel_id=1, source_target_pairs={{0,24},{8,16},{16,8},{24,0},{1,25},{9,17},{17,9},{25,1},{2,26},{10... | collective-permute-start | bytes 15368 | tf_op jit(solution)/shard_map/ppermute | solution.py:95
  6.0 31.6 %collective-permute-start.4 = (f32[1280]{0:T(1024)}, f32[1280]{0:T(1024)}, u32[]{:S(2)}, u32[]{:S(2)}) collective-permute-start(f32[1280]{0:T(1024)} %concatenate.123), channel_id=1, source_target_pairs={{0,16},{8,24},{16,0},{24,8},{1,17},{9,25},{17,1},{25,9},{2,18},{10... | collective-permute-start | bytes 15368 | tf_op jit(solution)/shard_map/ppermute | solution.py:95
  6.5 31.8 %collective-permute-start.3 = (f32[1280]{0:T(1024)}, f32[1280]{0:T(1024)}, u32[]{:S(2)}, u32[]{:S(2)}) collective-permute-start(f32[1280]{0:T(1024)} %concatenate.123), channel_id=1, source_target_pairs={{0,8},{8,0},{16,24},{24,16},{1,9},{9,1},{17,25},{25,17},{2,10},{10... | collective-permute-start | bytes 15368 | tf_op jit(solution)/shard_map/ppermute | solution.py:95
  9.3 64.7 %collective-permute-start.9 = (bf16[288,768]{1,0:T(8,128)(2,1)}, bf16[288,768]{1,0:T(8,128)(2,1)}, u32[]{:S(2)}, u32[]{:S(2)}) collective-permute-start(bf16[288,768]{1,0:T(8,128)(2,1)} %get-tuple-element.196), channel_id=1, source_target_pairs={{0,24},{8,16},{16,8},{24,0},{1,25},{9,17},{17,9},{25,1},{2,26},{10... | collective-permute-start | bytes 1327112 | tf_op jit(solution)/shard_map/ppermute | solution.py:95
  12.3 62.2 %collective-permute-start.8 = (bf16[288,768]{1,0:T(8,128)(2,1)}, bf16[288,768]{1,0:T(8,128)(2,1)}, u32[]{:S(2)}, u32[]{:S(2)}) collective-permute-start(bf16[288,768]{1,0:T(8,128)(2,1)} %get-tuple-element.196), channel_id=1, source_target_pairs={{0,16},{8,24},{16,0},{24,8},{1,17},{9,25},{17,1},{25,9},{2,18},{10... | collective-permute-start | bytes 1327112 | tf_op jit(solution)/shard_map/ppermute | solution.py:95
  68.8 75.0 %collective-permute-start.19 = (bf16[2,288,864]{2,1,0:T(8,128)(2,1)}, bf16[2,288,864]{2,1,0:T(8,128)(2,1)}, u32[]{:S(2)}, u32[]{:S(2)}) collective-permute-start(bf16[2,288,864]{2,1,0:T(8,128)(2,1)} %pad_maximum_fusion.37), channel_id=1, source_target_pairs={{0,24},{8,16},{16,8},{24,0},{1,25},{9,17},{17,9},{25,1},{2,26},{10... | collective-permute-start | bytes 2985992 | tf_op jit(solution)/shard_map/ppermute | solution.py:95
  74.0 70.4 %collective-permute-start.18 = (bf16[2,288,864]{2,1,0:T(8,128)(2,1)}, bf16[2,288,864]{2,1,0:T(8,128)(2,1)}, u32[]{:S(2)}, u32[]{:S(2)}) collective-permute-start(bf16[2,288,864]{2,1,0:T(8,128)(2,1)} %pad_maximum_fusion.36), channel_id=1, source_target_pairs={{0,16},{8,24},{16,0},{24,8},{1,17},{9,25},{17,1},{25,9},{2,18},{10... | collective-permute-start | bytes 2985992 | tf_op jit(solution)/shard_map/ppermute | solution.py:95
  74.5 70.4 %collective-permute-start.17 = (bf16[2,288,864]{2,1,0:T(8,128)(2,1)}, bf16[2,288,864]{2,1,0:T(8,128)(2,1)}, u32[]{:S(2)}, u32[]{:S(2)}) collective-permute-start(bf16[2,288,864]{2,1,0:T(8,128)(2,1)} %pad_maximum_fusion.35), channel_id=1, source_target_pairs={{0,8},{8,0},{16,24},{24,16},{1,9},{9,1},{17,25},{25,17},{2,10},{10... | collective-permute-start | bytes 2985992 | tf_op jit(solution)/shard_map/ppermute | solution.py:95
  81.8 40.7 %collective-permute-start.15 = (bf16[4,128,1152]{2,1,0:T(8,128)(2,1)}, bf16[4,128,1152]{2,1,0:T(8,128)(2,1)}, u32[]{:S(2)}, u32[]{:S(2)}) collective-permute-start(bf16[4,128,1152]{2,1,0:T(8,128)(2,1)} %pad_maximum_fusion.19), channel_id=1, source_target_pairs={{0,1},{1,0},{2,3},{3,2},{4,5},{5,4},{6,7},{7,6},{8,9},{9,8},{10,11... | collective-permute-start | bytes 3538952 | tf_op jit(solution)/shard_map/ppermute | solution.py:101
  122.4 130.2 %collective-permute-start.40 = (bf16[128,1152]{1,0:T(8,128)(2,1)}, bf16[128,1152]{1,0:T(8,128)(2,1)}, u32[]{:S(2)}, u32[]{:S(2)}) collective-permute-start(bf16[128,1152]{1,0:T(8,128)(2,1)} %get-tuple-element.157), channel_id=1, source_target_pairs={{0,6},{2,4},{4,2},{6,0},{1,7},{3,5},{5,3},{7,1},{8,14},{10,12},{12... | collective-permute-start | bytes 884744 | tf_op jit(solution)/shard_map/ppermute | solution.py:98
  143.6 30.3 %collective-permute-start.16 = (bf16[512,1152]{1,0:T(8,128)(2,1)S(1)}, bf16[512,1152]{1,0:T(8,128)(2,1)S(1)}, u32[]{:S(2)}, u32[]{:S(2)}) collective-permute-start(bf16[512,1152]{1,0:T(8,128)(2,1)S(1)} %get-tuple-element.30), channel_id=1, source_target_pairs={{0,1},{1,0},{2,3},{3,2},{4,5},{5,4},{6,7},{7,6},{8,9},{9,8},{10,11... | collective-permute-start | bytes 3538952 | tf_op jit(solution)/shard_map/ppermute | solution.py:101
  189.8 79.5 %collective-permute-start.20 = (bf16[512,1152]{1,0:T(8,128)(2,1)}, bf16[512,1152]{1,0:T(8,128)(2,1)}, u32[]{:S(2)}, u32[]{:S(2)}) collective-permute-start(bf16[512,1152]{1,0:T(8,128)(2,1)} %slice.603), channel_id=1, source_target_pairs={{0,1},{1,0},{2,3},{3,2},{4,5},{5,4},{6,7},{7,6},{8,9},{9,8},{10,11... | collective-permute-start | bytes 3538952 | tf_op jit(solution)/shard_map/ppermute | solution.py:101
  298.2 166.0 %collective-permute-start.37 = (bf16[128,1152]{1,0:T(8,128)(2,1)}, bf16[128,1152]{1,0:T(8,128)(2,1)}, u32[]{:S(2)}, u32[]{:S(2)}) collective-permute-start(bf16[128,1152]{1,0:T(8,128)(2,1)} %get-tuple-element.164), channel_id=1, source_target_pairs={{0,6},{2,4},{4,2},{6,0},{1,7},{3,5},{5,3},{7,1},{8,14},{10,12},{12... | collective-permute-start | bytes 884744 | tf_op jit(solution)/shard_map/ppermute | solution.py:98
  299.5 165.8 %collective-permute-start.36 = (bf16[128,1152]{1,0:T(8,128)(2,1)}, bf16[128,1152]{1,0:T(8,128)(2,1)}, u32[]{:S(2)}, u32[]{:S(2)}) collective-permute-start(bf16[128,1152]{1,0:T(8,128)(2,1)} %get-tuple-element.165), channel_id=1, source_target_pairs={{0,4},{2,6},{4,0},{6,2},{1,5},{3,7},{5,1},{7,3},{8,12},{10,14},{12... | collective-permute-start | bytes 884744 | tf_op jit(solution)/shard_map/ppermute | solution.py:98
  339.2 146.6 %collective-permute-start.35 = (bf16[128,1152]{1,0:T(8,128)(2,1)}, bf16[128,1152]{1,0:T(8,128)(2,1)}, u32[]{:S(2)}, u32[]{:S(2)}) collective-permute-start(bf16[128,1152]{1,0:T(8,128)(2,1)} %get-tuple-element.166), channel_id=1, source_target_pairs={{0,2},{2,0},{4,6},{6,4},{1,3},{3,1},{5,7},{7,5},{8,10},{10,8},{12,... | collective-permute-start | bytes 884744 | tf_op jit(solution)/shard_map/ppermute | solution.py:98
  340.1 38.7 %collective-permute-start.49 = (bf16[512,1152]{1,0:T(8,128)(2,1)S(1)}, bf16[512,1152]{1,0:T(8,128)(2,1)S(1)}, u32[]{:S(2)}, u32[]{:S(2)}) collective-permute-start(bf16[512,1152]{1,0:T(8,128)(2,1)S(1)} %pad_maximum_fusion.27), channel_id=1, source_target_pairs={{0,1},{1,0},{2,3},{3,2},{4,5},{5,4},{6,7},{7,6},{8,9},{9,8},{10,11... | collective-permute-start | bytes 3538952 | tf_op jit(solution)/shard_map/ppermute | solution.py:101
  359.0 95.6 %collective-permute-start.54 = (bf16[512,1152]{1,0:T(8,128)(2,1)}, bf16[512,1152]{1,0:T(8,128)(2,1)}, u32[]{:S(2)}, u32[]{:S(2)}) collective-permute-start(bf16[512,1152]{1,0:T(8,128)(2,1)} %slice.596), channel_id=1, source_target_pairs={{0,1},{1,0},{2,3},{3,2},{4,5},{5,4},{6,7},{7,6},{8,9},{9,8},{10,11... | collective-permute-start | bytes 3538952 | tf_op jit(solution)/shard_map/ppermute | solution.py:101
  464.2 39.6 %collective-permute-start.94 = (bf16[2,288,864]{2,1,0:T(8,128)(2,1)S(1)}, bf16[2,288,864]{2,1,0:T(8,128)(2,1)S(1)}, u32[]{:S(2)}, u32[]{:S(2)}) collective-permute-start(bf16[2,288,864]{2,1,0:T(8,128)(2,1)S(1)} %get-tuple-element.70), channel_id=1, source_target_pairs={{0,24},{8,16},{16,8},{24,0},{1,25},{9,17},{17,9},{25,1},{2,26},{10... | collective-permute-start | bytes 2985992 | tf_op jit(solution)/shard_map/ppermute | solution.py:95
  465.3 46.7 %collective-permute-start.89 = (bf16[2,288,864]{2,1,0:T(8,128)(2,1)S(1)}, bf16[2,288,864]{2,1,0:T(8,128)(2,1)S(1)}, u32[]{:S(2)}, u32[]{:S(2)}) collective-permute-start(bf16[2,288,864]{2,1,0:T(8,128)(2,1)S(1)} %get-tuple-element.69), channel_id=1, source_target_pairs={{0,16},{8,24},{16,0},{24,8},{1,17},{9,25},{17,1},{25,9},{2,18},{10... | collective-permute-start | bytes 2985992 | tf_op jit(solution)/shard_map/ppermute | solution.py:95
  466.3 36.1 %collective-permute-start.55 = (bf16[256,1152]{1,0:T(8,128)(2,1)S(1)}, bf16[256,1152]{1,0:T(8,128)(2,1)S(1)}, u32[]{:S(2)}, u32[]{:S(2)}) collective-permute-start(bf16[256,1152]{1,0:T(8,128)(2,1)S(1)} %get-tuple-element.150), channel_id=1, source_target_pairs={{0,8},{8,0},{16,24},{24,16},{1,9},{9,1},{17,25},{25,17},{2,10},{10... | collective-permute-start | bytes 1769480 | tf_op jit(solution)/shard_map/ppermute | solution.py:95
  484.8 39.6 %collective-permute-start.51 = (bf16[256,1152]{1,0:T(8,128)(2,1)S(1)}, bf16[256,1152]{1,0:T(8,128)(2,1)S(1)}, u32[]{:S(2)}, u32[]{:S(2)}) collective-permute-start(bf16[256,1152]{1,0:T(8,128)(2,1)S(1)} %get-tuple-element.149), channel_id=1, source_target_pairs={{0,16},{8,24},{16,0},{24,8},{1,17},{9,25},{17,1},{25,9},{2,18},{10... | collective-permute-start | bytes 1769480 | tf_op jit(solution)/shard_map/ppermute | solution.py:95
  485.7 40.4 %collective-permute-start.84 = (bf16[2,288,864]{2,1,0:T(8,128)(2,1)S(1)}, bf16[2,288,864]{2,1,0:T(8,128)(2,1)S(1)}, u32[]{:S(2)}, u32[]{:S(2)}) collective-permute-start(bf16[2,288,864]{2,1,0:T(8,128)(2,1)S(1)} %get-tuple-element.68), channel_id=1, source_target_pairs={{0,8},{8,0},{16,24},{24,16},{1,9},{9,1},{17,25},{25,17},{2,10},{10... | collective-permute-start | bytes 2985992 | tf_op jit(solution)/shard_map/ppermute | solution.py:95
  503.9 43.6 %collective-permute-start.102 = (bf16[432,1152]{1,0:T(8,128)(2,1)S(1)}, bf16[432,1152]{1,0:T(8,128)(2,1)S(1)}, u32[]{:S(2)}, u32[]{:S(2)}) collective-permute-start(bf16[432,1152]{1,0:T(8,128)(2,1)S(1)} %get-tuple-element.124), channel_id=1, source_target_pairs={{0,2},{6,4},{1,3},{7,5},{8,10},{14,12},{9,11},{15,13},{16,18},{22,... | collective-permute-start | bytes 2985992 | tf_op jit(solution)/shard_map/ppermute | solution.py:134
  512.0 57.5 %collective-permute-start.95 = (bf16[2,288,864]{2,1,0:T(8,128)(2,1)S(1)}, bf16[2,288,864]{2,1,0:T(8,128)(2,1)S(1)}, u32[]{:S(2)}, u32[]{:S(2)}) collective-permute-start(bf16[2,288,864]{2,1,0:T(8,128)(2,1)S(1)} %collective-permute-done.94), channel_id=1, source_target_pairs={{0,2},{6,4},{1,3},{7,5},{8,10},{14,12},{9,11},{15,13},{16,18},{22,... | collective-permute-start | bytes 2985992 | tf_op jit(solution)/shard_map/ppermute | solution.py:134
  524.4 67.2 %collective-permute-start.90 = (bf16[2,288,864]{2,1,0:T(8,128)(2,1)S(1)}, bf16[2,288,864]{2,1,0:T(8,128)(2,1)S(1)}, u32[]{:S(2)}, u32[]{:S(2)}) collective-permute-start(bf16[2,288,864]{2,1,0:T(8,128)(2,1)S(1)} %collective-permute-done.89), channel_id=1, source_target_pairs={{0,2},{6,4},{1,3},{7,5},{8,10},{14,12},{9,11},{15,13},{16,18},{22,... | collective-permute-start | bytes 2985992 | tf_op jit(solution)/shard_map/ppermute | solution.py:134
  526.1 86.8 %collective-permute-start.81 = (bf16[2,288,864]{2,1,0:T(8,128)(2,1)S(1)}, bf16[2,288,864]{2,1,0:T(8,128)(2,1)S(1)}, u32[]{:S(2)}, u32[]{:S(2)}) collective-permute-start(bf16[2,288,864]{2,1,0:T(8,128)(2,1)S(1)} %add.558), channel_id=1, source_target_pairs={{2,4},{4,2},{3,5},{5,3},{10,12},{12,10},{11,13},{13,11},{18,20},{2... | collective-permute-start | bytes 2985992 | tf_op jit(solution)/shard_map/ppermute | solution.py:136
  526.9 84.4 %collective-permute-start.85 = (bf16[2,288,864]{2,1,0:T(8,128)(2,1)S(1)}, bf16[2,288,864]{2,1,0:T(8,128)(2,1)S(1)}, u32[]{:S(2)}, u32[]{:S(2)}) collective-permute-start(bf16[2,288,864]{2,1,0:T(8,128)(2,1)S(1)} %collective-permute-done.84), channel_id=1, source_target_pairs={{0,2},{6,4},{1,3},{7,5},{8,10},{14,12},{9,11},{15,13},{16,18},{22,... | collective-permute-start | bytes 2985992 | tf_op jit(solution)/shard_map/ppermute | solution.py:134
  547.4 87.1 %collective-permute-start.42 = (bf16[512,1152]{1,0:T(8,128)(2,1)}, bf16[512,1152]{1,0:T(8,128)(2,1)}, u32[]{:S(2)}, u32[]{:S(2)}) collective-permute-start(bf16[512,1152]{1,0:T(8,128)(2,1)} %slice.599), channel_id=1, source_target_pairs={{0,1},{1,0},{2,3},{3,2},{4,5},{5,4},{6,7},{7,6},{8,9},{9,8},{10,11... | collective-permute-start | bytes 3538952 | tf_op jit(solution)/shard_map/ppermute | solution.py:101
  569.5 66.7 %collective-permute-start.56 = (bf16[512,1152]{1,0:T(8,128)(2,1)}, bf16[512,1152]{1,0:T(8,128)(2,1)}, u32[]{:S(2)}, u32[]{:S(2)}) collective-permute-start(bf16[512,1152]{1,0:T(8,128)(2,1)} %pad_maximum_fusion.29), channel_id=1, source_target_pairs={{0,16},{8,24},{16,0},{24,8},{1,17},{9,25},{17,1},{25,9},{2,18},{10... | collective-permute-start | bytes 3538952 | tf_op jit(solution)/shard_map/ppermute | solution.py:95
  592.7 44.9 %collective-permute-start.52 = (bf16[512,1152]{1,0:T(8,128)(2,1)}, bf16[512,1152]{1,0:T(8,128)(2,1)}, u32[]{:S(2)}, u32[]{:S(2)}) collective-permute-start(bf16[512,1152]{1,0:T(8,128)(2,1)} %pad_maximum_fusion.28), channel_id=1, source_target_pairs={{0,8},{8,0},{16,24},{24,16},{1,9},{9,1},{17,25},{25,17},{2,10},{10... | collective-permute-start | bytes 3538952 | tf_op jit(solution)/shard_map/ppermute | solution.py:95
  636.3 84.5 %collective-permute-start.82 = (bf16[2,288,864]{2,1,0:T(8,128)(2,1)}, bf16[2,288,864]{2,1,0:T(8,128)(2,1)}, u32[]{:S(2)}, u32[]{:S(2)}) collective-permute-start(bf16[2,288,864]{2,1,0:T(8,128)(2,1)} %add.559), channel_id=1, source_target_pairs={{2,0},{4,6},{3,1},{5,7},{10,8},{12,14},{11,9},{13,15},{18,16},{20,... | collective-permute-start | bytes 2985992 | tf_op jit(solution)/shard_map/ppermute | solution.py:138
  637.6 80.6 %collective-permute-start.104 = (bf16[432,1152]{1,0:T(8,128)(2,1)}, bf16[432,1152]{1,0:T(8,128)(2,1)}, u32[]{:S(2)}, u32[]{:S(2)}) collective-permute-start(bf16[432,1152]{1,0:T(8,128)(2,1)} %add.569), channel_id=1, source_target_pairs={{2,0},{4,6},{3,1},{5,7},{10,8},{12,14},{11,9},{13,15},{18,16},{20,... | collective-permute-start | bytes 2985992 | tf_op jit(solution)/shard_map/ppermute | solution.py:138
  643.6 95.2 %collective-permute-start.101 = (bf16[432,1152]{1,0:T(8,128)(2,1)}, bf16[432,1152]{1,0:T(8,128)(2,1)}, u32[]{:S(2)}, u32[]{:S(2)}) collective-permute-start(bf16[432,1152]{1,0:T(8,128)(2,1)} %add.567), channel_id=1, source_target_pairs={{2,0},{4,6},{3,1},{5,7},{10,8},{12,14},{11,9},{13,15},{18,16},{20,... | collective-permute-start | bytes 2985992 | tf_op jit(solution)/shard_map/ppermute | solution.py:138
  649.6 149.3 %collective-permute-start.57 = (bf16[4,128,1152]{2,1,0:T(8,128)(2,1)S(1)}, bf16[4,128,1152]{2,1,0:T(8,128)(2,1)S(1)}, u32[]{:S(2)}, u32[]{:S(2)}) collective-permute-start(bf16[4,128,1152]{2,1,0:T(8,128)(2,1)S(1)} %bitcast.410), channel_id=1, source_target_pairs={{0,1},{1,0},{2,3},{3,2},{4,5},{5,4},{6,7},{7,6},{8,9},{9,8},{10,11... | collective-permute-start | bytes 3538952 | tf_op jit(solution)/shard_map/ppermute | solution.py:101
  651.5 109.4 %collective-permute-start.97 = (bf16[2,288,864]{2,1,0:T(8,128)(2,1)S(1)}, bf16[2,288,864]{2,1,0:T(8,128)(2,1)S(1)}, u32[]{:S(2)}, u32[]{:S(2)}) collective-permute-start(bf16[2,288,864]{2,1,0:T(8,128)(2,1)S(1)} %add.565), channel_id=1, source_target_pairs={{2,0},{4,6},{3,1},{5,7},{10,8},{12,14},{11,9},{13,15},{18,16},{20,... | collective-permute-start | bytes 2985992 | tf_op jit(solution)/shard_map/ppermute | solution.py:138
  718.1 64.9 %collective-permute-start.92 = (bf16[2,288,864]{2,1,0:T(8,128)(2,1)S(1)}, bf16[2,288,864]{2,1,0:T(8,128)(2,1)S(1)}, u32[]{:S(2)}, u32[]{:S(2)}) collective-permute-start(bf16[2,288,864]{2,1,0:T(8,128)(2,1)S(1)} %add.563), channel_id=1, source_target_pairs={{2,0},{4,6},{3,1},{5,7},{10,8},{12,14},{11,9},{13,15},{18,16},{20,... | collective-permute-start | bytes 2985992 | tf_op jit(solution)/shard_map/ppermute | solution.py:138
  720.8 77.0 %collective-permute-start.87 = (bf16[2,288,864]{2,1,0:T(8,128)(2,1)S(1)}, bf16[2,288,864]{2,1,0:T(8,128)(2,1)S(1)}, u32[]{:S(2)}, u32[]{:S(2)}) collective-permute-start(bf16[2,288,864]{2,1,0:T(8,128)(2,1)S(1)} %add.561), channel_id=1, source_target_pairs={{2,0},{4,6},{3,1},{5,7},{10,8},{12,14},{11,9},{13,15},{18,16},{20,... | collective-permute-start | bytes 2985992 | tf_op jit(solution)/shard_map/ppermute | solution.py:138
  760.9 114.0 %collective-permute-start.105 = (bf16[864,1152]{1,0:T(8,128)(2,1)}, bf16[864,1152]{1,0:T(8,128)(2,1)}, u32[]{:S(2)}, u32[]{:S(2)}) collective-permute-start(bf16[864,1152]{1,0:T(8,128)(2,1)} %pad_maximum_fusion.10), channel_id=1, source_target_pairs={{0,1},{1,0},{2,3},{3,2},{4,5},{5,4},{6,7},{7,6},{8,9},{9,8},{10,11... | collective-permute-start | bytes 5971976 | tf_op jit(solution)/shard_map/ppermute | solution.py:101
  762.0 106.8 %collective-permute-start.98 = (bf16[2,288,864]{2,1,0:T(8,128)(2,1)}, bf16[2,288,864]{2,1,0:T(8,128)(2,1)}, u32[]{:S(2)}, u32[]{:S(2)}) collective-permute-start(bf16[2,288,864]{2,1,0:T(8,128)(2,1)} %broadcast_select_fusion), channel_id=1, source_target_pairs={{0,1},{1,0},{2,3},{3,2},{4,5},{5,4},{6,7},{7,6},{8,9},{9,8},{10,11... | collective-permute-start | bytes 2985992 | tf_op jit(solution)/shard_map/ppermute | solution.py:101
  831.0 30.5 %collective-permute-start.76 = (bf16[128,1152]{1,0:T(8,128)(2,1)}, bf16[128,1152]{1,0:T(8,128)(2,1)}, u32[]{:S(2)}, u32[]{:S(2)}) collective-permute-start(bf16[128,1152]{1,0:T(8,128)(2,1)} %fusion.137), channel_id=1, source_target_pairs={{0,2},{6,4},{1,3},{7,5},{8,10},{14,12},{9,11},{15,13},{16,18},{22,... | collective-permute-start | bytes 884744 | tf_op jit(solution)/shard_map/ppermute | solution.py:134
  865.7 63.3 %collective-permute-start.60 = (bf16[1024,512]{1,0:T(8,128)(2,1)}, bf16[1024,512]{1,0:T(8,128)(2,1)}, u32[]{:S(2)}, u32[]{:S(2)}) collective-permute-start(bf16[1024,512]{1,0:T(8,128)(2,1)} %copy-done.44), channel_id=1, source_target_pairs={{0,1},{1,0},{2,3},{3,2},{4,5},{5,4},{6,7},{7,6},{8,9},{9,8},{10,11... | collective-permute-start | bytes 3145736 | tf_op jit(solution)/shard_map/ppermute | solution.py:101
  871.7 47.1 %collective-permute-start.67 = (bf16[288,768]{1,0:T(8,128)(2,1)}, bf16[288,768]{1,0:T(8,128)(2,1)}, u32[]{:S(2)}, u32[]{:S(2)}) collective-permute-start(bf16[288,768]{1,0:T(8,128)(2,1)} %pad_maximum_fusion.43), channel_id=1, source_target_pairs={{0,16},{8,24},{16,0},{24,8},{1,17},{9,25},{17,1},{25,9},{2,18},{10... | collective-permute-start | bytes 1327112 | tf_op jit(solution)/shard_map/ppermute | solution.py:95
  874.9 43.9 %collective-permute-start.65 = (bf16[288,768]{1,0:T(8,128)(2,1)}, bf16[288,768]{1,0:T(8,128)(2,1)}, u32[]{:S(2)}, u32[]{:S(2)}) collective-permute-start(bf16[288,768]{1,0:T(8,128)(2,1)} %pad_maximum_fusion.42), channel_id=1, source_target_pairs={{0,8},{8,0},{16,24},{24,16},{1,9},{9,1},{17,25},{25,17},{2,10},{10... | collective-permute-start | bytes 1327112 | tf_op jit(solution)/shard_map/ppermute | solution.py:95
  887.2 40.0 %collective-permute-start.78 = (bf16[128,1152]{1,0:T(8,128)(2,1)}, bf16[128,1152]{1,0:T(8,128)(2,1)}, u32[]{:S(2)}, u32[]{:S(2)}) collective-permute-start(bf16[128,1152]{1,0:T(8,128)(2,1)} %add.557), channel_id=1, source_target_pairs={{2,0},{4,6},{3,1},{5,7},{10,8},{12,14},{11,9},{13,15},{18,16},{20,... | collective-permute-start | bytes 884744 | tf_op jit(solution)/shard_map/ppermute | solution.py:138
  921.2 52.7 %collective-permute-start.68 = (bf16[288,768]{1,0:T(8,128)(2,1)}, bf16[288,768]{1,0:T(8,128)(2,1)}, u32[]{:S(2)}, u32[]{:S(2)}) collective-permute-start(bf16[288,768]{1,0:T(8,128)(2,1)} %fusion.125), channel_id=1, source_target_pairs={{0,2},{6,4},{1,3},{7,5},{8,10},{14,12},{9,11},{15,13},{16,18},{22,... | collective-permute-start | bytes 1327112 | tf_op jit(solution)/shard_map/ppermute | solution.py:134
  942.6 40.4 %collective-permute-start.63 = (bf16[128,1152]{1,0:T(8,128)(2,1)S(1)}, bf16[128,1152]{1,0:T(8,128)(2,1)S(1)}, u32[]{:S(2)}, u32[]{:S(2)}) collective-permute-start(bf16[128,1152]{1,0:T(8,128)(2,1)S(1)} %get-tuple-element.146), channel_id=1, source_target_pairs={{0,6},{2,4},{4,2},{6,0},{1,7},{3,5},{5,3},{7,1},{8,14},{10,12},{12... | collective-permute-start | bytes 884744 | tf_op jit(solution)/shard_map/ppermute | solution.py:98
  944.0 39.0 %collective-permute-start.62 = (bf16[128,1152]{1,0:T(8,128)(2,1)S(1)}, bf16[128,1152]{1,0:T(8,128)(2,1)S(1)}, u32[]{:S(2)}, u32[]{:S(2)}) collective-permute-start(bf16[128,1152]{1,0:T(8,128)(2,1)S(1)} %get-tuple-element.147), channel_id=1, source_target_pairs={{0,4},{2,6},{4,0},{6,2},{1,5},{3,7},{5,1},{7,3},{8,12},{10,14},{12... | collective-permute-start | bytes 884744 | tf_op jit(solution)/shard_map/ppermute | solution.py:98
  946.3 36.7 %collective-permute-start.61 = (bf16[128,1152]{1,0:T(8,128)(2,1)S(1)}, bf16[128,1152]{1,0:T(8,128)(2,1)S(1)}, u32[]{:S(2)}, u32[]{:S(2)}) collective-permute-start(bf16[128,1152]{1,0:T(8,128)(2,1)S(1)} %get-tuple-element.148), channel_id=1, source_target_pairs={{0,2},{2,0},{4,6},{6,4},{1,3},{3,1},{5,7},{7,5},{8,10},{10,8},{12,... | collective-permute-start | bytes 884744 | tf_op jit(solution)/shard_map/ppermute | solution.py:98
  (239 other events, 2944.7 us)

commit v2 on v1

v2 whole, which is shorter than its diff:
```python
import functools

import jax
import jax.numpy as jnp
from jax import lax
from jax.experimental import pallas as pl
from jax.experimental.pallas import tpu as pltpu
from jax.sharding import Mesh
from jax.sharding import PartitionSpec as P

HEADS = 4
HD = 256
PIECE = 256
EPS = 1e-06
ROPE_BASE = 1000000.0
SCALE = 0.0625
BF = jnp.bfloat16
F32 = jnp.float32
VMEM = 56 * 1024 * 1024


def dot(a, b):
    return lax.dot_general(a, b, (((1,), (0,)), ((), ())), preferred_element_type=F32)


def dot_t(a, b):
    return lax.dot_general(a, b, (((1,), (1,)), ((), ())), preferred_element_type=F32)


def dot_rows(a, b):
    return lax.dot_general(a, b, (((0,), (0,)), ((), ())), preferred_element_type=F32)


def inv_rms(v):
    return lax.rsqrt(jnp.mean(v * v, axis=-1, keepdims=True) + EPS)


def rms_back(v, r, gain, z):
    gz = gain * z
    return r * gz - v * (r * r * r * jnp.mean(gz * v, axis=-1, keepdims=True))


def rope(v, cos, sin):
    half = v.shape[-1] // 2
    a, b = v[..., :half], v[..., half:]
    return jnp.concatenate([a * cos - b * sin, b * cos + a * sin], axis=-1)


def gelu_and_slope(u):
    k = 0.7978845608028654
    u2 = u * u
    t = jnp.tanh(k * (u + 0.044715 * u2 * u))
    half = 0.5 * (1.0 + t)
    slope = half + 0.5 * u * (1.0 - t * t) * (k * (1.0 + 3.0 * 0.044715 * u2))
    return u * half, slope


def call(kernel, grid, in_specs, out_specs, out_shape, flops, nbytes, scalars=0, scratch=(), exps=0):
    return pl.pallas_call(
        kernel,
        grid_spec=pltpu.PrefetchScalarGridSpec(
            num_scalar_prefetch=scalars,
            grid=grid,
            in_specs=in_specs,
            out_specs=out_specs,
            scratch_shapes=list(scratch),
        ),
        out_shape=out_shape,
        compiler_params=pltpu.CompilerParams(
            dimension_semantics=("arbitrary",) * len(grid), vmem_limit_bytes=VMEM
        ),
        cost_estimate=pl.CostEstimate(flops=flops, bytes_accessed=nbytes, transcendentals=exps),
    )


def full(shape):
    return pl.BlockSpec(shape, lambda *_: (0,) * len(shape))


def qkv_kernel(at, own, oth, w, ga, gq, gk, cos, sin, nin_o, raw_o, q_o, k_o, v_o):
    first = at[1] == 0
    a, b = own[0], oth[0]
    x = jnp.concatenate([jnp.where(first, a, b), jnp.where(first, b, a)]).astype(F32)
    nin = (x * inv_rms(x) * ga[...]).astype(BF)
    nin_o[...] = nin
    raw = dot(nin, w[...])
    raw_o[...] = raw[:, : 3 * HD]
    c, s = cos[...], sin[...]
    for h in range(2):
        q = raw[:, h * HD : (h + 1) * HD]
        q_o[:, h * HD : (h + 1) * HD] = rope(q * inv_rms(q) * gq[...], c, s).astype(BF)
    k = raw[:, 2 * HD : 3 * HD]
    k_o[...] = rope(k * inv_rms(k) * gk[...], c, s).astype(BF)
    v_o[...] = raw[:, 3 * HD :].astype(BF)


def project(at, own, oth, w, ga, gq, gk, cos, sin):
    seqs, n, width = own.shape
    rows = 2 * n * seqs
    cols = w.shape[1]
    block = pl.BlockSpec((1, n, width), lambda i, at: (i ^ at[0], 0, 0))

    def row(c):
        return pl.BlockSpec((2 * n, c), lambda i, at: (i, 0))

    shapes = [(width, BF), (3 * HD, F32), (2 * HD, BF), (HD, BF), (HD, BF)]
    return call(
        qkv_kernel,
        (seqs,),
        [block, block, full(w.shape), full(ga.shape), full(gq.shape), full(gk.shape), row(HD // 2), row(HD // 2)],
        [row(c) for c, _ in shapes],
        [jax.ShapeDtypeStruct((rows, c), t) for c, t in shapes],
        2 * rows * width * cols,
        rows * width * 8 + width * cols * 2,
        scalars=1,
    )(at, own, oth, w, ga, gq, gk, cos, sin)


def allowed(at, i, tile, length, transposed):
    a, b = (1, 0) if transposed else (0, 1)
    shape_q = (1, tile) if transposed else (tile, 1)
    shape_k = (length, 1) if transposed else (1, length)
    q = at[2] + i * tile + lax.broadcasted_iota(jnp.int32, shape_q, a)
    k = lax.broadcasted_iota(jnp.int32, shape_k, b)
    ok = k <= q
    for j in range(2):
        s = at[3 + j]
        ok = ok | (((q >= s) & (q < s + PIECE)) & ((k >= s) & (k < s + PIECE)))
    return ok


def attend_kernel(tile, at, q, k, v, o):
    s = dot_t(q[...], k[...]) * SCALE
    s = jnp.where(allowed(at, pl.program_id(1), tile, k.shape[0], False), s, -1e30)
    e = jnp.exp(s - jnp.max(s, axis=-1, keepdims=True))
    p = (e * (1.0 / jnp.sum(e, axis=-1, keepdims=True))).astype(BF)
    o[...] = dot(p, v[...]).astype(BF)


def attend(at, q, k, v, tile=256):
    rows, length = q.shape[0], k.shape[0]
    heads = q.shape[1] // HD
    qs = pl.BlockSpec((tile, HD), lambda h, i, at: (i, h))
    return call(
        functools.partial(attend_kernel, tile),
        (heads, rows // tile),
        [qs, full(k.shape), full(v.shape)],
        qs,
        jax.ShapeDtypeStruct(q.shape, BF),
        4 * rows * heads * length * HD,
        rows * heads * HD * 4 + length * HD * 4,
        scalars=1,
        exps=rows * heads * length,
    )(at, q, k, v)


def attend_back_kernel(tile, at, q, k, v, do, qraw, gq, cos, sin, dq_o, dk_o, dv_o, gg_o):
    @pl.when((pl.program_id(0) == 0) & (pl.program_id(1) == 0))
    def _():
        dk_o[...] = jnp.zeros_like(dk_o)
        dv_o[...] = jnp.zeros_like(dv_o)
        gg_o[...] = jnp.zeros_like(gg_o)

    s = dot_t(k[...], q[...]) * SCALE
    s = jnp.where(allowed(at, pl.program_id(1), tile, k.shape[0], True), s, -1e30)
    e = jnp.exp(s - jnp.max(s, axis=0, keepdims=True))
    p = e * (1.0 / jnp.sum(e, axis=0, keepdims=True))
    dp = dot_t(v[...], do[...])
    ds = (p * (dp - jnp.sum(p * dp, axis=0, keepdims=True))).astype(BF)
    dv_o[...] += dot(p.astype(BF), do[...])
    dk_o[...] += dot(ds, q[...]) * SCALE
    dq = dot_rows(ds, k[...]) * SCALE
    un = rope(dq, cos[...], -sin[...])
    raw = qraw[...]
    r = inv_rms(raw)
    gg_o[...] += jnp.sum(un * raw * r, axis=0, keepdims=True)
    dq_o[...] = rms_back(raw, r, gq[...], un).astype(BF)


def attend_back(at, q, k, v, do, raw, gq, cos, sin, tile=256):
    rows, length = q.shape[0], k.shape[0]
    heads = q.shape[1] // HD
    qs = pl.BlockSpec((tile, HD), lambda h, i, at: (i, h))
    cs = pl.BlockSpec((tile, HD // 2), lambda h, i, at: (i, 0))
    return call(
        functools.partial(attend_back_kernel, tile),
        (heads, rows // tile),
        [qs, full(k.shape), full(v.shape), qs, qs, full(gq.shape), cs, cs],
        [qs, full(k.shape), full(v.shape), full(gq.shape)],
        [
            jax.ShapeDtypeStruct(q.shape, BF),
            jax.ShapeDtypeStruct(k.shape, F32),
            jax.ShapeDtypeStruct(v.shape, F32),
            jax.ShapeDtypeStruct(gq.shape, F32),
        ],
        10 * rows * heads * length * HD,
        rows * heads * HD * 12 + length * HD * 12,
        scalars=1,
        exps=rows * heads * length,
    )(at, q, k, v, do, raw, gq, cos, sin)


def ffn_kernel(at, x, w, wd, g_o, u_o, h_o, p_o, acc):
    h = pl.program_id(0)
    xv = x[...]
    n_d, _, d, f = w.shape[1:]
    g = dot(xv, w[0, :, 0].reshape(n_d * d, f))
    u = dot(xv, w[0, :, 1].reshape(n_d * d, f))
    g_o[0] = g.astype(BF)
    u_o[0] = u.astype(BF)
    hid = (gelu_and_slope(g)[0] * u).astype(BF)
    h_o[0] = hid
    part = dot(hid, wd[...])

    @pl.when(h == 0)
    def _():
        acc[...] = part

    @pl.when(h == 1)
    def _():
        p_o[...] = (acc[...] + part).astype(p_o.dtype)


def ffn(at, x, w, wd, kind):
    rows, width = x.shape
    f = w.shape[-1]
    act = pl.BlockSpec((1, rows, f), lambda h, at: (h, 0, 0))
    return call(
        ffn_kernel,
        (2,),
        [
            full(x.shape),
            pl.BlockSpec((1,) + w.shape[1:], lambda h, at: (h, 0, 0, 0, 0)),
            pl.BlockSpec((f, width), lambda h, at: (h ^ at[1], 0)),
        ],
        [act, act, act, full(x.shape)],
        [jax.ShapeDtypeStruct((2, rows, f), BF)] * 3 + [jax.ShapeDtypeStruct(x.shape, kind)],
        12 * rows * width * f,
        12 * width * f + 16 * rows * f + 6 * rows * width,
        scalars=1,
        scratch=[pltpu.VMEM(x.shape, F32)],
        exps=2 * rows * f,
    )(at, x, w, wd)


def ffn_back_kernel(at, z, w, wd, g, u, gg_o, ug_o, p_o, acc):
    h = pl.program_id(0)
    n_d, _, d, f = w.shape[1:]
    hg = dot_t(z[...], wd[...])
    gel, slope = gelu_and_slope(g[0].astype(F32))
    gg = (hg * u[0].astype(F32) * slope).astype(BF)
    ug = (hg * gel).astype(BF)
    gg_o[0] = gg
    ug_o[0] = ug
    part = dot_t(gg, w[0, :, 0].reshape(n_d * d, f)) + dot_t(ug, w[0, :, 1].reshape(n_d * d, f))

    @pl.when(h == 0)
    def _():
        acc[...] = part

    @pl.when(h == 1)
    def _():
        p_o[...] = (acc[...] + part).astype(p_o.dtype)


def ffn_back(at, z, w, wd, g, u, kind):
    rows, width = z.shape
    f = w.shape[-1]
    act = pl.BlockSpec((1, rows, f), lambda h, at: (h, 0, 0))
    return call(
        ffn_back_kernel,
        (2,),
        [
            full(z.shape),
            pl.BlockSpec((1,) + w.shape[1:], lambda h, at: (h, 0, 0, 0, 0)),
            pl.BlockSpec((f, width), lambda h, at: (h ^ at[1], 0)),
            act,
            act,
        ],
        [act, act, full(z.shape)],
        [jax.ShapeDtypeStruct((2, rows, f), BF)] * 2 + [jax.ShapeDtypeStruct(z.shape, kind)],
        12 * rows * width * f,
        12 * width * f + 16 * rows * f + 6 * rows * width,
        scalars=1,
        scratch=[pltpu.VMEM(z.shape, F32)],
        exps=2 * rows * f,
    )(at, z, w, wd, g, u)


def gate_up_grad_kernel(n, add, *refs):
    x, g, u = refs[:n], refs[n : 2 * n], refs[2 * n : 3 * n]
    o = refs[-1]
    for m, v in ((0, g), (1, u)):
        total = dot_rows(x[0][...], v[0][0])
        for k in range(1, n):
            total += dot_rows(x[k][...], v[k][0])
        if add:
            total += refs[3 * n][m].astype(F32)
        o[m] = total.astype(BF)


def gate_up_grad(h, xs, gs, us, more, tile=384):
    n = len(xs)
    rows, width = xs[0].shape
    f = gs[0].shape[-1]
    out = pl.BlockSpec((2, tile, f), lambda i: (0, i, 0))
    return call(
        functools.partial(gate_up_grad_kernel, n, more is not None),
        (width // tile,),
        [pl.BlockSpec((rows, tile), lambda i: (0, i))] * n
        + [pl.BlockSpec((1, rows, f), lambda i: (h, 0, 0))] * (2 * n)
        + ([out] if more is not None else []),
        out,
        jax.ShapeDtypeStruct((2, width, f), BF),
        4 * n * rows * width * f,
        n * rows * (width + 2 * f) * 2 + 4 * width * f,
    )(*xs, *gs, *us, *([more] if more is not None else []))


def down_grad_kernel(n, add, *refs):
    hid, z = refs[:n], refs[n : 2 * n]
    o = refs[-1]
    total = dot_rows(hid[0][0], z[0][...])
    for k in range(1, n):
        total += dot_rows(hid[k][0], z[k][...])
    if add:
        total += refs[2 * n][...].astype(F32)
    o[...] = total.astype(BF)


def down_grad(h, hids, zs, more, tile=384):
    n = len(zs)
    rows, width = zs[0].shape
    f = hids[0].shape[-1]
    out = pl.BlockSpec((f, tile), lambda i: (0, i))
    return call(
        functools.partial(down_grad_kernel, n, more is not None),
        (width // tile,),
        [pl.BlockSpec((1, rows, f), lambda i: (h, 0, 0))] * n
        + [pl.BlockSpec((rows, tile), lambda i: (0, i))] * n
        + ([out] if more is not None else []),
        out,
        jax.ShapeDtypeStruct((f, width), BF),
        2 * n * rows * width * f,
        n * rows * (width + f) * 2 + 2 * width * f,
    )(*hids, *zs, *([more] if more is not None else []))


def lay_kernel(n_s, at, mine, oth, g_o, u_o):
    f = mine.shape[-1]
    first = at[1] == 0
    for m, o in ((0, g_o), (1, u_o)):
        for j in range(n_s):
            a, b = mine[0, j, m].astype(F32), oth[0, j, m].astype(F32)
            o[:, 2 * j * f : (2 * j + 1) * f] = jnp.where(first, a, b)
            o[:, (2 * j + 1) * f : (2 * j + 2) * f] = jnp.where(first, b, a)


def lay(at, mine, oth):
    n_z, n_s, _, rows, f = mine.shape
    block = pl.BlockSpec((1,) + mine.shape[1:], lambda i, at: (i, 0, 0, 0, 0))
    out = pl.BlockSpec((rows, 2 * n_s * f), lambda i, at: (i, 0))
    return call(
        functools.partial(lay_kernel, n_s),
        (n_z,),
        [block, block],
        [out, out],
        [jax.ShapeDtypeStruct((n_z * rows, 2 * n_s * f), F32)] * 2,
        0,
        n_z * n_s * rows * f * 24,
        scalars=1,
    )(at, mine, oth)


def body(
    tokens,
    cotangent,
    pictures,
    w_query,
    w_key,
    w_value,
    w_out,
    w_gate,
    w_up,
    w_down,
    g_attn_in,
    g_attn_out,
    g_ffn_in,
    g_ffn_out,
    g_query,
    g_key,
):
    seqs, piece_len, width = tokens.shape
    n_s = lax.axis_size("shard")
    n_r = lax.axis_size("r")
    n_z = lax.axis_size("z")
    s, z, c = lax.axis_index("shard"), lax.axis_index("z"), lax.axis_index("c")
    own = seqs * piece_len
    both = 2 * own
    heads = HEADS // 2
    hw = heads * HD
    d_own = width // n_s
    ff = w_gate.shape[1]
    ff_own = ff // (2 * n_s)

    def px(v, k):
        return lax.ppermute(v, "shard", [(i, i ^ k) for i in range(n_s)])

    def pz(v, k):
        return lax.ppermute(v, "z", [(i, i ^ k) for i in range(n_z)])

    def pc(v):
        return lax.ppermute(v, "c", [(0, 1), (1, 0)])

    def natural(pieces, index):
        stacked = jnp.stack(pieces)
        n = len(pieces)
        return jnp.stack(
            [lax.dynamic_index_in_dim(stacked, index ^ j, 0, keepdims=False) for j in range(n)]
        )

    def pick(v, index, axis=0):
        return lax.dynamic_index_in_dim(v, index, axis, keepdims=False)

    def by_core(mine, other, axis):
        first = jnp.where(c == 0, mine, other)
        second = jnp.where(c == 0, other, mine)
        return jnp.stack([first, second], axis=axis)

    def gather4(v):
        h = v.shape[0] // 2
        f1, f2 = px(v, 1), px(v, 2)
        f3 = jnp.concatenate([px(f1[:h], 2), px(f2[h:], 1)])
        return [v, f1, f2, f3]

    def scatter4(p):
        h = p[0].shape[0] // 2
        a = px(p[3][:h], 2)
        b = px(p[3][h:], 1)
        q1 = jnp.concatenate([p[1][:h] + a, p[1][h:]])
        q2 = jnp.concatenate([p[2][:h], p[2][h:] + b])
        return p[0] + px(q1, 1).astype(F32) + px(q2, 2).astype(F32)

    def sum_z(v):
        if n_z == 4:
            t = lax.ppermute(v, "z", [(0, 1), (3, 2)])
            part = v + t
            u = lax.ppermute(part, "z", [(1, 2), (2, 1)])
            total = part + u
            back = lax.ppermute(total, "z", [(1, 0), (2, 3)])
            v = jnp.where((z == 0) | (z == 3), back, total)
        else:
            v = lax.psum(v, "z")
        return lax.psum(v, "r") if n_r > 1 else v

    def spread(v):
        return jnp.stack([pick(v, z)] + [pz(pick(v, z ^ k), k) for k in range(1, n_z)])

    def in_order(v):
        return jnp.stack([pick(v, z ^ j) for j in range(n_z)])

    wq_half = lax.dynamic_slice_in_dim(w_query, c * hw, hw, 1)
    qkv_mine = jnp.concatenate([wq_half, w_key, w_value], axis=1)
    w_qkv = lax.all_gather(qkv_mine, "shard", axis=0, tiled=True)
    w_out_all = lax.all_gather(w_out, "shard", axis=0, tiled=True)
    x_near = spread(tokens)
    x_near_other = pc(x_near)
    gains = jnp.concatenate([g_attn_in, g_attn_out, g_ffn_in, g_ffn_out, g_query, g_key])
    gains = natural([gains] + [px(gains, k) for k in range(1, n_s)], s)

    def gain(first, size):
        return gains[:, first : first + size].reshape(1, n_s * size)

    hd_own = HD // n_s
    ga_in, ga_out, gf_in, gf_out = (gain(i * d_own, d_own) for i in range(4))
    gq, gk = gain(4 * d_own, hd_own), gain(4 * d_own + hd_own, hd_own)

    def col_piece(w, k):
        first = (s ^ k) * (2 * ff_own) + c * ff_own
        return lax.dynamic_slice_in_dim(w, first, ff_own, 1)

    gu = [jnp.stack([col_piece(w_gate, k), col_piece(w_up, k)]) for k in range(n_s)]
    gu = natural([gu[0]] + [px(gu[k], k) for k in range(1, n_s)], s)
    gu = jnp.stack([gu, pc(gu)])
    wq_other = pc(w_qkv[:, :hw])

    base = lax.axis_index("r") * both
    q_pos = base + jnp.arange(both, dtype=jnp.int32)
    half = HD // 2
    inverse = jnp.exp(
        -(jnp.arange(half).astype(F32) * 2.0 / HD) * jnp.log(jnp.float32(ROPE_BASE))
    )
    angle = q_pos.astype(F32)[:, None] * inverse[None, :]
    cos, sin = jnp.cos(angle), jnp.sin(angle)
    starts = pick(pictures, z)
    at = jnp.concatenate([jnp.stack([z, c, base]).astype(jnp.int32), starts.astype(jnp.int32)])

    def rows_of(v, core):
        n = v.shape[1]
        return pick(v.reshape(seqs, 2, piece_len, n), core, 1).reshape(own, n)

    def whole(mine):
        n = mine.shape[1]
        mine = mine.reshape(seqs, piece_len, n)
        return by_core(mine, pc(mine), 1).reshape(both, n)

    nin, raw, queries, keys, values = project(at, x_near, x_near_other, w_qkv, ga_in, gq, gk, cos, sin)
    if n_r > 1:
        keys = lax.all_gather(keys, "r", axis=0, tiled=True)
        values = lax.all_gather(values, "r", axis=0, tiled=True)
    mixed = attend(at, queries, keys, values)
    w_out_mine = lax.dynamic_slice_in_dim(w_out_all, c * hw, hw, 0)
    w_out_other = lax.dynamic_slice_in_dim(w_out_all, (1 - c) * hw, hw, 0)
    mixed_there = pc(rows_of(mixed, 1 - c))
    x = in_order(x_near).reshape(own, width).astype(F32)
    attn_out = dot(rows_of(mixed, c), w_out_mine) + dot(mixed_there, w_out_other)
    r_x = inv_rms(x)
    r_ao = inv_rms(attn_out)
    residual = x + attn_out * r_ao * ga_out
    r_res = inv_rms(residual)
    nffn = (residual * r_res * gf_in).astype(BF)

    rows = gather4(nffn)
    acts = [ffn(at, v, gu, w_down, F32 if k == 0 else BF) for k, v in enumerate(rows)]
    branch = scatter4([a[3] for a in acts])
    r_b = inv_rms(branch)
    output = (residual + branch * r_b * gf_out).astype(BF)
    output = in_order(spread(output.reshape(tokens.shape)))

    zf = in_order(spread(cotangent)).reshape(own, width).astype(F32)
    gg_ffn_out = jnp.sum(zf * branch * r_b, axis=0)
    lows = gather4(rms_back(branch, r_b, gf_out, zf).astype(BF))
    backs = [
        ffn_back(at, v, gu, w_down, acts[k][0], acts[k][1], F32 if k == 0 else BF)
        for k, v in enumerate(lows)
    ]
    nffn_grad = scatter4([b[2] for b in backs])
    hids = [a[2] for a in acts]
    gates, ups = [b[0] for b in backs], [b[1] for b in backs]
    gw_down = down_grad(0, hids, lows, pc(down_grad(1, hids, lows, None)))
    gw_gu = gate_up_grad(0, rows, gates, ups, pc(gate_up_grad(1, rows, gates, ups, None)))

    gw_down = lax.psum_scatter(gw_down, "z", scatter_dimension=0, tiled=True)
    dz = d_own // n_z
    gw_gu = gw_gu.reshape(2, n_s, n_z, dz, ff_own).transpose(2, 1, 0, 3, 4)
    gw_gu = lax.psum_scatter(gw_gu.reshape(-1, ff_own), "z", scatter_dimension=0, tiled=True)
    gw_gu = gw_gu.reshape(n_s, 2, dz, ff_own)
    if n_r > 1:
        gw_down, gw_gu = lax.psum(gw_down, "r"), lax.psum(gw_gu, "r")
    gw_gu = natural([pick(gw_gu, s)] + [px(pick(gw_gu, s ^ k), k) for k in range(1, n_s)], s)
    gw_down = lax.all_gather(gw_down, "z", axis=0, tiled=True)
    gw_gu = lax.all_gather(gw_gu.reshape(-1, ff_own), "z", axis=0, tiled=True)
    gw_gu = gw_gu.reshape(n_z, n_s, 2, dz, ff_own)

    res_grad = zf + rms_back(residual, r_res, gf_in, nffn_grad)
    gg_ffn_in = jnp.sum(nffn_grad * residual * r_res, axis=0)
    gg_attn_out = jnp.sum(res_grad * attn_out * r_ao, axis=0)
    attn_grad = whole(rms_back(attn_out, r_ao, ga_out, res_grad).astype(BF))
    mixed_grad = dot_t(attn_grad, w_out_mine).astype(BF)
    q_low, k_grad, v_grad, gg_query = attend_back(
        at, queries, keys, values, mixed_grad, raw, gq, cos, sin
    )
    k_grad = k_grad + pc(k_grad.astype(BF)).astype(F32)
    v_grad = v_grad + pc(v_grad.astype(BF)).astype(F32)
    if n_r > 1:
        k_grad = lax.psum_scatter(k_grad.astype(BF), "r", scatter_dimension=0, tiled=True).astype(F32)
        v_grad = lax.psum_scatter(v_grad.astype(BF), "r", scatter_dimension=0, tiled=True).astype(F32)
    k_raw = raw[:, hw:]
    rk = inv_rms(k_raw)
    k_un = rope(k_grad, cos, -sin)
    gg_key = jnp.sum(rows_of(k_un * k_raw * rk, c), axis=0)
    k_low = rms_back(k_raw, rk, gk, k_un).astype(BF)
    v_low = v_grad.astype(BF)
    low_own = jnp.concatenate([rows_of(q_low, c), rows_of(k_low, c), rows_of(v_low, c)], axis=1)
    nin_grad = dot_t(low_own, w_qkv) + dot_t(pc(rows_of(q_low, 1 - c)), wq_other)
    gg_attn_in = jnp.sum(nin_grad * x * r_x, axis=0)
    input_grad = (res_grad + rms_back(x, r_x, ga_in, nin_grad)).astype(BF)
    input_grad = in_order(spread(input_grad.reshape(tokens.shape)))

    low_mine = jnp.concatenate([q_low, jnp.where(c == 0, k_low, v_low)], axis=1)
    gw_qkv = dot_rows(nin, low_mine).astype(BF)
    gw_out = dot_rows(mixed, attn_grad).astype(BF).reshape(heads, 2, HD // 2, width)
    there = pc(pick(gw_out, 1 - c, 1))
    gw_out = by_core(pick(gw_out, c, 1), there, 0)

    def to_shards(v):
        v = v.reshape(n_s, v.size // (n_s * v.shape[-1]), v.shape[-1])
        parts = [pick(v, s ^ k) for k in range(n_s)]
        return scatter4([parts[0].astype(F32)] + parts[1:]).astype(BF)

    gw_qkv = sum_z(to_shards(gw_qkv))
    gw_out = sum_z(to_shards(gw_out))

    parts = [gg_attn_in, gg_attn_out, gg_ffn_in, gg_ffn_out, gg_query, gg_key]
    small = jnp.concatenate([p.reshape(n_s, -1) for p in parts], axis=1)
    small = small + pc(small)
    if n_z == 4:
        for k in (1, 2):
            small = small + pz(small, k)
    else:
        small = lax.psum(small, "z")
    if n_r > 1:
        small = lax.psum(small, "r")
    for k in (1, 2):
        small = small + px(small, k)
    small = pick(small, s)
    small_out = []
    first = 0
    for size in [d_own] * 4 + [hd_own] * 2:
        small_out.append(small[first : first + size])
        first += size

    qkv_pair = by_core(gw_qkv, pc(gw_qkv), 0).astype(F32)
    gw_query = jnp.concatenate([qkv_pair[0][:, :hw], qkv_pair[1][:, :hw]], axis=1)
    gw_key, gw_value = qkv_pair[0][:, hw:], qkv_pair[1][:, hw:]
    gw_out = by_core(gw_out, pc(gw_out), 0).reshape(w_out.shape).astype(F32)
    gw_down = by_core(gw_down, pc(gw_down), 0).reshape(w_down.shape).astype(F32)
    gw_gate, gw_up = lay(at, gw_gu, pc(gw_gu))
    return (
        output,
        input_grad,
        gw_query,
        gw_key,
        gw_value,
        gw_out,
        gw_gate,
        gw_up,
        gw_down,
        *small_out,
    )


def solution(mesh):
    n_s, n_c = mesh.shape["shard"], mesh.shape["ctx"]

    def run(*args):
        seqs = args[0].shape[0] // n_s
        groups = n_c // (2 * seqs)
        fine = Mesh(mesh.devices.reshape(n_s, groups, seqs, 2), ("shard", "r", "z", "c"))
        ctx = ("r", "z", "c")
        rows, mat, vec = P("shard", ctx, None), P("shard", None), P("shard")
        return jax.shard_map(
            body,
            mesh=fine,
            in_specs=(rows, rows, mat) + (mat,) * 7 + (vec,) * 6,
            out_specs=(rows, rows) + (mat,) * 7 + (vec,) * 6,
            check_vma=False,
        )(*args)

    return run
```

time: 1010 us -> 779 us (0.77)
  Pallas kernels: 0 us -> 227 us
  matrix products: 187 us -> 19.2 us
  waiting for transfers between devices: 402 us -> 292 us
  local copies, waits for them, and re-layouts: 144 us -> 65.4 us
  other arithmetic: 153 us -> 80.1 us
  starting transfers between devices: 112 us -> 73.9 us
  between operations: 4.09 us -> 16 us
    pallas_call x0 -> x16, Pallas kernels: none -> 227 us  [the longest x4 62.9 us: ffn_back(): call(ffn_back_kernel, (2,), [full(z.shape), pl.BlockSpec((1,) + w.shape[1...]
    ppermute x8 -> x2, waiting for transfers between devices: 144 us -> 39.8 us  [sum_z(): back = lax.ppermute(total, 'z', [(1, 0), (2, 3)])]
    dot_general x15 -> x3, matrix products: 76.7 us -> 10.3 us  [dot_t(): lax.dot_general(a, b, (((1,), (1,)), ((), ())), preferred_element_type=F32)]
    ppermute x8 -> x2, waiting for transfers between devices: 89.9 us -> 27.2 us  [sum_z(): t = lax.ppermute(v, 'z', [(0, 1), (3, 2)])]
    dot_general x15 -> x2, matrix products: 54.1 us -> 3.49 us  [dot(): lax.dot_general(a, b, (((1,), (0,)), ((), ())), preferred_element_type=F32)]
    dot_general x5 -> x2, matrix products: 44.6 us -> 5.36 us  [dot_rows(): lax.dot_general(a, b, (((0,), (0,)), ((), ())), preferred_element_type=F32)]
    unnamed x372 -> x176, local copies, waits for them, and re-layouts: 50.1 us -> 13.4 us
    ppermute x14, waiting for transfers between devices: 53 us -> 88.3 us  [pz(): return lax.ppermute(v, 'z', [(i, i ^ k) for i in range(n_z)])]
  transfers between devices with their start and end apart: 111 -> 77, of which waited for: 36 -> 26; matrix products, arithmetic and copies ran while one was open for 44% -> 19% of each run, Pallas kernels for 0% -> 27%
where the time goes in v2:
time: 779 us; the launch traced here: 774 us
  waiting for transfers between devices  292 us (37%)
  Pallas kernels  227 us (29%)
  other arithmetic  80.1 us (10%)
  starting transfers between devices  73.9 us (9%)
  local copies, waits for them, and re-layouts  65.4 us (8%)
  matrix products  19.2 us (2%)
  between operations  16 us (2%)
    ppermute x35, waiting for transfers between devices, px(): return lax.ppermute(v, 'shard', [(i, i ^ k) for i in range(n_s)])  136 us
    ppermute x14, waiting for transfers between devices, pz(): return lax.ppermute(v, 'z', [(i, i ^ k) for i in range(n_z)])  88.3 us
    pallas_call x4, Pallas kernels, ffn_back(): call(ffn_back_kernel, (2,), [full(z.shape), pl.BlockSpec((1,) + w.shape[1...  62.9 us
    pallas_call x4, Pallas kernels, ffn(): call(ffn_kernel, (2,), [full(x.shape), pl.BlockSpec((1,) + w.shape[1:], l...  59 us
    ppermute x35, starting transfers between devices, px(): return lax.ppermute(v, 'shard', [(i, i ^ k) for i in range(n_s)])  40.9 us
    ppermute x2, waiting for transfers between devices, sum_z(): back = lax.ppermute(total, 'z', [(1, 0), (2, 3)])  39.8 us
    pallas_call x2, Pallas kernels, gate_up_grad(): call(functools.partial(gate_up_grad_kernel, n, more is not None), (width...  30.8 us
    ppermute x2, waiting for transfers between devices, sum_z(): t = lax.ppermute(v, 'z', [(0, 1), (3, 2)])  27.2 us
  transfers between devices with their start and end apart: 77, of which 26 were waited for; matrix products, arithmetic and copies ran while one was open for 19% of the time, Pallas kernels for 27%

profile of v2, /device:TPU:0, one launch (start us, length us, event | category | flops | bytes accessed | tf_op | source)
XLA Modules:
  0.0 773.8 jit_solution(5296884512987981221)
XLA Ops:
  10.4 3.9 collective-permute-start.6
  15.9 4.0 collective-permute-start.2
  26.9 3.6 multiply_sine_fusion
  37.0 7.5 collective-permute-done.1
  50.3 21.9 %collective-permute-done.10 = bf16[2,288,864]{2,1,0:T(8,128)(2,1)} collective-permute-done((bf16[2,288,864]{2,1,0:T(8,128)(2,1)}, bf16[2,288,864]{2,1,0:T(8,128)(2,1)}, u32[]{:S(2)}, u32[]{:S(2)}) %collective-permute-start.10) | collective-permute-done | bytes 995360 | tf_op jit(solution)/shard_map/ppermute | solution.py:407
  72.2 19.2 %collective-permute-done.9 = bf16[2,288,864]{2,1,0:T(8,128)(2,1)} collective-permute-done((bf16[2,288,864]{2,1,0:T(8,128)(2,1)}, bf16[2,288,864]{2,1,0:T(8,128)(2,1)}, u32[]{:S(2)}, u32[]{:S(2)}) %collective-permute-start.9) | collective-permute-done | bytes 995360 | tf_op jit(solution)/shard_map/ppermute | solution.py:407
  94.4 3.8 fusion.49
  98.2 9.4 %shard_map.271 = (bf16[1024,1152]{1,0:T(8,128)(2,1)}, f32[1024,768]{1,0:T(8,128)}, bf16[1024,512]{1,0:T(8,128)(2,1)}, bf16[1024,256]{1,0:T(8,128)(2,1)}, bf16[1024,256]{1,0:T(8,128)(2,1)}) custom-call(s32[5]{0:T(128)} %pad_add_fusion.at, bf16[4,128,1152]{2,1,0:T(8,128)(2,1)} %copy-done.8, bf16[4,128,1152]{2,1,0:T(8,128)(2,1)} %collective-permute-done.3.oth, ...), custom_call_target="tpu_custom_call" | custom-call | flops 2415919104 | bytes 11796480 | tf_op jit(solution)/shard_map/pallas_call | solution.py:107
  107.5 15.6 %shard_map.272 = bf16[1024,512]{1,0:T(8,128)(2,1)} custom-call(s32[5]{0:T(128)} %pad_add_fusion.at, bf16[1024,512]{1,0:T(8,128)(2,1)} %get-tuple-element.54.q, bf16[1024,256]{1,0:T(8,128)(2,1)} %get-tuple-element.55.k, bf16[1024,256]{1,0:T(8,128)(2,1)} %get-tuple-element.56.v), custom_call_target="tpu_custom_call" | custom-call | flops 2147483648 | bytes 3145728 | tf_op jit(solution)/shard_map/pallas_call | solution.py:144
  133.5 25.1 %collective-permute-done.12.x.refs_1_ = bf16[512,1152]{1,0:T(8,128)(2,1)S(1)} collective-permute-done((bf16[512,1152]{1,0:T(8,128)(2,1)S(1)}, bf16[512,1152]{1,0:T(8,128)(2,1)S(1)}, u32[]{:S(2)}, u32[]{:S(2)}) %collective-permute-start.12) | collective-permute-done | bytes 1179680 | tf_op jit(solution)/shard_map/ppermute | solution.py:407
  163.0 3.8 collective-permute-start.25
  171.4 7.8 %pad_maximum_fusion.w = bf16[2,4,2,288,864]{4,3,2,1,0:T(8,128)(2,1)} fusion(bf16[1,4,2,288,864]{4,3,2,1,0:T(8,128)(2,1)} %bitcast.25, bf16[1,4,2,288,864]{4,3,2,1,0:T(8,128)(2,1)} %get-tuple-element.115), kind=kLoop, calls=%fused_computation | loop fusion | flops 3981312 | bytes 15925248 | tf_op jit(solution)/shard_map/stack | solution.py:484
  184.7 14.7 %shard_map.275 = (bf16[2,512,864]{2,1,0:T(8,128)(2,1)}, bf16[2,512,864]{2,1,0:T(8,128)(2,1)}, bf16[2,512,864]{2,1,0:T(8,128)(2,1)}, bf16[512,1152]{1,0:T(8,128)(2,1)}) custom-call(s32[5]{0:T(128)} %pad_add_fusion.at, bf16[512,1152]{1,0:T(8,128)(2,1)} %copy-done.54, bf16[2,4,2,288,864]{4,3,2,1,0:T(8,128)(2,1)} %pad_maximum_fusion.w, bf16[1728,1152]{1,0:T(8,128)(2,1)} %wd.15), custom_call_target="tpu_custom_call" | custom-call | flops 6115295232 | bytes 22560768 | tf_op jit(solution)/shard_map/pallas_call | solution.py:228
  202.3 14.5 %shard_map.276 = (bf16[2,512,864]{2,1,0:T(8,128)(2,1)}, bf16[2,512,864]{2,1,0:T(8,128)(2,1)}, bf16[2,512,864]{2,1,0:T(8,128)(2,1)}, bf16[512,1152]{1,0:T(8,128)(2,1)}) custom-call(s32[5]{0:T(128)} %pad_add_fusion.at, bf16[512,1152]{1,0:T(8,128)(2,1)} %collective-permute-done.14.x.refs_2_, bf16[2,4,2,288,864]{4,3,2,1,0:T(8,128)(2,1)} %pad_maximum_fusion.w, ...), custom_call_target="tpu_custom_call" | custom-call | flops 6115295232 | bytes 22560768 | tf_op jit(solution)/shard_map/pallas_call | solution.py:228
  216.8 14.8 %shard_map.274 = (bf16[2,512,864]{2,1,0:T(8,128)(2,1)}, bf16[2,512,864]{2,1,0:T(8,128)(2,1)}, bf16[2,512,864]{2,1,0:T(8,128)(2,1)}, bf16[512,1152]{1,0:T(8,128)(2,1)}) custom-call(s32[5]{0:T(128)} %pad_add_fusion.at, bf16[512,1152]{1,0:T(8,128)(2,1)} %copy-done.53, bf16[2,4,2,288,864]{4,3,2,1,0:T(8,128)(2,1)} %pad_maximum_fusion.w, bf16[1728,1152]{1,0:T(8,128)(2,1)} %wd.15), custom_call_target="tpu_custom_call" | custom-call | flops 6115295232 | bytes 22560768 | tf_op jit(solution)/shard_map/pallas_call | solution.py:228
  234.1 13.9 %collective-permute-done.16 = bf16[256,1152]{1,0:T(8,128)(2,1)S(1)} collective-permute-done((bf16[256,1152]{1,0:T(8,128)(2,1)S(1)}, bf16[256,1152]{1,0:T(8,128)(2,1)S(1)}, u32[]{:S(2)}, u32[]{:S(2)}) %collective-permute-start.16) | collective-permute-done | bytes 589856 | tf_op jit(solution)/shard_map/ppermute | solution.py:407
  250.7 14.9 %shard_map.273 = (bf16[2,512,864]{2,1,0:T(8,128)(2,1)}, bf16[2,512,864]{2,1,0:T(8,128)(2,1)}, bf16[2,512,864]{2,1,0:T(8,128)(2,1)}, f32[512,1152]{1,0:T(8,128)}) custom-call(s32[5]{0:T(128)} %pad_add_fusion.at, bf16[512,1152]{1,0:T(8,128)(2,1)} %copy-done.32, bf16[2,4,2,288,864]{4,3,2,1,0:T(8,128)(2,1)} %pad_maximum_fusion.w, bf16[1728,1152]{1,0:T(8,128)(2,1)} %wd.15), custom_call_target="tpu_custom_call" | custom-call | flops 6115295232 | bytes 22560768 | tf_op jit(solution)/shard_map/pallas_call | solution.py:228
  265.7 3.9 collective-permute-done.19
  276.1 23.1 %collective-permute-done.26.z.refs_5_ = bf16[512,1152]{1,0:T(8,128)(2,1)S(1)} collective-permute-done((bf16[512,1152]{1,0:T(8,128)(2,1)S(1)}, bf16[512,1152]{1,0:T(8,128)(2,1)S(1)}, u32[]{:S(2)}, u32[]{:S(2)}) %collective-permute-start.26) | collective-permute-done | bytes 1179680 | tf_op jit(solution)/shard_map/ppermute | solution.py:407
  300.0 16.0 %shard_map.277 = (bf16[2,512,864]{2,1,0:T(8,128)(2,1)}, bf16[2,512,864]{2,1,0:T(8,128)(2,1)}, f32[512,1152]{1,0:T(8,128)}) custom-call(s32[5]{0:T(128)} %pad_add_fusion.at, bf16[512,1152]{1,0:T(8,128)(2,1)} %copy-done.7, bf16[2,4,2,288,864]{4,3,2,1,0:T(8,128)(2,1)} %pad_maximum_fusion.w, bf16[1728,1152]{1,0:T(8,128)(2,1)} %wd.15, ...), custom_call_target="tpu_custom_call" | custom-call | flops 6115295232 | bytes 22560768 | tf_op jit(solution)/shard_map/pallas_call | solution.py:270
  317.1 15.8 %shard_map.280 = (bf16[2,512,864]{2,1,0:T(8,128)(2,1)}, bf16[2,512,864]{2,1,0:T(8,128)(2,1)}, bf16[512,1152]{1,0:T(8,128)(2,1)}) custom-call(s32[5]{0:T(128)} %pad_add_fusion.at, bf16[512,1152]{1,0:T(8,128)(2,1)} %copy-done.25, bf16[2,4,2,288,864]{4,3,2,1,0:T(8,128)(2,1)} %pad_maximum_fusion.w, bf16[1728,1152]{1,0:T(8,128)(2,1)} %wd.15, ...), custom_call_target="tpu_custom_call" | custom-call | flops 6115295232 | bytes 22560768 | tf_op jit(solution)/shard_map/pallas_call | solution.py:270
  334.1 9.7 %shard_map.285 = bf16[864,1152]{1,0:T(8,128)(2,1)} custom-call(bf16[2,512,864]{2,1,0:T(8,128)(2,1)} %get-tuple-element.88.refs_0_, bf16[2,512,864]{2,1,0:T(8,128)(2,1)} %get-tuple-element.89.refs_1_, bf16[2,512,864]{2,1,0:T(8,128)(2,1)} %get-tuple-element.90.refs_2_, bf16[2,512,864]{2,1,0:T(8,128)(2,1)} %get-tuple-element.91.refs_3_, ...), custom_call_target="tpu_custom_call" | custom-call | flops 4076863488 | bytes 10248192 | tf_op jit(solution)/shard_map/pallas_call | solution.py:336
  343.8 15.4 %shard_map.278 = (bf16[2,512,864]{2,1,0:T(8,128)(2,1)}, bf16[2,512,864]{2,1,0:T(8,128)(2,1)}, bf16[512,1152]{1,0:T(8,128)(2,1)}) custom-call(s32[5]{0:T(128)} %pad_add_fusion.at, bf16[512,1152]{1,0:T(8,128)(2,1)} %copy-done.24, bf16[2,4,2,288,864]{4,3,2,1,0:T(8,128)(2,1)} %pad_maximum_fusion.w, bf16[1728,1152]{1,0:T(8,128)(2,1)} %wd.15, ...), custom_call_target="tpu_custom_call" | custom-call | flops 6115295232 | bytes 22560768 | tf_op jit(solution)/shard_map/pallas_call | solution.py:270
  359.2 15.6 %shard_map.279 = (bf16[2,512,864]{2,1,0:T(8,128)(2,1)}, bf16[2,512,864]{2,1,0:T(8,128)(2,1)}, bf16[512,1152]{1,0:T(8,128)(2,1)}) custom-call(s32[5]{0:T(128)} %pad_add_fusion.at, bf16[512,1152]{1,0:T(8,128)(2,1)} %copy-done.26, bf16[2,4,2,288,864]{4,3,2,1,0:T(8,128)(2,1)} %pad_maximum_fusion.w, bf16[1728,1152]{1,0:T(8,128)(2,1)} %wd.15, ...), custom_call_target="tpu_custom_call" | custom-call | flops 6115295232 | bytes 22560768 | tf_op jit(solution)/shard_map/pallas_call | solution.py:270
  374.8 15.2 %shard_map.282 = bf16[2,1152,864]{2,1,0:T(8,128)(2,1)} custom-call(bf16[512,1152]{1,0:T(8,128)(2,1)} %copy-done.32, bf16[512,1152]{1,0:T(8,128)(2,1)} %copy-done.53, bf16[512,1152]{1,0:T(8,128)(2,1)} %collective-permute-done.14.x.refs_2_, bf16[512,1152]{1,0:T(8,128)(2,1)} %copy-done.54, bf16[2,512,864]{2,1,0:T(8,128)(2,1)} %get-tuple-element.78.refs_4_, ...), custom_call_target="tpu_custom_call" | custom-call | flops 8153726976 | bytes 15777792 | tf_op jit(solution)/shard_map/pallas_call | solution.py:307
  390.1 6.3 copy.34
  396.9 10.1 %shard_map.286 = bf16[864,1152]{1,0:T(8,128)(2,1)} custom-call(bf16[2,512,864]{2,1,0:T(8,128)(2,1)} %get-tuple-element.88.refs_0_, bf16[2,512,864]{2,1,0:T(8,128)(2,1)} %get-tuple-element.89.refs_1_, bf16[2,512,864]{2,1,0:T(8,128)(2,1)} %get-tuple-element.90.refs_2_, bf16[2,512,864]{2,1,0:T(8,128)(2,1)} %get-tuple-element.91.refs_3_, ...), custom_call_target="tpu_custom_call" | custom-call | flops 4076863488 | bytes 10248192 | tf_op jit(solution)/shard_map/pallas_call | solution.py:336
  411.0 12.8 %collective-permute-done.32 = bf16[256,1152]{1,0:T(8,128)(2,1)S(1)} collective-permute-done((bf16[256,1152]{1,0:T(8,128)(2,1)S(1)}, bf16[256,1152]{1,0:T(8,128)(2,1)S(1)}, u32[]{:S(2)}, u32[]{:S(2)}) %collective-permute-start.32) | collective-permute-done | bytes 589856 | tf_op jit(solution)/shard_map/ppermute | solution.py:407
  431.4 6.4 copy.35.refs_12_
  437.8 15.6 %shard_map.283 = bf16[2,1152,864]{2,1,0:T(8,128)(2,1)} custom-call(bf16[512,1152]{1,0:T(8,128)(2,1)} %copy-done.32, bf16[512,1152]{1,0:T(8,128)(2,1)} %copy-done.53, bf16[512,1152]{1,0:T(8,128)(2,1)} %collective-permute-done.14.x.refs_2_, bf16[512,1152]{1,0:T(8,128)(2,1)} %copy-done.54, bf16[2,512,864]{2,1,0:T(8,128)(2,1)} %get-tuple-element.78.refs_4_, ...), custom_call_target="tpu_custom_call" | custom-call | flops 8153726976 | bytes 15777792 | tf_op jit(solution)/shard_map/pallas_call | solution.py:307
  453.4 4.5 copy.36
  468.1 4.0 multiply_reduce_fusion.1
  477.7 42.8 %collective-permute-done.21 = bf16[128,1152]{1,0:T(8,128)(2,1)} collective-permute-done((bf16[128,1152]{1,0:T(8,128)(2,1)}, bf16[128,1152]{1,0:T(8,128)(2,1)}, u32[]{:S(2)}, u32[]{:S(2)}) %collective-permute-start.21) | collective-permute-done | bytes 294944 | tf_op jit(solution)/shard_map/ppermute | solution.py:410
  529.0 19.4 %shard_map.281 = (bf16[1024,512]{1,0:T(8,128)(2,1)}, f32[1024,256]{1,0:T(8,128)}, f32[1024,256]{1,0:T(8,128)}, f32[1,256]{1,0:T(1,128)}) custom-call(s32[5]{0:T(128)} %pad_add_fusion.at, bf16[1024,512]{1,0:T(8,128)(2,1)} %get-tuple-element.54.q, bf16[1024,256]{1,0:T(8,128)(2,1)} %get-tuple-element.55.k, bf16[1024,256]{1,0:T(8,128)(2,1)} %get-tuple-element.56.v, ...), custom_call_target="tpu_custom_call" | custom-call | flops 5368709120 | bytes 9437184 | tf_op jit(solution)/shard_map/pallas_call | solution.py:185
  567.5 4.8 fusion.13
  574.3 3.8 convolution_convert_fusion
  578.3 5.0 collective-permute-done.67
  597.6 5.8 collective-permute-done.62
  621.9 4.3 collective-permute-done.54
  631.5 10.9 %collective-permute-done.55 = bf16[128,1152]{1,0:T(8,128)(2,1)S(1)} collective-permute-done((bf16[128,1152]{1,0:T(8,128)(2,1)S(1)}, bf16[128,1152]{1,0:T(8,128)(2,1)S(1)}, u32[]{:S(2)}, u32[]{:S(2)}) %collective-permute-start.55) | collective-permute-done | bytes 294944 | tf_op jit(solution)/shard_map/ppermute | solution.py:446
  645.9 4.8 collective-permute-start.46
  653.3 4.7 collective-permute-done.41
  658.0 23.1 %collective-permute-done.40 = bf16[128,1152]{1,0:T(8,128)(2,1)S(1)} collective-permute-done((bf16[128,1152]{1,0:T(8,128)(2,1)S(1)}, bf16[128,1152]{1,0:T(8,128)(2,1)S(1)}, u32[]{:S(2)}, u32[]{:S(2)}) %collective-permute-start.40) | collective-permute-done | bytes 294944 | tf_op jit(solution)/shard_map/ppermute | solution.py:410
  681.3 16.3 %collective-permute-done.46 = bf16[288,768]{1,0:T(8,128)(2,1)S(1)} collective-permute-done((bf16[288,768]{1,0:T(8,128)(2,1)S(1)}, bf16[288,768]{1,0:T(8,128)(2,1)S(1)}, u32[]{:S(2)}, u32[]{:S(2)}) %collective-permute-start.46) | collective-permute-done | bytes 442400 | tf_op jit(solution)/shard_map/ppermute | solution.py:446
  698.5 11.9 %collective-permute-done.57 = bf16[128,1152]{1,0:T(8,128)(2,1)S(1)} collective-permute-done((bf16[128,1152]{1,0:T(8,128)(2,1)S(1)}, bf16[128,1152]{1,0:T(8,128)(2,1)S(1)}, u32[]{:S(2)}, u32[]{:S(2)}) %collective-permute-start.57) | collective-permute-done | bytes 294944 | tf_op jit(solution)/shard_map/ppermute | solution.py:450
  714.1 27.9 %collective-permute-done.48 = bf16[288,768]{1,0:T(8,128)(2,1)} collective-permute-done((bf16[288,768]{1,0:T(8,128)(2,1)S(1)}, bf16[288,768]{1,0:T(8,128)(2,1)}, u32[]{:S(2)}, u32[]{:S(2)}) %collective-permute-start.48) | collective-permute-done | bytes 442400 | tf_op jit(solution)/shard_map/ppermute | solution.py:450
  750.0 4.1 bitcast_convert_fusion
  756.1 10.6 %shard_map.284 = (f32[288,6912]{1,0:T(8,128)}, f32[288,6912]{1,0:T(8,128)}) custom-call(s32[5]{0:T(128)} %pad_add_fusion.at, bf16[4,4,2,72,864]{4,3,2,1,0:T(8,128)(2,1)} %bitcast.232, bf16[4,4,2,72,864]{4,3,2,1,0:T(8,128)(2,1)} %copy-done.22), custom_call_target="tpu_custom_call" | custom-call | bytes 23887872 | tf_op jit(solution)/shard_map/pallas_call | solution.py:363
  (466 shorter events, 184.9 us)
Async XLA Ops:
  7.3 90.9 %all-gather.5.cloned.1.call-start = ((), (), s32[]{:S(2)}) async-start(), calls=%async_computation.2 | async-start | bytes 2949120 | tf_op jit(solution)/shard_map/all_gather | solution.py:464
  10.2 115.1 %all-gather.7.cloned.1.call-start = ((), (), s32[]{:S(2)}) async-start(), calls=%async_computation.3 | async-start | bytes 2949120 | tf_op jit(solution)/shard_map/all_gather | solution.py:465
  10.4 20.7 %collective-permute-start.6 = (f32[1280]{0:T(1024)S(1)}, f32[1280]{0:T(1024)}, u32[]{:S(2)}, u32[]{:S(2)}) collective-permute-start(f32[1280]{0:T(1024)S(1)} %concatenate.56), channel_id=1, source_target_pairs={{0,24},{8,16},{16,8},{24,0},{1,25},{9,17},{17,9},{25,1},{2,26},{10... | collective-permute-start | bytes 15368 | tf_op jit(solution)/shard_map/ppermute | solution.py:407
  14.3 18.3 %collective-permute-start.5 = (f32[1280]{0:T(1024)S(1)}, f32[1280]{0:T(1024)}, u32[]{:S(2)}, u32[]{:S(2)}) collective-permute-start(f32[1280]{0:T(1024)S(1)} %concatenate.56), channel_id=1, source_target_pairs={{0,16},{8,24},{16,0},{24,8},{1,17},{9,25},{17,1},{25,9},{2,18},{10... | collective-permute-start | bytes 15368 | tf_op jit(solution)/shard_map/ppermute | solution.py:407
  14.8 21.2 %collective-permute-start.4 = (f32[1280]{0:T(1024)S(1)}, f32[1280]{0:T(1024)S(1)}, u32[]{:S(2)}, u32[]{:S(2)}) collective-permute-start(f32[1280]{0:T(1024)S(1)} %concatenate.56), channel_id=1, source_target_pairs={{0,8},{8,0},{16,24},{24,16},{1,9},{9,1},{17,25},{25,17},{2,10},{10... | collective-permute-start | bytes 15368 | tf_op jit(solution)/shard_map/ppermute | solution.py:407
  15.9 20.7 %collective-permute-start.2 = (bf16[128,1152]{1,0:T(8,128)(2,1)}, bf16[128,1152]{1,0:T(8,128)(2,1)S(1)}, u32[]{:S(2)}, u32[]{:S(2)}) collective-permute-start(bf16[128,1152]{1,0:T(8,128)(2,1)} %get-tuple-element.193), channel_id=1, source_target_pairs={{0,6},{2,4},{4,2},{6,0},{1,7},{3,5},{5,3},{7,1},{8,14},{10,12},{12... | collective-permute-start | bytes 884744 | tf_op jit(solution)/shard_map/ppermute | solution.py:410
  19.9 24.6 %collective-permute-start.1 = (bf16[128,1152]{1,0:T(8,128)(2,1)}, bf16[128,1152]{1,0:T(8,128)(2,1)S(1)}, u32[]{:S(2)}, u32[]{:S(2)}) collective-permute-start(bf16[128,1152]{1,0:T(8,128)(2,1)} %get-tuple-element.194), channel_id=1, source_target_pairs={{0,4},{2,6},{4,0},{6,2},{1,5},{3,7},{5,1},{7,3},{8,12},{10,14},{12... | collective-permute-start | bytes 884744 | tf_op jit(solution)/shard_map/ppermute | solution.py:410
  19.9 547.1 %reduce-scatter.7.cloned.1.call-start = ((), (), s32[]{:S(2)}) async-start(), calls=%async_computation.7 | async-start | bytes 2488320
  32.6 39.6 %collective-permute-start.10 = (bf16[2,288,864]{2,1,0:T(8,128)(2,1)}, bf16[2,288,864]{2,1,0:T(8,128)(2,1)}, u32[]{:S(2)}, u32[]{:S(2)}) collective-permute-start(bf16[2,288,864]{2,1,0:T(8,128)(2,1)} %pad_maximum_fusion.22), channel_id=1, source_target_pairs={{0,24},{8,16},{16,8},{24,0},{1,25},{9,17},{17,9},{25,1},{2,26},{10... | collective-permute-start | bytes 2985992 | tf_op jit(solution)/shard_map/ppermute | solution.py:407
  36.0 55.4 %collective-permute-start.9 = (bf16[2,288,864]{2,1,0:T(8,128)(2,1)}, bf16[2,288,864]{2,1,0:T(8,128)(2,1)}, u32[]{:S(2)}, u32[]{:S(2)}) collective-permute-start(bf16[2,288,864]{2,1,0:T(8,128)(2,1)} %pad_maximum_fusion.21), channel_id=1, source_target_pairs={{0,16},{8,24},{16,0},{24,8},{1,17},{9,25},{17,1},{25,9},{2,18},{10... | collective-permute-start | bytes 2985992 | tf_op jit(solution)/shard_map/ppermute | solution.py:407
  36.6 54.9 %collective-permute-start.8 = (bf16[2,288,864]{2,1,0:T(8,128)(2,1)S(1)}, bf16[2,288,864]{2,1,0:T(8,128)(2,1)}, u32[]{:S(2)}, u32[]{:S(2)}) collective-permute-start(bf16[2,288,864]{2,1,0:T(8,128)(2,1)S(1)} %pad_maximum_fusion.20), channel_id=1, source_target_pairs={{0,8},{8,0},{16,24},{24,16},{1,9},{9,1},{17,25},{25,17},{2,10},{10... | collective-permute-start | bytes 2985992 | tf_op jit(solution)/shard_map/ppermute | solution.py:407
  46.5 51.7 %collective-permute-start.3 = (bf16[4,128,1152]{2,1,0:T(8,128)(2,1)S(1)}, bf16[4,128,1152]{2,1,0:T(8,128)(2,1)}, u32[]{:S(2)}, u32[]{:S(2)}) collective-permute-start(bf16[4,128,1152]{2,1,0:T(8,128)(2,1)S(1)} %pad_maximum_fusion.5.own), channel_id=1, source_target_pairs={{0,1},{1,0},{2,3},{3,2},{4,5},{5,4},{6,7},{7,6},{8,9},{9,8},{10,11... | collective-permute-start | bytes 3538952 | tf_op jit(solution)/shard_map/ppermute | solution.py:413
  98.1 71.7 %collective-permute-start.11 = (bf16[4,2,288,864]{3,2,1,0:T(8,128)(2,1)}, bf16[4,2,288,864]{3,2,1,0:T(8,128)(2,1)}, u32[]{:S(2)}, u32[]{:S(2)}) collective-permute-start(bf16[4,2,288,864]{3,2,1,0:T(8,128)(2,1)} %get-tuple-element.116), channel_id=1, source_target_pairs={{0,1},{1,0},{2,3},{3,2},{4,5},{5,4},{6,7},{7,6},{8,9},{9,8},{10,11... | collective-permute-start | bytes 11943944 | tf_op jit(solution)/shard_map/ppermute | solution.py:413
  130.5 28.0 %collective-permute-start.12 = (bf16[512,1152]{1,0:T(8,128)(2,1)S(1)}, bf16[512,1152]{1,0:T(8,128)(2,1)S(1)}, u32[]{:S(2)}, u32[]{:S(2)}) collective-permute-start(bf16[512,1152]{1,0:T(8,128)(2,1)S(1)} %multiply_convert_fusion.x.refs_0_), channel_id=1, source_target_pairs={{0,8},{8,0},{16,24},{24,16},{1,9},{9,1},{17,25},{25,17},{2,10},{10... | collective-permute-start | bytes 3538952 | tf_op jit(solution)/shard_map/ppermute | solution.py:407
  132.1 36.0 %collective-permute-start.14 = (bf16[512,1152]{1,0:T(8,128)(2,1)S(1)}, bf16[512,1152]{1,0:T(8,128)(2,1)}, u32[]{:S(2)}, u32[]{:S(2)}) collective-permute-start(bf16[512,1152]{1,0:T(8,128)(2,1)S(1)} %multiply_convert_fusion.x.refs_0_), channel_id=1, source_target_pairs={{0,16},{8,24},{16,0},{24,8},{1,17},{9,25},{17,1},{25,9},{2,18},{10... | collective-permute-start | bytes 3538952 | tf_op jit(solution)/shard_map/ppermute | solution.py:407
  160.5 18.8 %collective-permute-start.13 = (bf16[256,1152]{1,0:T(8,128)(2,1)}, bf16[256,1152]{1,0:T(8,128)(2,1)}, u32[]{:S(2)}, u32[]{:S(2)}) collective-permute-start(bf16[256,1152]{1,0:T(8,128)(2,1)} %slice.277), channel_id=1, source_target_pairs={{0,16},{8,24},{16,0},{24,8},{1,17},{9,25},{17,1},{25,9},{2,18},{10... | collective-permute-start | bytes 1769480 | tf_op jit(solution)/shard_map/ppermute | solution.py:407
  163.0 85.9 %collective-permute-start.25 = (bf16[128,1152]{1,0:T(8,128)(2,1)}, bf16[128,1152]{1,0:T(8,128)(2,1)}, u32[]{:S(2)}, u32[]{:S(2)}) collective-permute-start(bf16[128,1152]{1,0:T(8,128)(2,1)} %get-tuple-element.171), channel_id=1, source_target_pairs={{0,6},{2,4},{4,2},{6,0},{1,7},{3,5},{5,3},{7,1},{8,14},{10,12},{12... | collective-permute-start | bytes 884744 | tf_op jit(solution)/shard_map/ppermute | solution.py:410
  166.7 82.1 %collective-permute-start.24 = (bf16[128,1152]{1,0:T(8,128)(2,1)}, bf16[128,1152]{1,0:T(8,128)(2,1)}, u32[]{:S(2)}, u32[]{:S(2)}) collective-permute-start(bf16[128,1152]{1,0:T(8,128)(2,1)} %get-tuple-element.172), channel_id=1, source_target_pairs={{0,4},{2,6},{4,0},{6,2},{1,5},{3,7},{5,1},{7,3},{8,12},{10,14},{12... | collective-permute-start | bytes 884744 | tf_op jit(solution)/shard_map/ppermute | solution.py:410
  168.1 80.8 %collective-permute-start.23 = (bf16[128,1152]{1,0:T(8,128)(2,1)}, bf16[128,1152]{1,0:T(8,128)(2,1)}, u32[]{:S(2)}, u32[]{:S(2)}) collective-permute-start(bf16[128,1152]{1,0:T(8,128)(2,1)} %get-tuple-element.170), channel_id=1, source_target_pairs={{0,2},{2,0},{4,6},{6,4},{1,3},{3,1},{5,7},{7,5},{8,10},{10,8},{12,... | collective-permute-start | bytes 884744 | tf_op jit(solution)/shard_map/ppermute | solution.py:410
  200.8 31.6 %collective-permute-start.18 = (bf16[256,1152]{1,0:T(8,128)(2,1)S(1)}, bf16[256,1152]{1,0:T(8,128)(2,1)S(1)}, u32[]{:S(2)}, u32[]{:S(2)}) collective-permute-start(bf16[256,1152]{1,0:T(8,128)(2,1)S(1)} %get-tuple-element.184), channel_id=1, source_target_pairs={{0,8},{8,0},{16,24},{24,16},{1,9},{9,1},{17,25},{25,17},{2,10},{10... | collective-permute-start | bytes 1769480 | tf_op jit(solution)/shard_map/ppermute | solution.py:407
  232.6 37.0 %collective-permute-start.19 = (bf16[512,1152]{1,0:T(8,128)(2,1)S(1)}, bf16[512,1152]{1,0:T(8,128)(2,1)S(1)}, u32[]{:S(2)}, u32[]{:S(2)}) collective-permute-start(bf16[512,1152]{1,0:T(8,128)(2,1)S(1)} %pad_maximum_fusion.8), channel_id=1, source_target_pairs={{0,16},{8,24},{16,0},{24,8},{1,17},{9,25},{17,1},{25,9},{2,18},{10... | collective-permute-start | bytes 3538952 | tf_op jit(solution)/shard_map/ppermute | solution.py:407
  248.2 21.3 %collective-permute-start.17 = (bf16[512,1152]{1,0:T(8,128)(2,1)S(1)}, bf16[512,1152]{1,0:T(8,128)(2,1)S(1)}, u32[]{:S(2)}, u32[]{:S(2)}) collective-permute-start(bf16[512,1152]{1,0:T(8,128)(2,1)S(1)} %pad_maximum_fusion.7), channel_id=1, source_target_pairs={{0,8},{8,0},{16,24},{24,16},{1,9},{9,1},{17,25},{25,17},{2,10},{10... | collective-permute-start | bytes 3538952 | tf_op jit(solution)/shard_map/ppermute | solution.py:407
  275.0 24.2 %collective-permute-start.26 = (bf16[512,1152]{1,0:T(8,128)(2,1)S(1)}, bf16[512,1152]{1,0:T(8,128)(2,1)S(1)}, u32[]{:S(2)}, u32[]{:S(2)}) collective-permute-start(bf16[512,1152]{1,0:T(8,128)(2,1)S(1)} %get-tuple-element.131.z.refs_4_), channel_id=1, source_target_pairs={{0,8},{8,0},{16,24},{24,16},{1,9},{9,1},{17,25},{25,17},{2,10},{10... | collective-permute-start | bytes 3538952 | tf_op jit(solution)/shard_map/ppermute | solution.py:407
  275.5 40.5 %collective-permute-start.28 = (bf16[512,1152]{1,0:T(8,128)(2,1)S(1)}, bf16[512,1152]{1,0:T(8,128)(2,1)S(1)}, u32[]{:S(2)}, u32[]{:S(2)}) collective-permute-start(bf16[512,1152]{1,0:T(8,128)(2,1)S(1)} %get-tuple-element.131.z.refs_4_), channel_id=1, source_target_pairs={{0,16},{8,24},{16,0},{24,8},{1,17},{9,25},{17,1},{25,9},{2,18},{10... | collective-permute-start | bytes 3538952 | tf_op jit(solution)/shard_map/ppermute | solution.py:407
  299.3 33.6 %collective-permute-start.27 = (bf16[256,1152]{1,0:T(8,128)(2,1)S(1)}, bf16[256,1152]{1,0:T(8,128)(2,1)S(1)}, u32[]{:S(2)}, u32[]{:S(2)}) collective-permute-start(bf16[256,1152]{1,0:T(8,128)(2,1)S(1)} %slice.280), channel_id=1, source_target_pairs={{0,16},{8,24},{16,0},{24,8},{1,17},{9,25},{17,1},{25,9},{2,18},{10... | collective-permute-start | bytes 1769480 | tf_op jit(solution)/shard_map/ppermute | solution.py:407
  343.8 53.1 %collective-permute-start.64 = (bf16[864,1152]{1,0:T(8,128)(2,1)}, bf16[864,1152]{1,0:T(8,128)(2,1)}, u32[]{:S(2)}, u32[]{:S(2)}) collective-permute-start(bf16[864,1152]{1,0:T(8,128)(2,1)} %shard_map.285), channel_id=1, source_target_pairs={{0,1},{1,0},{2,3},{3,2},{4,5},{5,4},{6,7},{7,6},{8,9},{9,8},{10,11... | collective-permute-start | bytes 5971976 | tf_op jit(solution)/shard_map/ppermute | solution.py:413
  396.4 35.1 %collective-permute-start.59 = (bf16[2,1152,864]{1,2,0:T(8,128)(2,1)}, bf16[2,1152,864]{1,2,0:T(8,128)(2,1)}, u32[]{:S(2)}, u32[]{:S(2)}) collective-permute-start(bf16[2,1152,864]{1,2,0:T(8,128)(2,1)} %copy.34), channel_id=1, source_target_pairs={{0,1},{1,0},{2,3},{3,2},{4,5},{5,4},{6,7},{7,6},{8,9},{9,8},{10,11... | collective-permute-start | bytes 11943944 | tf_op jit(solution)/shard_map/ppermute | solution.py:413
  407.0 184.8 %reduce-scatter.5.cloned.1.call-start = ((), (), s32[]{:S(2)}) async-start(), calls=%async_computation.4 | async-start | bytes 5160960 | tf_op jit(solution)/shard_map/reduce_scatter | solution.py:546
  425.0 39.7 %collective-permute-start.33 = (bf16[512,1152]{1,0:T(8,128)(2,1)}, bf16[512,1152]{1,0:T(8,128)(2,1)}, u32[]{:S(2)}, u32[]{:S(2)}) collective-permute-start(bf16[512,1152]{1,0:T(8,128)(2,1)} %pad_maximum_fusion.14), channel_id=1, source_target_pairs={{0,16},{8,24},{16,0},{24,8},{1,17},{9,25},{17,1},{25,9},{2,18},{10... | collective-permute-start | bytes 3538952 | tf_op jit(solution)/shard_map/ppermute | solution.py:407
  427.7 37.1 %collective-permute-start.31 = (bf16[512,1152]{1,0:T(8,128)(2,1)}, bf16[512,1152]{1,0:T(8,128)(2,1)}, u32[]{:S(2)}, u32[]{:S(2)}) collective-permute-start(bf16[512,1152]{1,0:T(8,128)(2,1)} %pad_maximum_fusion.13), channel_id=1, source_target_pairs={{0,8},{8,0},{16,24},{24,16},{1,9},{9,1},{17,25},{25,17},{2,10},{10... | collective-permute-start | bytes 3538952 | tf_op jit(solution)/shard_map/ppermute | solution.py:407
  457.9 255.5 %all-gather.11.cloned.1.call-start = ((), (), s32[]{:S(2)}) async-start(), calls=%async_computation.6 | async-start | bytes 2488320 | tf_op jit(solution)/shard_map/all_gather | solution.py:551
  463.5 57.0 %collective-permute-start.21 = (bf16[128,1152]{1,0:T(8,128)(2,1)}, bf16[128,1152]{1,0:T(8,128)(2,1)}, u32[]{:S(2)}, u32[]{:S(2)}) collective-permute-start(bf16[128,1152]{1,0:T(8,128)(2,1)} %get-tuple-element.179), channel_id=1, source_target_pairs={{0,4},{2,6},{4,0},{6,2},{1,5},{3,7},{5,1},{7,3},{8,12},{10,14},{12... | collective-permute-start | bytes 884744 | tf_op jit(solution)/shard_map/ppermute | solution.py:410
  463.6 56.8 %collective-permute-start.20 = (bf16[128,1152]{1,0:T(8,128)(2,1)}, bf16[128,1152]{1,0:T(8,128)(2,1)}, u32[]{:S(2)}, u32[]{:S(2)}) collective-permute-start(bf16[128,1152]{1,0:T(8,128)(2,1)} %get-tuple-element.180), channel_id=1, source_target_pairs={{0,2},{2,0},{4,6},{6,4},{1,3},{3,1},{5,7},{7,5},{8,10},{10,8},{12,... | collective-permute-start | bytes 884744 | tf_op jit(solution)/shard_map/ppermute | solution.py:410
  473.5 49.8 %collective-permute-start.34 = (bf16[4,128,1152]{2,1,0:T(8,128)(2,1)S(1)}, bf16[4,128,1152]{2,1,0:T(8,128)(2,1)}, u32[]{:S(2)}, u32[]{:S(2)}) collective-permute-start(bf16[4,128,1152]{2,1,0:T(8,128)(2,1)S(1)} %bitcast.222), channel_id=1, source_target_pairs={{0,1},{1,0},{2,3},{3,2},{4,5},{5,4},{6,7},{7,6},{8,9},{9,8},{10,11... | collective-permute-start | bytes 3538952 | tf_op jit(solution)/shard_map/ppermute | solution.py:413
  476.1 91.3 %collective-permute-start.38 = (bf16[1152,512]{1,0:T(8,128)(2,1)}, bf16[1152,512]{1,0:T(8,128)(2,1)}, u32[]{:S(2)}, u32[]{:S(2)}) collective-permute-start(bf16[1152,512]{1,0:T(8,128)(2,1)} %slice.284), channel_id=1, source_target_pairs={{0,1},{1,0},{2,3},{3,2},{4,5},{5,4},{6,7},{7,6},{8,9},{9,8},{10,11... | collective-permute-start | bytes 3538952 | tf_op jit(solution)/shard_map/ppermute | solution.py:413
  555.6 34.8 %collective-permute-start.50 = (bf16[2,128,1152]{2,1,0:T(8,128)(2,1)}, bf16[2,128,1152]{2,1,0:T(8,128)(2,1)}, u32[]{:S(2)}, u32[]{:S(2)}) collective-permute-start(bf16[2,128,1152]{2,1,0:T(8,128)(2,1)} %dynamic-slice_bitcast_fusion), channel_id=1, source_target_pairs={{0,1},{1,0},{2,3},{3,2},{4,5},{5,4},{6,7},{7,6},{8,9},{9,8},{10,11... | collective-permute-start | bytes 1769480 | tf_op jit(solution)/shard_map/ppermute | solution.py:413
  567.0 176.1 %all-gather.9.cloned.1.call-start = ((), (), s32[]{:S(2)}) async-start(), calls=%async_computation.5 | async-start | bytes 5160960 | tf_op jit(solution)/shard_map/all_gather | solution.py:552
  584.3 34.1 %collective-permute-start.42 = (bf16[144,768]{1,0:T(8,128)(2,1)}, bf16[144,768]{1,0:T(8,128)(2,1)}, u32[]{:S(2)}, u32[]{:S(2)}) collective-permute-start(bf16[144,768]{1,0:T(8,128)(2,1)} %get-tuple-element.141), channel_id=1, source_target_pairs={{0,16},{8,24},{16,0},{24,8},{1,17},{9,25},{17,1},{25,9},{2,18},{10... | collective-permute-start | bytes 663560 | tf_op jit(solution)/shard_map/ppermute | solution.py:407
  585.6 32.7 %collective-permute-start.44 = (bf16[144,768]{1,0:T(8,128)(2,1)}, bf16[144,768]{1,0:T(8,128)(2,1)}, u32[]{:S(2)}, u32[]{:S(2)}) collective-permute-start(bf16[144,768]{1,0:T(8,128)(2,1)} %get-tuple-element.143), channel_id=1, source_target_pairs={{0,8},{8,0},{16,24},{24,16},{1,9},{9,1},{17,25},{25,17},{2,10},{10... | collective-permute-start | bytes 663560 | tf_op jit(solution)/shard_map/ppermute | solution.py:407
  619.6 25.4 %collective-permute-start.45 = (bf16[288,768]{1,0:T(8,128)(2,1)S(1)}, bf16[288,768]{1,0:T(8,128)(2,1)S(1)}, u32[]{:S(2)}, u32[]{:S(2)}) collective-permute-start(bf16[288,768]{1,0:T(8,128)(2,1)S(1)} %pad_maximum_fusion.28), channel_id=1, source_target_pairs={{0,16},{8,24},{16,0},{24,8},{1,17},{9,25},{17,1},{25,9},{2,18},{10... | collective-permute-start | bytes 1327112 | tf_op jit(solution)/shard_map/ppermute | solution.py:407
  620.6 25.1 %collective-permute-start.43 = (bf16[288,768]{1,0:T(8,128)(2,1)S(1)}, bf16[288,768]{1,0:T(8,128)(2,1)S(1)}, u32[]{:S(2)}, u32[]{:S(2)}) collective-permute-start(bf16[288,768]{1,0:T(8,128)(2,1)S(1)} %pad_maximum_fusion.27), channel_id=1, source_target_pairs={{0,8},{8,0},{16,24},{24,16},{1,9},{9,1},{17,25},{25,17},{2,10},{10... | collective-permute-start | bytes 1327112 | tf_op jit(solution)/shard_map/ppermute | solution.py:407
  628.9 29.1 %collective-permute-start.41 = (bf16[128,1152]{1,0:T(8,128)(2,1)S(1)}, bf16[128,1152]{1,0:T(8,128)(2,1)S(1)}, u32[]{:S(2)}, u32[]{:S(2)}) collective-permute-start(bf16[128,1152]{1,0:T(8,128)(2,1)S(1)} %get-tuple-element.156), channel_id=1, source_target_pairs={{0,6},{2,4},{4,2},{6,0},{1,7},{3,5},{5,3},{7,1},{8,14},{10,12},{12... | collective-permute-start | bytes 884744 | tf_op jit(solution)/shard_map/ppermute | solution.py:410
  631.5 49.7 %collective-permute-start.40 = (bf16[128,1152]{1,0:T(8,128)(2,1)S(1)}, bf16[128,1152]{1,0:T(8,128)(2,1)S(1)}, u32[]{:S(2)}, u32[]{:S(2)}) collective-permute-start(bf16[128,1152]{1,0:T(8,128)(2,1)S(1)} %get-tuple-element.157), channel_id=1, source_target_pairs={{0,4},{2,6},{4,0},{6,2},{1,5},{3,7},{5,1},{7,3},{8,12},{10,14},{12... | collective-permute-start | bytes 884744 | tf_op jit(solution)/shard_map/ppermute | solution.py:410
  642.4 38.7 %collective-permute-start.39 = (bf16[128,1152]{1,0:T(8,128)(2,1)S(1)}, bf16[128,1152]{1,0:T(8,128)(2,1)S(1)}, u32[]{:S(2)}, u32[]{:S(2)}) collective-permute-start(bf16[128,1152]{1,0:T(8,128)(2,1)S(1)} %get-tuple-element.158), channel_id=1, source_target_pairs={{0,2},{2,0},{4,6},{6,4},{1,3},{3,1},{5,7},{7,5},{8,10},{10,8},{12,... | collective-permute-start | bytes 884744 | tf_op jit(solution)/shard_map/ppermute | solution.py:410
  645.9 51.8 %collective-permute-start.46 = (bf16[288,768]{1,0:T(8,128)(2,1)S(1)}, bf16[288,768]{1,0:T(8,128)(2,1)S(1)}, u32[]{:S(2)}, u32[]{:S(2)}) collective-permute-start(bf16[288,768]{1,0:T(8,128)(2,1)S(1)} %fusion.28), channel_id=1, source_target_pairs={{0,2},{6,4},{1,3},{7,5},{8,10},{14,12},{9,11},{15,13},{16,18},{22,... | collective-permute-start | bytes 1327112 | tf_op jit(solution)/shard_map/ppermute | solution.py:446
  651.3 59.0 %collective-permute-start.57 = (bf16[128,1152]{1,0:T(8,128)(2,1)S(1)}, bf16[128,1152]{1,0:T(8,128)(2,1)S(1)}, u32[]{:S(2)}, u32[]{:S(2)}) collective-permute-start(bf16[128,1152]{1,0:T(8,128)(2,1)S(1)} %add.359), channel_id=1, source_target_pairs={{2,0},{4,6},{3,1},{5,7},{10,8},{12,14},{11,9},{13,15},{18,16},{20,... | collective-permute-start | bytes 884744 | tf_op jit(solution)/shard_map/ppermute | solution.py:450
  711.9 30.1 %collective-permute-start.48 = (bf16[288,768]{1,0:T(8,128)(2,1)S(1)}, bf16[288,768]{1,0:T(8,128)(2,1)}, u32[]{:S(2)}, u32[]{:S(2)}) collective-permute-start(bf16[288,768]{1,0:T(8,128)(2,1)S(1)} %add.353), channel_id=1, source_target_pairs={{2,0},{4,6},{3,1},{5,7},{10,8},{12,14},{11,9},{13,15},{18,16},{20,... | collective-permute-start | bytes 1327112 | tf_op jit(solution)/shard_map/ppermute | solution.py:450
  713.4 35.7 %collective-permute-start.65 = (bf16[864,1152]{1,0:T(8,128)(2,1)}, bf16[864,1152]{1,0:T(8,128)(2,1)S(1)}, u32[]{:S(2)}, u32[]{:S(2)}) collective-permute-start(bf16[864,1152]{1,0:T(8,128)(2,1)} %all-gather.11.cloned.1.call-done), channel_id=1, source_target_pairs={{0,1},{1,0},{2,3},{3,2},{4,5},{5,4},{6,7},{7,6},{8,9},{9,8},{10,11... | collective-permute-start | bytes 5971976 | tf_op jit(solution)/shard_map/ppermute | solution.py:413
  (116 other events, 996.9 us)
Sparse Core Ops, SparseCore 0:
  10.5 71.5 all-gather.4
  83.9 39.0 all-gather.6
  407.1 42.0 reduce-scatter.6
  458.0 92.4 reduce-scatter.4
  567.1 41.8 all-gather.10
  611.1 117.1 all-gather.8

commit v3 on v2

v3 whole, which is shorter than its diff:
```python
import functools

import jax
import jax.numpy as jnp
from jax import lax
from jax.experimental import pallas as pl
from jax.experimental.pallas import tpu as pltpu
from jax.sharding import Mesh
from jax.sharding import PartitionSpec as P

HEADS = 4
HD = 256
PIECE = 256
EPS = 1e-06
ROPE_BASE = 1000000.0
SCALE = 0.0625
BF = jnp.bfloat16
F32 = jnp.float32
LANES = 128
ORDER = (0, 1, 3, 2)


def dot(a, b):
    return lax.dot_general(a, b, (((1,), (0,)), ((), ())), preferred_element_type=F32)


def dot_t(a, b):
    return lax.dot_general(a, b, (((1,), (1,)), ((), ())), preferred_element_type=F32)


def dot_rows(a, b):
    return lax.dot_general(a, b, (((0,), (0,)), ((), ())), preferred_element_type=F32)


def inv_rms(v):
    return lax.rsqrt(jnp.mean(v * v, axis=-1, keepdims=True) + EPS)


def rms_back(v, r, gain, z):
    gz = gain * z
    return r * gz - v * (r * r * r * jnp.mean(gz * v, axis=-1, keepdims=True))


def rope(v, cos, sin):
    half = v.shape[-1] // 2
    a, b = v[..., :half], v[..., half:]
    return jnp.concatenate([a * cos - b * sin, b * cos + a * sin], axis=-1)


def gelu_and_slope(u):
    k = 0.7978845608028654
    u2 = u * u
    t = jnp.tanh(k * (u + 0.044715 * u2 * u))
    half = 0.5 * (1.0 + t)
    slope = half + 0.5 * u * (1.0 - t * t) * (k * (1.0 + 3.0 * 0.044715 * u2))
    return u * half, slope


def call(kernel, grid, in_specs, out_specs, out_shape, flops, nbytes, scalars=0, scratch=(), exps=0, vmem=56):
    return pl.pallas_call(
        kernel,
        grid_spec=pltpu.PrefetchScalarGridSpec(
            num_scalar_prefetch=scalars,
            grid=grid,
            in_specs=in_specs,
            out_specs=out_specs,
            scratch_shapes=list(scratch),
        ),
        out_shape=out_shape,
        compiler_params=pltpu.CompilerParams(
            dimension_semantics=("arbitrary",) * len(grid), vmem_limit_bytes=vmem * 1024 * 1024
        ),
        cost_estimate=pl.CostEstimate(flops=flops, bytes_accessed=nbytes, transcendentals=exps),
    )


def full(shape):
    return pl.BlockSpec(shape, lambda *_: (0,) * len(shape))


def qkv_kernel(at, own, oth, w, ga, gq, gk, cos, sin, nin_o, raw_o, q_o, k_o, v_o):
    first = at[1] == 0
    a, b = own[0], oth[0]
    x = jnp.concatenate([jnp.where(first, a, b), jnp.where(first, b, a)]).astype(F32)
    nin = (x * inv_rms(x) * ga[...]).astype(BF)
    nin_o[...] = nin
    raw = dot(nin, w[...])
    raw_o[...] = raw[:, : 3 * HD]
    c, s = cos[...], sin[...]
    for h in range(2):
        q = raw[:, h * HD : (h + 1) * HD]
        q_o[:, h * HD : (h + 1) * HD] = rope(q * inv_rms(q) * (gq[...] * SCALE), c, s).astype(BF)
    k = raw[:, 2 * HD : 3 * HD]
    k_o[...] = rope(k * inv_rms(k) * gk[...], c, s).astype(BF)
    v_o[...] = raw[:, 3 * HD :].astype(BF)


def project(at, own, oth, w, ga, gq, gk, cos, sin):
    seqs, n, width = own.shape
    rows = 2 * n * seqs
    cols = w.shape[1]
    block = pl.BlockSpec((1, n, width), lambda i, at: (i ^ at[0], 0, 0))

    def row(c):
        return pl.BlockSpec((2 * n, c), lambda i, at: (i, 0))

    shapes = [(width, BF), (3 * HD, F32), (2 * HD, BF), (HD, BF), (HD, BF)]
    return call(
        qkv_kernel,
        (seqs,),
        [block, block, pl.BlockSpec(memory_space=pltpu.VMEM), full(ga.shape), full(gq.shape), full(gk.shape), row(HD // 2), row(HD // 2)],
        [row(c) for c, _ in shapes],
        [jax.ShapeDtypeStruct((rows, c), t) for c, t in shapes],
        2 * rows * width * cols,
        rows * width * 8 + width * cols * 2,
        scalars=1,
    )(at, own, oth, w, ga, gq, gk, cos, sin)


def reach(at, q):
    last = q
    for j in range(2):
        s = at[3 + j]
        last = jnp.where((q >= s) & (q < s + PIECE), s + (PIECE - 1), last)
    return last


def key_parts(at, tile, length):
    first = at[2] + pl.program_id(1) * tile
    last = first + tile - 1
    for j in range(2):
        s = at[3 + j]
        meets = (s < first + tile) & (s + PIECE > first)
        last = jnp.maximum(last, jnp.where(meets, s + (PIECE - 1), 0))
    return last // (length // 4) + 1


def tile_places(at, tile, shape, axis):
    return at[2] + pl.program_id(1) * tile + lax.broadcasted_iota(jnp.int32, shape, axis)


def attend_kernel(tile, at, q, k, v, o):
    length = k.shape[0]
    parts = key_parts(at, tile, length)
    last = reach(at, tile_places(at, tile, (tile, 1), 0))
    for n in range(1, 5):

        @pl.when(parts == n)
        def _():
            m = n * (length // 4)
            s = dot_t(q[...], k[:m])
            s = jnp.where(lax.broadcasted_iota(jnp.int32, (tile, m), 1) <= last, s, -1e30)
            e = jnp.exp(s - jnp.max(s, axis=-1, keepdims=True))
            p = (e * (1.0 / jnp.sum(e, axis=-1, keepdims=True))).astype(BF)
            o[...] = dot(p, v[:m]).astype(BF)


def attend(at, q, k, v, tile=256):
    rows, length = q.shape[0], k.shape[0]
    heads = q.shape[1] // HD
    qs = pl.BlockSpec((tile, HD), lambda h, i, at: (i, h))
    return call(
        functools.partial(attend_kernel, tile),
        (heads, rows // tile),
        [qs, full(k.shape), full(v.shape)],
        qs,
        jax.ShapeDtypeStruct(q.shape, BF),
        4 * rows * heads * length * HD,
        rows * heads * HD * 4 + length * HD * 4,
        scalars=1,
        exps=rows * heads * length,
    )(at, q, k, v)


def attend_back_kernel(tile, at, q, k, v, do, qraw, gq, cos, sin, dq_o, dk_o, dv_o, gg_o, dq_t):
    length = k.shape[0]

    @pl.when((pl.program_id(0) == 0) & (pl.program_id(1) == 0))
    def _():
        dk_o[...] = jnp.zeros_like(dk_o)
        dv_o[...] = jnp.zeros_like(dv_o)
        gg_o[...] = jnp.zeros_like(gg_o)

    parts = key_parts(at, tile, length)
    last = reach(at, tile_places(at, tile, (1, tile), 1))
    for n in range(1, 5):

        @pl.when(parts == n)
        def _():
            m = n * (length // 4)
            s = dot_t(k[:m], q[...])
            s = jnp.where(lax.broadcasted_iota(jnp.int32, (m, tile), 0) <= last, s, -1e30)
            e = jnp.exp(s - jnp.max(s, axis=0, keepdims=True))
            p = e * (1.0 / jnp.sum(e, axis=0, keepdims=True))
            dp = dot_t(v[:m], do[...])
            ds = (p * (dp - jnp.sum(p * dp, axis=0, keepdims=True))).astype(BF)
            dv_o[:m] += dot(p.astype(BF), do[...])
            dk_o[:m] += dot(ds, q[...])
            dq_t[...] = dot_rows(ds, k[:m])

    un = rope(dq_t[...] * SCALE, cos[...], -sin[...])
    raw = qraw[...]
    r = inv_rms(raw)
    gg_o[...] += jnp.sum(un * raw * r, axis=0, keepdims=True)
    dq_o[...] = rms_back(raw, r, gq[...], un).astype(BF)


def attend_back(at, q, k, v, do, raw, gq, cos, sin, tile=256):
    rows, length = q.shape[0], k.shape[0]
    heads = q.shape[1] // HD
    qs = pl.BlockSpec((tile, HD), lambda h, i, at: (i, h))
    cs = pl.BlockSpec((tile, HD // 2), lambda h, i, at: (i, 0))
    return call(
        functools.partial(attend_back_kernel, tile),
        (heads, rows // tile),
        [qs, full(k.shape), full(v.shape), qs, qs, full(gq.shape), cs, cs],
        [qs, full(k.shape), full(v.shape), full(gq.shape)],
        [
            jax.ShapeDtypeStruct(q.shape, BF),
            jax.ShapeDtypeStruct(k.shape, F32),
            jax.ShapeDtypeStruct(v.shape, F32),
            jax.ShapeDtypeStruct(gq.shape, F32),
        ],
        10 * rows * heads * length * HD,
        rows * heads * HD * 12 + length * HD * 12,
        scalars=1,
        scratch=[pltpu.VMEM((tile, HD), F32)],
        exps=rows * heads * length,
    )(at, q, k, v, do, raw, gq, cos, sin)


def ffn_kernel(x, w, wd, gel_o, slope_o, h_o, p_o):
    xv = x[...]
    u = dot(xv, w[1])
    gel, slope = gelu_and_slope(dot(xv, w[0]))
    hid = (gel * u).astype(BF)
    gel_o[...] = gel.astype(BF)
    slope_o[...] = (slope * u).astype(BF)
    h_o[...] = hid
    p_o[...] = dot(hid, wd[...]).astype(p_o.dtype)


def ffn(x, w, wd, kind, tile=256):
    rows, width = x.shape
    f = w.shape[-1]
    keep = pl.BlockSpec(memory_space=pltpu.VMEM)
    act = pl.BlockSpec((tile, f), lambda i: (i, 0))
    row = pl.BlockSpec((tile, width), lambda i: (i, 0))
    return call(
        ffn_kernel,
        (rows // tile,),
        [row, keep, keep],
        [act, act, act, row],
        [jax.ShapeDtypeStruct((rows, f), BF)] * 3 + [jax.ShapeDtypeStruct(x.shape, kind)],
        6 * rows * width * f,
        6 * width * f + 6 * rows * f + 4 * rows * width,
        exps=rows * f,
        vmem=40,
    )(x, w, wd)


def ffn_back_kernel(z, w, wd, gel, slope, gu_o, p_o):
    hg = dot_t(z[...], wd[...])
    gg = (hg * slope[...].astype(F32)).astype(BF)
    ug = (hg * gel[...].astype(F32)).astype(BF)
    gu_o[0] = gg
    gu_o[1] = ug
    p_o[...] = (dot_t(gg, w[0]) + dot_t(ug, w[1])).astype(p_o.dtype)


def ffn_back(z, w, wd, gel, slope, kind, tile=256):
    rows, width = z.shape
    f = w.shape[-1]
    keep = pl.BlockSpec(memory_space=pltpu.VMEM)
    act = pl.BlockSpec((tile, f), lambda i: (i, 0))
    row = pl.BlockSpec((tile, width), lambda i: (i, 0))
    return call(
        ffn_back_kernel,
        (rows // tile,),
        [row, keep, keep, act, act],
        [pl.BlockSpec((2, tile, f), lambda i: (0, i, 0)), row],
        [jax.ShapeDtypeStruct((2, rows, f), BF), jax.ShapeDtypeStruct(z.shape, kind)],
        6 * rows * width * f,
        6 * width * f + 6 * rows * f + 4 * rows * width,
        vmem=40,
    )(z, w, wd, gel, slope)


def columns_grad_kernel(n, *refs):
    x, g = refs[:n], refs[n : 2 * n]
    outs = refs[2 * n : 2 * n + 2]
    f = outs[0].shape[-1]
    xt = [x[k][...].T for k in range(n)]
    for i, o in enumerate(outs):
        total = dot(xt[0], g[0][0, :, i * f : (i + 1) * f])
        for k in range(1, n):
            total += dot(xt[k], g[k][0, :, i * f : (i + 1) * f])
        n_z, n_s, d, _ = o.shape
        for j in range(n_s):
            for q in range(n_z):
                first = (j * n_z + q) * d
                o[q, j] = total[first : first + d].astype(BF)


def columns_grad(m, xs, gus, form):
    n = len(xs)
    rows, width = xs[0].shape
    f = gus[0].shape[-1]
    out = full(form)
    return call(
        functools.partial(columns_grad_kernel, n),
        (1,),
        [full((rows, width))] * n + [pl.BlockSpec((1, rows, f), lambda i: (m, 0, 0))] * n,
        [out, out],
        [jax.ShapeDtypeStruct(form, BF)] * 2,
        2 * n * rows * width * f,
        n * rows * (width + f) * 2 + 2 * width * f,
    )(*xs, *gus)


def down_grad_kernel(n, *refs):
    hid, z = refs[:n], refs[n : 2 * n]
    outs = refs[2 * n :]
    f = hid[0].shape[-1] // 2
    for i, o in enumerate(outs):
        total = dot_rows(hid[0][:, i * f : (i + 1) * f], z[0][...])
        for k in range(1, n):
            total += dot_rows(hid[k][:, i * f : (i + 1) * f], z[k][...])
        o[...] = total[: o.shape[0]].astype(BF)


def down_grad(hids, zs, f_own):
    n = len(zs)
    rows, width = zs[0].shape
    f = hids[0].shape[-1]
    out = full((f_own, width))
    return call(
        functools.partial(down_grad_kernel, n),
        (1,),
        [full((rows, f))] * n + [full((rows, width))] * n,
        [out, out],
        [jax.ShapeDtypeStruct((f_own, width), BF)] * 2,
        2 * n * rows * width * f,
        n * rows * (width + f) * 2 + 2 * width * f,
    )(*hids, *zs)


def collect_kernel(n, at, *refs):
    o = refs[-1]
    d, f = refs[0].shape[1:]
    for h in range(2):
        for k in range(n):
            first = pl.multiple_of((at[5] ^ k) * d, d)
            for m in range(2):
                o[m, pl.ds(first, d), h * f : (h + 1) * f] = refs[h * n + k][m]


def collect(at, mine, other):
    n = len(mine)
    _, d, f = mine[0].shape
    keep = pl.BlockSpec(memory_space=pltpu.VMEM)
    shape = (2, n * d, 2 * f)
    return call(
        functools.partial(collect_kernel, n),
        (1,),
        [keep] * (2 * n),
        full(shape),
        jax.ShapeDtypeStruct(shape, BF),
        0,
        4 * n * d * f * 4,
        scalars=1,
        vmem=24,
    )(at, *mine, *other)


def fill_kernel(at, w, o):
    rows = w.shape[0]
    o[:rows] = w[...]
    o[rows:] = jnp.zeros((o.shape[0] - rows, o.shape[1]), BF)


def fill(at, w, f, pad):
    width = w.shape[1]
    return call(
        fill_kernel,
        (2,),
        [pl.BlockSpec((f, width), lambda h, at: (h ^ at[1], 0))],
        pl.BlockSpec((pad, width), lambda h, at: (h, 0)),
        jax.ShapeDtypeStruct((2 * pad, width), BF),
        0,
        8 * f * width,
        scalars=1,
    )(at, w)


def lay_kernel(f, at, mine, oth, g_o, u_o):
    first = at[1] == 0
    for j in range(mine.shape[1]):
        for m, o in ((0, g_o), (1, u_o)):
            a, b = mine[0, j, m, :, :f].astype(F32), oth[0, j, m, :, :f].astype(F32)
            o[:, 2 * j * f : (2 * j + 1) * f] = jnp.where(first, a, b)
            o[:, (2 * j + 1) * f : (2 * j + 2) * f] = jnp.where(first, b, a)


def lay(at, mine, other, f):
    n_z, n_s, _, rows, _ = mine.shape
    block = pl.BlockSpec((1,) + mine.shape[1:], lambda i, at: (i, 0, 0, 0, 0))
    out = pl.BlockSpec((rows, 2 * n_s * f), lambda i, at: (i, 0))
    return call(
        functools.partial(lay_kernel, f),
        (n_z,),
        [block, block],
        [out, out],
        [jax.ShapeDtypeStruct((n_z * rows, 2 * n_s * f), F32)] * 2,
        0,
        n_z * n_s * rows * f * 24,
        scalars=1,
    )(at, mine, other)


def body(
    tokens,
    cotangent,
    pictures,
    w_query,
    w_key,
    w_value,
    w_out,
    w_gate,
    w_up,
    w_down,
    g_attn_in,
    g_attn_out,
    g_ffn_in,
    g_ffn_out,
    g_query,
    g_key,
):
    seqs, piece_len, width = tokens.shape
    n_s = lax.axis_size("shard")
    n_r = lax.axis_size("r")
    n_z = lax.axis_size("z")
    s, z, c = lax.axis_index("shard"), lax.axis_index("z"), lax.axis_index("c")
    own = seqs * piece_len
    both = 2 * own
    heads = HEADS // 2
    hw = heads * HD
    d_own = width // n_s
    ff = w_gate.shape[1]
    ff_own = ff // (2 * n_s)
    ff_pad = -(-ff_own // LANES) * LANES

    def after(v, *others):
        return lax.optimization_barrier((v,) + others)[0]

    def px(v, k):
        return lax.ppermute(v, "shard", [(i, i ^ k) for i in range(n_s)])

    def pz(v, k):
        return lax.ppermute(v, "z", [(i, i ^ k) for i in range(n_z)])

    def pc(v):
        return lax.ppermute(v, "c", [(0, 1), (1, 0)])

    def natural(pieces, index):
        stacked = jnp.stack(pieces)
        n = len(pieces)
        return jnp.stack(
            [lax.dynamic_index_in_dim(stacked, index ^ j, 0, keepdims=False) for j in range(n)]
        )

    def pick(v, index, axis=0):
        return lax.dynamic_index_in_dim(v, index, axis, keepdims=False)

    def by_core(mine, other, axis):
        first = jnp.where(c == 0, mine, other)
        second = jnp.where(c == 0, other, mine)
        return jnp.stack([first, second], axis=axis)

    def gather4(v):
        h = v.shape[0] // 2
        f1, f2 = px(v, 1), px(v, 2)
        f3 = jnp.concatenate([px(f1[:h], 2), px(f2[h:], 1)])
        return [v, f1, f2, f3]

    def scatter_first(p):
        h = p[0].shape[0] // 2
        return px(p[3][:h], 2), px(p[3][h:], 1)

    def scatter_second(p, a, b):
        h = p[0].shape[0] // 2
        q1 = jnp.concatenate([p[1][:h] + a, p[1][h:]])
        q2 = jnp.concatenate([p[2][:h], p[2][h:] + b])
        return q1, q2

    def scatter_last(p, sent):
        return p[0] + px(sent[0], 1).astype(F32) + px(sent[1], 2).astype(F32)

    def scatter4(p):
        return scatter_last(p, scatter_second(p, *scatter_first(p)))

    class Line:
        def __init__(self, v):
            self.part = v
            self.got = lax.ppermute(v, "z", [(0, 1), (3, 2)]) if n_z == 4 else v

        def middle(self, *others):
            if n_z == 4:
                self.part = self.part + after(self.got, *others)
                self.got = lax.ppermute(self.part, "z", [(1, 2), (2, 1)])

        def last(self, *others):
            if n_z == 4:
                self.part = self.part + after(self.got, *others)
                self.got = lax.ppermute(self.part, "z", [(1, 0), (2, 3)])

        @property
        def total(self):
            return self.part

        def done(self, *others):
            if n_z != 4:
                return lax.psum(self.part, ("r", "z"))
            v = jnp.where((z == 0) | (z == 3), after(self.got, *others), self.part)
            return lax.psum(v, "r") if n_r > 1 else v

    def spread(v):
        return jnp.stack([pick(v, z)] + [pz(pick(v, z ^ k), k) for k in range(1, n_z)])

    def in_order(v):
        return jnp.stack([pick(v, z ^ j) for j in range(n_z)])

    wq_half = lax.dynamic_slice_in_dim(w_query, c * hw, hw, 1)
    qkv_mine = jnp.concatenate([wq_half, w_key, w_value], axis=1)
    w_qkv = lax.all_gather(qkv_mine, "shard", axis=0, tiled=True)
    half_head = w_out.shape[0] // 2
    out_mine = lax.dynamic_slice_in_dim(w_out, c * half_head, half_head, 0)
    out_mine = after(out_mine, w_qkv)
    out_half = [out_mine] + [px(out_mine, k) for k in range(1, n_s)]
    near = [pz(pick(tokens, z ^ k), k) for k in range(1, n_z)]
    x_near = jnp.stack([pick(tokens, z)] + near)
    x_near_other = pc(x_near)
    gains = jnp.concatenate([g_attn_in, g_attn_out, g_ffn_in, g_ffn_out, g_query, g_key])
    base = lax.axis_index("r") * both
    w_gate, w_up, w_down_late, gains, base = lax.optimization_barrier(
        (w_gate, w_up, w_down, gains, base, near[0])
    )[:5]
    gains = natural([gains] + [px(gains, k) for k in range(1, n_s)], s)

    def gain(first, size):
        return gains[:, first : first + size].reshape(1, n_s * size)

    hd_own = HD // n_s
    ga_in, ga_out, gf_in, gf_out = (gain(i * d_own, d_own) for i in range(4))
    gq, gk = gain(4 * d_own, hd_own), gain(4 * d_own + hd_own, hd_own)

    def col_piece(w, k):
        first = (s ^ k) * (2 * ff_own) + c * ff_own
        piece = lax.dynamic_slice_in_dim(w, first, ff_own, 1)
        return jnp.pad(piece, ((0, 0), (0, ff_pad - ff_own)))

    gu = [jnp.stack([col_piece(w_gate, k), col_piece(w_up, k)]) for k in range(n_s)]
    gu = [gu[0]] + list(lax.optimization_barrier((*gu[1:], out_mine))[: n_s - 1])
    gu = [gu[0]] + [px(gu[k], k) for k in range(1, n_s)]
    cot_near = spread(after(cotangent, x_near))

    q_pos = base + jnp.arange(both, dtype=jnp.int32)
    half = HD // 2
    inverse = jnp.exp(
        -(jnp.arange(half).astype(F32) * 2.0 / HD) * jnp.log(jnp.float32(ROPE_BASE))
    )
    angle = q_pos.astype(F32)[:, None] * inverse[None, :]
    cos, sin = jnp.cos(angle), jnp.sin(angle)
    starts = pick(pictures, z)
    at = jnp.concatenate([jnp.stack([z, c, base]).astype(jnp.int32), starts.astype(jnp.int32), s[None]])
    wd = fill(at, w_down_late, ff_own, ff_pad)
    x_near_other = after(x_near_other, wd)

    def rows_of(v, core):
        n = v.shape[1]
        return pick(v.reshape(seqs, 2, piece_len, n), core, 1).reshape(own, n)

    def whole(mine):
        n = mine.shape[1]
        mine = mine.reshape(seqs, piece_len, n)
        return by_core(mine, pc(mine), 1).reshape(both, n)

    nin, raw, queries, keys, values = project(at, x_near, x_near_other, w_qkv, ga_in, gq, gk, cos, sin)
    if n_r > 1:
        keys = lax.all_gather(keys, "r", axis=0, tiled=True)
        values = lax.all_gather(values, "r", axis=0, tiled=True)
    mixed = attend(at, queries, keys, values)
    out_half = natural(out_half, s)
    w_out_all = by_core(out_half, pc(out_half), 1).reshape(HEADS * HD, width)
    wq_other = pc(w_qkv[:, :hw])
    w_out_mine = lax.dynamic_slice_in_dim(w_out_all, c * hw, hw, 0)
    w_out_other = lax.dynamic_slice_in_dim(w_out_all, (1 - c) * hw, hw, 0)
    mixed_there = pc(rows_of(mixed, 1 - c))
    x = in_order(x_near).reshape(own, width).astype(F32)
    attn_out = dot(rows_of(mixed, c), w_out_mine) + dot(mixed_there, w_out_other)
    r_x = inv_rms(x)
    r_ao = inv_rms(attn_out)
    residual = x + attn_out * r_ao * ga_out
    r_res = inv_rms(residual)
    nffn = (residual * r_res * gf_in).astype(BF)

    rows = gather4(nffn)
    gu = list(lax.optimization_barrier((*gu, mixed))[:-1])
    gu = collect(at, gu, [pc(g) for g in gu])
    acts = [None] * n_s
    before = None
    for k in ORDER:
        v = rows[k] if before is None else after(rows[k], before)
        acts[k] = ffn(v, gu, wd, F32 if k == 0 else BF)
        before = acts[k][3]
    branch = scatter4([a[3] for a in acts])
    r_b = inv_rms(branch)
    output = (residual + branch * r_b * gf_out).astype(BF)
    output = in_order(spread(output.reshape(tokens.shape)))

    zf = in_order(cot_near).reshape(own, width).astype(F32)
    gg_ffn_out = jnp.sum(zf * branch * r_b, axis=0)
    lows = gather4(rms_back(branch, r_b, gf_out, zf).astype(BF))
    backs = [None] * n_s
    before = None
    for k in ORDER:
        v = lows[k] if before is None else after(lows[k], before)
        if k == ORDER[1]:
            v = after(v, output)
        if k == ORDER[2]:
            down_mine, down_other = down_grad([after(a[2], before) for a in acts], lows, ff_own)
            gw_down = down_mine + pc(down_other)
            before = gw_down
            v = after(v, gw_down)
        backs[k] = ffn_back(v, gu, wd, acts[k][0], acts[k][1], F32 if k == 0 else BF)
        before = backs[k][1]
    hop_a, hop_b = scatter_first([b[1] for b in backs])
    sent = scatter_second([b[1] for b in backs], hop_a, hop_b)
    gw_down = lax.psum_scatter(gw_down, "z", scatter_dimension=0, tiled=True)
    gus = [after(b[0], *sent, gw_down) for b in backs]
    form = (n_z, n_s, d_own // n_z, ff_pad)
    up_mine, up_other = columns_grad(1, rows, gus, form)
    nffn_grad = scatter_last([after(backs[0][1], up_mine)], sent)
    gus = [after(g, up_mine, nffn_grad) for g in gus]
    gate_mine, gate_other = columns_grad(0, rows, gus, form)

    def scatter_z(v):
        v = lax.psum_scatter(v, "z", scatter_dimension=0, tiled=True)
        return lax.psum(v, "r") if n_r > 1 else v

    def pieces(v):
        v = v.reshape(2, n_s, -1, ff_pad)
        v = natural([pick(v, s, 1)] + [px(pick(v, s ^ k, 1), k) for k in range(1, n_s)], s)
        v = lax.all_gather(v.reshape(-1, ff_pad), "z", axis=0, tiled=True)
        return v.reshape(n_z, n_s, 2, -1, ff_pad)

    if n_r > 1:
        gw_down = lax.psum(gw_down, "r")
    gw_down = lax.all_gather(gw_down, "z", axis=0, tiled=True)
    gw_up = up_mine + pc(up_other)
    gw_gate = gate_mine + pc(gate_other)
    gw_gu = jnp.stack([gw_gate, gw_up], axis=1).reshape(-1, ff_pad)
    nffn_grad = after(nffn_grad, gw_gu)
    gw_gu = scatter_z(gw_gu)

    res_grad = zf + rms_back(residual, r_res, gf_in, nffn_grad)
    gg_ffn_in = jnp.sum(nffn_grad * residual * r_res, axis=0)
    gg_attn_out = jnp.sum(res_grad * attn_out * r_ao, axis=0)
    attn_grad = whole(rms_back(attn_out, r_ao, ga_out, res_grad).astype(BF))
    def to_shards(v):
        v = v.reshape(n_s, v.size // (n_s * v.shape[-1]), v.shape[-1])
        parts = [pick(v, s ^ k) for k in range(n_s)]
        return scatter4([parts[0].astype(F32)] + parts[1:]).astype(BF)

    gw_out = dot_rows(mixed, attn_grad).astype(BF).reshape(heads, 2, HD // 2, width)
    there = pc(pick(gw_out, 1 - c, 1))
    gw_out = to_shards(by_core(pick(gw_out, c, 1), there, 0))
    mixed_grad = dot_t(attn_grad, w_out_mine).astype(BF)
    q_low, k_grad, v_grad, gg_query = attend_back(
        at, queries, keys, values, mixed_grad, raw, gq, cos, sin
    )
    k_grad = k_grad + pc(k_grad.astype(BF)).astype(F32)
    v_grad = v_grad + pc(v_grad.astype(BF)).astype(F32)
    if n_r > 1:
        k_grad = lax.psum_scatter(k_grad.astype(BF), "r", scatter_dimension=0, tiled=True).astype(F32)
        v_grad = lax.psum_scatter(v_grad.astype(BF), "r", scatter_dimension=0, tiled=True).astype(F32)
    k_raw = raw[:, hw:]
    rk = inv_rms(k_raw)
    k_un = rope(k_grad, cos, -sin)
    gg_key = jnp.sum(rows_of(k_un * k_raw * rk, c), axis=0)
    k_low = rms_back(k_raw, rk, gk, k_un).astype(BF)
    v_low = v_grad.astype(BF)
    low_own = jnp.concatenate([rows_of(q_low, c), rows_of(k_low, c), rows_of(v_low, c)], axis=1)
    nin_grad = dot_t(low_own, w_qkv) + dot_t(pc(rows_of(q_low, 1 - c)), wq_other)
    gg_attn_in = jnp.sum(nin_grad * x * r_x, axis=0)
    input_grad = (res_grad + rms_back(x, r_x, ga_in, nin_grad)).astype(BF)

    low_mine = jnp.concatenate([q_low, jnp.where(c == 0, k_low, v_low)], axis=1)
    gw_qkv = dot_rows(nin, low_mine).astype(BF)
    cols = gw_qkv.shape[1]
    parts = [gg_attn_in, gg_attn_out, gg_ffn_in, gg_ffn_out, gg_query, gg_key]
    small = jnp.concatenate([p.reshape(n_s, -1) for p in parts], axis=1)
    count = small.shape[1]
    out_rows = gw_out.size // cols
    extra = -(-(d_own + out_rows + -(-count // cols)) // (16 * n_z)) * (16 * n_z) - d_own - out_rows
    small = jnp.pad(small, ((0, 0), (0, extra * cols - count))).reshape(n_s, extra, cols)
    gw_qkv = jnp.concatenate([gw_qkv.reshape(n_s, d_own, cols), small.astype(BF)], axis=1)
    parts = [pick(gw_qkv, s ^ k) for k in range(n_s)]
    parts[0] = parts[0].astype(F32)
    hop_a, hop_b = scatter_first(parts)
    sent = scatter_second(parts, hop_a, hop_b)
    gw_qkv = scatter_last(parts, sent).astype(BF)
    line = Line(jnp.concatenate([gw_qkv, gw_out.reshape(out_rows, cols)]))
    gw_gu = pieces(after(gw_gu, gw_qkv))
    line.middle(gw_qkv)
    line.last(gw_qkv)
    gw_attn = line.done(gw_qkv)
    input_grad = after(input_grad, gw_gu)
    input_grad = in_order(spread(input_grad.reshape(tokens.shape)))

    attn_there = pc(gw_attn)
    gw_qkv, qkv_there = gw_attn[: d_own + extra], attn_there[: d_own + extra]
    gw_out, out_there = (
        v[d_own + extra :].reshape(half_head, width) for v in (gw_attn, attn_there)
    )
    small = (gw_qkv[d_own:].astype(F32) + qkv_there[d_own:].astype(F32)).reshape(-1)
    small_out = []
    first = 0
    for size in [d_own] * 4 + [hd_own] * 2:
        small_out.append(small[first : first + size])
        first += size
    qkv_pair = by_core(gw_qkv[:d_own], qkv_there[:d_own], 0).astype(F32)
    gw_query = jnp.concatenate([qkv_pair[0][:, :hw], qkv_pair[1][:, :hw]], axis=1)
    gw_key, gw_value = qkv_pair[0][:, hw:], qkv_pair[1][:, hw:]
    gw_out = by_core(gw_out, out_there, 0).reshape(w_out.shape).astype(F32)
    gw_down = by_core(gw_down, pc(gw_down), 0).reshape(w_down.shape).astype(F32)
    gw_gate, gw_up = lay(at, gw_gu, pc(gw_gu), ff_own)
    return (
        output,
        input_grad,
        gw_query,
        gw_key,
        gw_value,
        gw_out,
        gw_gate,
        gw_up,
        gw_down,
        *small_out,
    )


def solution(mesh):
    n_s, n_c = mesh.shape["shard"], mesh.shape["ctx"]

    def run(*args):
        seqs = args[0].shape[0] // n_s
        groups = n_c // (2 * seqs)
        fine = Mesh(mesh.devices.reshape(n_s, groups, seqs, 2), ("shard", "r", "z", "c"))
        ctx = ("r", "z", "c")
        rows, mat, vec = P("shard", ctx, None), P("shard", None), P("shard")
        return jax.shard_map(
            body,
            mesh=fine,
            in_specs=(rows, rows, mat) + (mat,) * 7 + (vec,) * 6,
            out_specs=(rows, rows) + (mat,) * 7 + (vec,) * 6,
            check_vma=False,
        )(*args)

    return run
```

time: 779 us -> 696 us (0.89)
  waiting for transfers between devices: 292 us -> 226 us
  Pallas kernels: 227 us -> 200 us
  local copies, waits for them, and re-layouts: 65.4 us -> 74.6 us
    ppermute x35 -> x36, waiting for transfers between devices: 136 us -> 72.6 us  [px(): return lax.ppermute(v, 'shard', [(i, i ^ k) for i in range(n_s)])]
    ppermute x14 -> x12, waiting for transfers between devices: 88.3 us -> 48.2 us  [pz(): return lax.ppermute(v, 'z', [(i, i ^ k) for i in range(n_z)])]
    unnamed x176 -> x243, local copies, waits for them, and re-layouts: 13.4 us -> 31.6 us
    ppermute x6 -> x3, waiting for transfers between devices: 67 us -> 84.8 us  [the longest x1 55.5 us: last(): self.got = lax.ppermute(self.part, 'z', [(1, 0), (2, 3)])]
    pallas_call x14 -> x15, Pallas kernels: 192 us -> 175 us  [the longest x4 51.1 us: ffn_back(): call(ffn_back_kernel, (rows // tile,), [row, keep, keep, act, act], [pl.B...]
    ppermute x16 -> x19, waiting for transfers between devices: 0.32 us -> 10.4 us  [pc(): return lax.ppermute(v, 'c', [(0, 1), (1, 0)])]
    another operation x2 -> x5, other arithmetic: 11.6 us -> 1.58 us  [the longest x3 0.88 us: body(): gw_gu = jnp.stack([gw_gate, gw_up], axis=1).reshape(-1, ff_pad)]
    all_gather x1, waiting for transfers between devices: 0.02 us -> 7.82 us  [body(): w_qkv = lax.all_gather(qkv_mine, 'shard', axis=0, tiled=True)]
  transfers between devices with their start and end apart: 77 -> 75, of which waited for: 26 -> 29; matrix products, arithmetic and copies ran while one was open for 19% -> 18% of each run, Pallas kernels for 27% -> 24%
where the time goes in v3:
time: 696 us; the launch traced here: 688 us
  waiting for transfers between devices  226 us (32%)
  Pallas kernels  200 us (29%)
  other arithmetic  79.5 us (11%)
  local copies, waits for them, and re-layouts  74.6 us (11%)
  starting transfers between devices  72.9 us (10%)
  matrix products  18.2 us (3%)
  between operations  15.8 us (2%)
    ppermute x36, waiting for transfers between devices, px(): return lax.ppermute(v, 'shard', [(i, i ^ k) for i in range(n_s)])  72.6 us
    ppermute x1, waiting for transfers between devices, last(): self.got = lax.ppermute(self.part, 'z', [(1, 0), (2, 3)])  55.5 us
    pallas_call x4, Pallas kernels, ffn_back(): call(ffn_back_kernel, (rows // tile,), [row, keep, keep, act, act], [pl.B...  51.1 us
    pallas_call x4, Pallas kernels, ffn(): call(ffn_kernel, (rows // tile,), [row, keep, keep], [act, act, act, row]...  49 us
    ppermute x12, waiting for transfers between devices, pz(): return lax.ppermute(v, 'z', [(i, i ^ k) for i in range(n_z)])  48.2 us
    ppermute x36, starting transfers between devices, px(): return lax.ppermute(v, 'shard', [(i, i ^ k) for i in range(n_s)])  39.8 us
    pallas_call x2, Pallas kernels, columns_grad(): call(functools.partial(columns_grad_kernel, n), (1,), [full((rows, width)...  32 us
    unnamed x243, local copies, waits for them, and re-layouts  31.6 us
  transfers between devices with their start and end apart: 75, of which 29 were waited for; matrix products, arithmetic and copies ran while one was open for 18% of the time, Pallas kernels for 24%

profile of v3, /device:TPU:0, one launch (start us, length us, event | category | flops | bytes accessed | tf_op | source)
XLA Modules:
  0.0 687.5 jit_solution(17619575269178079558)
XLA Ops:
  19.3 7.3 %collective-permute-done = bf16[128,1152]{1,0:T(8,128)(2,1)S(1)} collective-permute-done((bf16[128,1152]{1,0:T(8,128)(2,1)S(1)}, bf16[128,1152]{1,0:T(8,128)(2,1)S(1)}, u32[]{:S(2)}, u32[]{:S(2)}) %collective-permute-start) | collective-permute-done | bytes 294944 | tf_op jit(solution)/shard_map/ppermute | solution.py:460
  30.1 4.7 constant_dynamic-slice_fusion.23
  38.4 3.2 multiply_sine_fusion
  42.9 7.8 %all-gather.4.cloned.1.call-done.w = bf16[1152,1024]{1,0:T(8,128)(2,1)} async-done(((bf16[288,1024]{1,0:T(8,128)(2,1)}), bf16[1152,1024]{1,0:T(8,128)(2,1)}) %all-gather.4.cloned.1.call-update) | async-done | bytes 2359312 | tf_op jit(solution)/shard_map/all_gather | solution.py:535
  56.3 4.5 shard_map.271.wd
  61.6 5.7 collective-permute-done.8
  81.4 9.4 %shard_map.272 = (bf16[1024,1152]{1,0:T(8,128)(2,1)}, f32[1024,768]{1,0:T(8,128)}, bf16[1024,512]{1,0:T(8,128)(2,1)}, bf16[1024,256]{1,0:T(8,128)(2,1)}, bf16[1024,256]{1,0:T(8,128)(2,1)}) custom-call(s32[6]{0:T(128)} %concatenate.62.at, bf16[4,128,1152]{2,1,0:T(8,128)(2,1)} %copy-done.53, bf16[4,128,1152]{2,1,0:T(8,128)(2,1)} %collective-permute-done.3.oth, ...), custom_call_target="tpu_custom_call" | custom-call | flops 2415919104 | bytes 11796480 | tf_op jit(solution)/shard_map/pallas_call | solution.py:108
  90.8 10.6 %shard_map.273 = bf16[1024,512]{1,0:T(8,128)(2,1)} custom-call(s32[6]{0:T(128)} %concatenate.62.at, bf16[1024,512]{1,0:T(8,128)(2,1)} %get-tuple-element.102.q, bf16[1024,256]{1,0:T(8,128)(2,1)} %get-tuple-element.103.k, bf16[1024,256]{1,0:T(8,128)(2,1)} %get-tuple-element.104.v), custom_call_target="tpu_custom_call" | custom-call | flops 2147483648 | bytes 3145728 | tf_op jit(solution)/shard_map/pallas_call | solution.py:162
  102.9 15.4 %collective-permute-done.13.refs_2_ = bf16[2,288,896]{2,1,0:T(8,128)(2,1)} collective-permute-done((bf16[2,288,896]{2,1,0:T(8,128)(2,1)}, bf16[2,288,896]{2,1,0:T(8,128)(2,1)}, u32[]{:S(2)}, u32[]{:S(2)}) %collective-permute-start.13) | collective-permute-done | bytes 1032224 | tf_op jit(solution)/shard_map/ppermute | solution.py:457
  130.3 3.3 copy-done.2
  133.6 12.2 %shard_map.275 = (bf16[512,1792]{1,0:T(8,128)(2,1)S(1)}, bf16[512,1792]{1,0:T(8,128)(2,1)S(1)}, bf16[512,1792]{1,0:T(8,128)(2,1)S(1)}, f32[512,1152]{1,0:T(8,128)S(1)}) custom-call(bf16[512,1152]{1,0:T(8,128)(2,1)S(1)} %multiply_convert_fusion.x.refs_0_, bf16[2,1152,1792]{2,1,0:T(8,128)(2,1)} %copy-done.2, bf16[1792,1152]{1,0:T(8,128)(2,1)S(1)} %copy-done.3), custom_call_target="tpu_custom_call" | custom-call | flops 6341787648 | bytes 20250624 | tf_op jit(solution)/shard_map/pallas_call | solution.py:249
  147.0 6.4 collective-permute-done.19.x.refs_1_
  155.7 12.0 %shard_map.276 = (bf16[512,1792]{1,0:T(8,128)(2,1)S(1)}, bf16[512,1792]{1,0:T(8,128)(2,1)S(1)}, bf16[512,1792]{1,0:T(8,128)(2,1)S(1)}, bf16[512,1152]{1,0:T(8,128)(2,1)S(1)}) custom-call(bf16[512,1152]{1,0:T(8,128)(2,1)S(1)} %collective-permute-done.19.x.refs_1_, bf16[2,1152,1792]{2,1,0:T(8,128)(2,1)} %copy-done.2, bf16[1792,1152]{1,0:T(8,128)(2,1)S(1)} %copy-done.3), custom_call_target="tpu_custom_call" | custom-call | flops 6341787648 | bytes 20250624 | tf_op jit(solution)/shard_map/pallas_call | solution.py:249
  170.2 12.4 %shard_map.277 = (bf16[512,1792]{1,0:T(8,128)(2,1)S(1)}, bf16[512,1792]{1,0:T(8,128)(2,1)S(1)}, bf16[512,1792]{1,0:T(8,128)(2,1)S(1)}, bf16[512,1152]{1,0:T(8,128)(2,1)S(1)}) custom-call(bf16[512,1152]{1,0:T(8,128)(2,1)S(1)} %constant_dynamic-update-slice_fusion.x.refs_3_, bf16[2,1152,1792]{2,1,0:T(8,128)(2,1)} %copy-done.2, bf16[1792,1152]{1,0:T(8,128)(2,1)S(1)} %copy-done.3), custom_call_target="tpu_custom_call" | custom-call | flops 6341787648 | bytes 20250624 | tf_op jit(solution)/shard_map/pallas_call | solution.py:249
  186.6 12.4 %shard_map.278 = (bf16[512,1792]{1,0:T(8,128)(2,1)S(1)}, bf16[512,1792]{1,0:T(8,128)(2,1)S(1)}, bf16[512,1792]{1,0:T(8,128)(2,1)S(1)}, bf16[512,1152]{1,0:T(8,128)(2,1)S(1)}) custom-call(bf16[512,1152]{1,0:T(8,128)(2,1)S(1)} %collective-permute-done.21.x.refs_2_, bf16[2,1152,1792]{2,1,0:T(8,128)(2,1)} %copy-done.2, bf16[1792,1152]{1,0:T(8,128)(2,1)S(1)} %copy-done.3), custom_call_target="tpu_custom_call" | custom-call | flops 6341787648 | bytes 20250624 | tf_op jit(solution)/shard_map/pallas_call | solution.py:249
  212.5 5.5 collective-permute-done.30
  218.0 13.5 %collective-permute-done.31 = bf16[128,1152]{1,0:T(8,128)(2,1)S(1)} collective-permute-done((bf16[128,1152]{1,0:T(8,128)(2,1)}, bf16[128,1152]{1,0:T(8,128)(2,1)S(1)}, u32[]{:S(2)}, u32[]{:S(2)}) %collective-permute-start.31) | collective-permute-done | bytes 294944 | tf_op jit(solution)/shard_map/ppermute | solution.py:460
  239.3 3.8 collective-permute-start.27
  245.6 13.5 %shard_map.279 = (bf16[2,512,1792]{2,1,0:T(8,128)(2,1)S(1)}, f32[512,1152]{1,0:T(8,128)S(1)}) custom-call(bf16[512,1152]{1,0:T(8,128)(2,1)S(1)} %get-tuple-element.209.z.refs_4_, bf16[2,1152,1792]{2,1,0:T(8,128)(2,1)} %copy-done.2, bf16[1792,1152]{1,0:T(8,128)(2,1)} %shard_map.271.wd, bf16[512,1792]{1,0:T(8,128)(2,1)S(1)} %copy-done.34, ...), custom_call_target="tpu_custom_call" | custom-call | flops 6341787648 | bytes 20250624 | tf_op jit(solution)/shard_map/pallas_call | solution.py:277
  259.1 5.9 collective-permute-done.28
  269.6 12.3 %shard_map.280 = (bf16[2,512,1792]{2,1,0:T(8,128)(2,1)S(1)}, bf16[512,1152]{1,0:T(8,128)(2,1)S(1)}) custom-call(bf16[512,1152]{1,0:T(8,128)(2,1)S(1)} %collective-permute-done.33.z.refs_5_, bf16[2,1152,1792]{2,1,0:T(8,128)(2,1)} %copy-done.2, bf16[1792,1152]{1,0:T(8,128)(2,1)S(1)} %copy-done.4, bf16[512,1792]{1,0:T(8,128)(2,1)S(1)} %copy-done.30, ...), custom_call_target="tpu_custom_call" | custom-call | flops 6341787648 | bytes 20250624 | tf_op jit(solution)/shard_map/pallas_call | solution.py:277
  284.9 15.5 %shard_map.281 = (bf16[864,1152]{1,0:T(8,128)(2,1)}, bf16[864,1152]{1,0:T(8,128)(2,1)}) custom-call(bf16[512,1792]{1,0:T(8,128)(2,1)} %copy-done.37, bf16[512,1792]{1,0:T(8,128)(2,1)} %copy-done.38, bf16[512,1792]{1,0:T(8,128)(2,1)} %copy-done.40, bf16[512,1792]{1,0:T(8,128)(2,1)} %copy-done.39, bf16[512,1152]{1,0:T(8,128)(2,1)} %copy-done.6, ...), custom_call_target="tpu_custom_call" | custom-call | flops 8455716864 | bytes 16187392 | tf_op jit(solution)/shard_map/pallas_call | solution.py:337
  300.4 4.2 collective-permute-done.37
  304.6 3.3 add.356
  314.5 12.7 %shard_map.282 = (bf16[2,512,1792]{2,1,0:T(8,128)(2,1)S(1)}, bf16[512,1152]{1,0:T(8,128)(2,1)S(1)}) custom-call(bf16[512,1152]{1,0:T(8,128)(2,1)S(1)} %copy-done.15, bf16[2,1152,1792]{2,1,0:T(8,128)(2,1)} %copy-done.2, bf16[1792,1152]{1,0:T(8,128)(2,1)S(1)} %copy-done.5, bf16[512,1792]{1,0:T(8,128)(2,1)S(1)} %copy-done.26, bf16[512,1792]{1,0:T(8,128)(2,1)S(1)} %copy-done.28), custom_call_target="tpu_custom_call" | custom-call | flops 6341787648 | bytes 20250624 | tf_op jit(solution)/shard_map/pallas_call | solution.py:277
  331.2 12.6 %shard_map.283 = (bf16[2,512,1792]{2,1,0:T(8,128)(2,1)S(1)}, bf16[512,1152]{1,0:T(8,128)(2,1)S(1)}) custom-call(bf16[512,1152]{1,0:T(8,128)(2,1)S(1)} %copy-done.11, bf16[2,1152,1792]{2,1,0:T(8,128)(2,1)} %copy-done.2, bf16[1792,1152]{1,0:T(8,128)(2,1)S(1)} %copy-done.5, bf16[512,1792]{1,0:T(8,128)(2,1)S(1)} %copy-done.22, bf16[512,1792]{1,0:T(8,128)(2,1)S(1)} %copy-done.24), custom_call_target="tpu_custom_call" | custom-call | flops 6341787648 | bytes 20250624 | tf_op jit(solution)/shard_map/pallas_call | solution.py:277
  351.7 15.9 %shard_map.284 = (bf16[4,4,72,896]{3,2,1,0:T(8,128)(2,1)}, bf16[4,4,72,896]{3,2,1,0:T(8,128)(2,1)}) custom-call(bf16[512,1152]{1,0:T(8,128)(2,1)} %copy-done.7, bf16[512,1152]{1,0:T(8,128)(2,1)} %copy-done.8, bf16[512,1152]{1,0:T(8,128)(2,1)} %copy-done.9, bf16[512,1152]{1,0:T(8,128)(2,1)} %copy-done.13, bf16[2,512,1792]{2,1,0:T(8,128)(2,1)} %copy-done.17, ...), custom_call_target="tpu_custom_call" | custom-call | flops 8455716864 | bytes 16187392 | tf_op jit(solution)/shard_map/pallas_call | solution.py:310
  367.6 6.1 collective-permute-done.40
  378.8 16.1 %shard_map.285 = (bf16[4,4,72,896]{3,2,1,0:T(8,128)(2,1)}, bf16[4,4,72,896]{3,2,1,0:T(8,128)(2,1)}) custom-call(bf16[512,1152]{1,0:T(8,128)(2,1)} %copy-done.7, bf16[512,1152]{1,0:T(8,128)(2,1)} %copy-done.8, bf16[512,1152]{1,0:T(8,128)(2,1)} %copy-done.9, bf16[512,1152]{1,0:T(8,128)(2,1)} %copy-done.13, bf16[2,512,1792]{2,1,0:T(8,128)(2,1)} %copy-done.17, ...), custom_call_target="tpu_custom_call" | custom-call | flops 8455716864 | bytes 16187392 | tf_op jit(solution)/shard_map/pallas_call | solution.py:310
  395.5 3.7 collective-permute-done.42
  418.0 14.8 %shard_map.286 = (bf16[1024,512]{1,0:T(8,128)(2,1)}, f32[1024,256]{1,0:T(8,128)}, f32[1024,256]{1,0:T(8,128)}, f32[1,256]{1,0:T(1,128)}) custom-call(s32[6]{0:T(128)} %concatenate.62.at, bf16[1024,512]{1,0:T(8,128)(2,1)} %get-tuple-element.102.q, bf16[1024,256]{1,0:T(8,128)(2,1)} %get-tuple-element.103.k, bf16[1024,256]{1,0:T(8,128)(2,1)} %get-tuple-element.104.v, ...), custom_call_target="tpu_custom_call" | custom-call | flops 5368709120 | bytes 9437184 | tf_op jit(solution)/shard_map/pallas_call | solution.py:213
  459.1 3.5 fusion.18
  462.7 4.6 fusion.13
  469.0 4.1 convolution_convert_fusion
  475.4 6.1 collective-permute-done.49
  485.4 9.0 %collective-permute-done.50 = bf16[320,768]{1,0:T(8,128)(2,1)S(1)} collective-permute-done((bf16[320,768]{1,0:T(8,128)(2,1)S(1)}, bf16[320,768]{1,0:T(8,128)(2,1)S(1)}, u32[]{:S(2)}, u32[]{:S(2)}) %collective-permute-start.50) | collective-permute-done | bytes 491552 | tf_op jit(solution)/shard_map/ppermute | solution.py:457
  501.1 5.6 collective-permute-done.53
  506.8 3.8 collective-permute-done.54
  515.6 3.2 collective-permute-done.60
  523.1 4.5 collective-permute-done.61
  532.0 6.2 collective-permute-start.64
  538.2 29.4 %collective-permute-done.64 = bf16[512,768]{1,0:T(8,128)(2,1)} collective-permute-done((bf16[512,768]{1,0:T(8,128)(2,1)}, bf16[512,768]{1,0:T(8,128)(2,1)}, u32[]{:S(2)}, u32[]{:S(2)}) %collective-permute-start.64) | collective-permute-done | bytes 786464 | tf_op jit(solution)/shard_map/ppermute | solution.py:505
  570.9 3.2 fusion.11
  580.2 55.5 %collective-permute-done.66 = bf16[512,768]{1,0:T(8,128)(2,1)S(1)} collective-permute-done((bf16[512,768]{1,0:T(8,128)(2,1)S(1)}, bf16[512,768]{1,0:T(8,128)(2,1)S(1)}, u32[]{:S(2)}, u32[]{:S(2)}) %collective-permute-start.66) | collective-permute-done | bytes 786464 | tf_op jit(solution)/shard_map/ppermute | solution.py:515
  636.3 5.9 bitcast_convert_fusion
  652.7 5.9 collective-permute-done.56
  658.6 10.0 %collective-permute-done.57 = bf16[128,1152]{1,0:T(8,128)(2,1)S(1)} collective-permute-done((bf16[128,1152]{1,0:T(8,128)(2,1)S(1)}, bf16[128,1152]{1,0:T(8,128)(2,1)S(1)}, u32[]{:S(2)}, u32[]{:S(2)}) %collective-permute-start.57) | collective-permute-done | bytes 294944 | tf_op jit(solution)/shard_map/ppermute | solution.py:460
  670.1 10.7 %shard_map.287 = (f32[288,6912]{1,0:T(8,128)}, f32[288,6912]{1,0:T(8,128)}) custom-call(s32[6]{0:T(128)} %concatenate.62.at, bf16[4,4,2,72,896]{4,3,2,1,0:T(8,128)(2,1)} %bitcast.241, bf16[4,4,2,72,896]{4,3,2,1,0:T(8,128)(2,1)} %collective-permute-done.68.oth), custom_call_target="tpu_custom_call" | custom-call | bytes 23887872 | tf_op jit(solution)/shard_map/pallas_call | solution.py:409
  (545 shorter events, 213.7 us)
Async XLA Ops:
  7.2 43.5 %all-gather.4.cloned.1.call-start = ((), (), s32[]{:S(2)}) async-start(), calls=%async_computation.2 | async-start | bytes 2949120 | tf_op jit(solution)/shard_map/all_gather | solution.py:535
  10.2 341.5 %reduce-scatter.7.cloned.1.call-start = ((), (), s32[]{:S(2)}) async-start(), calls=%async_computation.6 | async-start | bytes 2488320
  11.1 15.5 %collective-permute-start = (bf16[128,1152]{1,0:T(8,128)(2,1)S(1)}, bf16[128,1152]{1,0:T(8,128)(2,1)S(1)}, u32[]{:S(2)}, u32[]{:S(2)}) collective-permute-start(bf16[128,1152]{1,0:T(8,128)(2,1)S(1)} %get-tuple-element.277), channel_id=1, source_target_pairs={{0,2},{2,0},{4,6},{6,4},{1,3},{3,1},{5,7},{7,5},{8,10},{10,8},{12,... | collective-permute-start | bytes 884744 | tf_op jit(solution)/shard_map/ppermute | solution.py:460
  14.2 27.5 %collective-permute-start.1 = (bf16[128,1152]{1,0:T(8,128)(2,1)}, bf16[128,1152]{1,0:T(8,128)(2,1)S(1)}, u32[]{:S(2)}, u32[]{:S(2)}) collective-permute-start(bf16[128,1152]{1,0:T(8,128)(2,1)} %get-tuple-element.279), channel_id=1, source_target_pairs={{0,4},{2,6},{4,0},{6,2},{1,5},{3,7},{5,1},{7,3},{8,12},{10,14},{12... | collective-permute-start | bytes 884744 | tf_op jit(solution)/shard_map/ppermute | solution.py:460
  16.7 24.9 %collective-permute-start.2 = (bf16[128,1152]{1,0:T(8,128)(2,1)S(1)}, bf16[128,1152]{1,0:T(8,128)(2,1)S(1)}, u32[]{:S(2)}, u32[]{:S(2)}) collective-permute-start(bf16[128,1152]{1,0:T(8,128)(2,1)S(1)} %get-tuple-element.278), channel_id=1, source_target_pairs={{0,6},{2,4},{4,2},{6,0},{1,7},{3,5},{5,3},{7,1},{8,14},{10,12},{12... | collective-permute-start | bytes 884744 | tf_op jit(solution)/shard_map/ppermute | solution.py:460
  26.6 26.2 %collective-permute-start.4 = (f32[1280]{0:T(1024)S(1)}, f32[1280]{0:T(1024)S(1)}, u32[]{:S(2)}, u32[]{:S(2)}) collective-permute-start(f32[1280]{0:T(1024)S(1)} %concatenate.61), channel_id=1, source_target_pairs={{0,8},{8,0},{16,24},{24,16},{1,9},{9,1},{17,25},{25,17},{2,10},{10... | collective-permute-start | bytes 15368 | tf_op jit(solution)/shard_map/ppermute | solution.py:457
  28.3 32.5 %collective-permute-start.5 = (f32[1280]{0:T(1024)S(1)}, f32[1280]{0:T(1024)}, u32[]{:S(2)}, u32[]{:S(2)}) collective-permute-start(f32[1280]{0:T(1024)S(1)} %concatenate.61), channel_id=1, source_target_pairs={{0,16},{8,24},{16,0},{24,8},{1,17},{9,25},{17,1},{25,9},{2,18},{10... | collective-permute-start | bytes 15368 | tf_op jit(solution)/shard_map/ppermute | solution.py:457
  29.8 31.8 %collective-permute-start.6 = (f32[1280]{0:T(1024)S(1)}, f32[1280]{0:T(1024)S(1)}, u32[]{:S(2)}, u32[]{:S(2)}) collective-permute-start(f32[1280]{0:T(1024)S(1)} %concatenate.61), channel_id=1, source_target_pairs={{0,24},{8,16},{16,8},{24,0},{1,25},{9,17},{17,9},{25,1},{2,26},{10... | collective-permute-start | bytes 15368 | tf_op jit(solution)/shard_map/ppermute | solution.py:457
  52.2 15.1 %collective-permute-start.8 = (bf16[128,1152]{1,0:T(8,128)(2,1)}, bf16[128,1152]{1,0:T(8,128)(2,1)}, u32[]{:S(2)}, u32[]{:S(2)}) collective-permute-start(bf16[128,1152]{1,0:T(8,128)(2,1)} %constant_dynamic-slice_fusion.36), channel_id=1, source_target_pairs={{0,16},{8,24},{16,0},{24,8},{1,17},{9,25},{17,1},{25,9},{2,18},{10... | collective-permute-start | bytes 884744 | tf_op jit(solution)/shard_map/ppermute | solution.py:457
  60.8 20.6 %collective-permute-start.3 = (bf16[4,128,1152]{2,1,0:T(8,128)(2,1)S(1)}, bf16[4,128,1152]{2,1,0:T(8,128)(2,1)}, u32[]{:S(2)}, u32[]{:S(2)}) collective-permute-start(bf16[4,128,1152]{2,1,0:T(8,128)(2,1)S(1)} %pad_maximum_fusion.4.own), channel_id=1, source_target_pairs={{0,1},{1,0},{2,3},{3,2},{4,5},{5,4},{6,7},{7,6},{8,9},{9,8},{10,11... | collective-permute-start | bytes 3538952 | tf_op jit(solution)/shard_map/ppermute | solution.py:463
  70.2 48.6 %collective-permute-start.10 = (bf16[4,128,1152]{2,1,0:T(8,128)(2,1)}, bf16[4,128,1152]{2,1,0:T(8,128)(2,1)}, u32[]{:S(2)}, u32[]{:S(2)}) collective-permute-start(bf16[4,128,1152]{2,1,0:T(8,128)(2,1)} %pad_maximum_fusion.7), channel_id=1, source_target_pairs={{0,1},{1,0},{2,3},{3,2},{4,5},{5,4},{6,7},{7,6},{8,9},{9,8},{10,11... | collective-permute-start | bytes 3538952 | tf_op jit(solution)/shard_map/ppermute | solution.py:463
  70.3 32.5 %collective-permute-start.12 = (bf16[2,288,896]{2,1,0:T(8,128)(2,1)}, bf16[2,288,896]{2,1,0:T(8,128)(2,1)S(1)}, u32[]{:S(2)}, u32[]{:S(2)}) collective-permute-start(bf16[2,288,896]{2,1,0:T(8,128)(2,1)} %pad_maximum_fusion.22), channel_id=1, source_target_pairs={{0,8},{8,0},{16,24},{24,16},{1,9},{9,1},{17,25},{25,17},{2,10},{10... | collective-permute-start | bytes 3096584 | tf_op jit(solution)/shard_map/ppermute | solution.py:457
  71.0 47.4 %collective-permute-start.13 = (bf16[2,288,896]{2,1,0:T(8,128)(2,1)}, bf16[2,288,896]{2,1,0:T(8,128)(2,1)}, u32[]{:S(2)}, u32[]{:S(2)}) collective-permute-start(bf16[2,288,896]{2,1,0:T(8,128)(2,1)} %pad_maximum_fusion.23), channel_id=1, source_target_pairs={{0,16},{8,24},{16,0},{24,8},{1,17},{9,25},{17,1},{25,9},{2,18},{10... | collective-permute-start | bytes 3096584 | tf_op jit(solution)/shard_map/ppermute | solution.py:457
  72.4 45.9 %collective-permute-start.14 = (bf16[2,288,896]{2,1,0:T(8,128)(2,1)}, bf16[2,288,896]{2,1,0:T(8,128)(2,1)}, u32[]{:S(2)}, u32[]{:S(2)}) collective-permute-start(bf16[2,288,896]{2,1,0:T(8,128)(2,1)} %pad_maximum_fusion.24), channel_id=1, source_target_pairs={{0,24},{8,16},{16,8},{24,0},{1,25},{9,17},{17,9},{25,1},{2,26},{10... | collective-permute-start | bytes 3096584 | tf_op jit(solution)/shard_map/ppermute | solution.py:457
  102.8 19.3 %collective-permute-start.11 = (bf16[512,512]{1,0:T(8,128)(2,1)S(1)}, bf16[512,512]{1,0:T(8,128)(2,1)S(1)}, u32[]{:S(2)}, u32[]{:S(2)}) collective-permute-start(bf16[512,512]{1,0:T(8,128)(2,1)S(1)} %bitcast.253), channel_id=1, source_target_pairs={{0,1},{1,0},{2,3},{3,2},{4,5},{5,4},{6,7},{7,6},{8,9},{9,8},{10,11... | collective-permute-start | bytes 1572872 | tf_op jit(solution)/shard_map/ppermute | solution.py:463
  125.5 28.0 %collective-permute-start.19 = (bf16[512,1152]{1,0:T(8,128)(2,1)S(1)}, bf16[512,1152]{1,0:T(8,128)(2,1)S(1)}, u32[]{:S(2)}, u32[]{:S(2)}) collective-permute-start(bf16[512,1152]{1,0:T(8,128)(2,1)S(1)} %multiply_convert_fusion.x.refs_0_), channel_id=1, source_target_pairs={{0,8},{8,0},{16,24},{24,16},{1,9},{9,1},{17,25},{25,17},{2,10},{10... | collective-permute-start | bytes 3538952 | tf_op jit(solution)/shard_map/ppermute | solution.py:457
  127.0 28.0 %collective-permute-start.21 = (bf16[512,1152]{1,0:T(8,128)(2,1)S(1)}, bf16[512,1152]{1,0:T(8,128)(2,1)S(1)}, u32[]{:S(2)}, u32[]{:S(2)}) collective-permute-start(bf16[512,1152]{1,0:T(8,128)(2,1)S(1)} %multiply_convert_fusion.x.refs_0_), channel_id=1, source_target_pairs={{0,16},{8,24},{16,0},{24,8},{1,17},{9,25},{17,1},{25,9},{2,18},{10... | collective-permute-start | bytes 3538952 | tf_op jit(solution)/shard_map/ppermute | solution.py:457
  153.5 15.6 %collective-permute-start.20 = (bf16[256,1152]{1,0:T(8,128)(2,1)S(1)}, bf16[256,1152]{1,0:T(8,128)(2,1)S(1)}, u32[]{:S(2)}, u32[]{:S(2)}) collective-permute-start(bf16[256,1152]{1,0:T(8,128)(2,1)S(1)} %slice.283), channel_id=1, source_target_pairs={{0,16},{8,24},{16,0},{24,8},{1,17},{9,25},{17,1},{25,9},{2,18},{10... | collective-permute-start | bytes 1769480 | tf_op jit(solution)/shard_map/ppermute | solution.py:457
  155.1 14.2 %collective-permute-start.22 = (bf16[256,1152]{1,0:T(8,128)(2,1)S(1)}, bf16[256,1152]{1,0:T(8,128)(2,1)S(1)}, u32[]{:S(2)}, u32[]{:S(2)}) collective-permute-start(bf16[256,1152]{1,0:T(8,128)(2,1)S(1)} %slice.284), channel_id=1, source_target_pairs={{0,8},{8,0},{16,24},{24,16},{1,9},{9,1},{17,25},{25,17},{2,10},{10... | collective-permute-start | bytes 1769480 | tf_op jit(solution)/shard_map/ppermute | solution.py:457
  184.0 16.3 %collective-permute-start.23 = (bf16[256,1152]{1,0:T(8,128)(2,1)S(1)}, bf16[256,1152]{1,0:T(8,128)(2,1)S(1)}, u32[]{:S(2)}, u32[]{:S(2)}) collective-permute-start(bf16[256,1152]{1,0:T(8,128)(2,1)S(1)} %get-tuple-element.264), channel_id=1, source_target_pairs={{0,16},{8,24},{16,0},{24,8},{1,17},{9,25},{17,1},{25,9},{2,18},{10... | collective-permute-start | bytes 1769480 | tf_op jit(solution)/shard_map/ppermute | solution.py:457
  185.6 18.0 %collective-permute-start.25 = (bf16[256,1152]{1,0:T(8,128)(2,1)S(1)}, bf16[256,1152]{1,0:T(8,128)(2,1)S(1)}, u32[]{:S(2)}, u32[]{:S(2)}) collective-permute-start(bf16[256,1152]{1,0:T(8,128)(2,1)S(1)} %get-tuple-element.265), channel_id=1, source_target_pairs={{0,8},{8,0},{16,24},{24,16},{1,9},{9,1},{17,25},{25,17},{2,10},{10... | collective-permute-start | bytes 1769480 | tf_op jit(solution)/shard_map/ppermute | solution.py:457
  202.5 29.6 %collective-permute-start.24 = (bf16[512,1152]{1,0:T(8,128)(2,1)}, bf16[512,1152]{1,0:T(8,128)(2,1)}, u32[]{:S(2)}, u32[]{:S(2)}) collective-permute-start(bf16[512,1152]{1,0:T(8,128)(2,1)} %pad_maximum_fusion.8), channel_id=1, source_target_pairs={{0,8},{8,0},{16,24},{24,16},{1,9},{9,1},{17,25},{25,17},{2,10},{10... | collective-permute-start | bytes 3538952 | tf_op jit(solution)/shard_map/ppermute | solution.py:457
  204.8 27.4 %collective-permute-start.26 = (bf16[512,1152]{1,0:T(8,128)(2,1)}, bf16[512,1152]{1,0:T(8,128)(2,1)}, u32[]{:S(2)}, u32[]{:S(2)}) collective-permute-start(bf16[512,1152]{1,0:T(8,128)(2,1)} %pad_maximum_fusion.9), channel_id=1, source_target_pairs={{0,16},{8,24},{16,0},{24,8},{1,17},{9,25},{17,1},{25,9},{2,18},{10... | collective-permute-start | bytes 3538952 | tf_op jit(solution)/shard_map/ppermute | solution.py:457
  208.2 23.4 %collective-permute-start.31 = (bf16[128,1152]{1,0:T(8,128)(2,1)}, bf16[128,1152]{1,0:T(8,128)(2,1)S(1)}, u32[]{:S(2)}, u32[]{:S(2)}) collective-permute-start(bf16[128,1152]{1,0:T(8,128)(2,1)} %get-tuple-element.252), channel_id=1, source_target_pairs={{0,4},{2,6},{4,0},{6,2},{1,5},{3,7},{5,1},{7,3},{8,12},{10,14},{12... | collective-permute-start | bytes 884744 | tf_op jit(solution)/shard_map/ppermute | solution.py:460
  210.6 21.0 %collective-permute-start.32 = (bf16[128,1152]{1,0:T(8,128)(2,1)}, bf16[128,1152]{1,0:T(8,128)(2,1)S(1)}, u32[]{:S(2)}, u32[]{:S(2)}) collective-permute-start(bf16[128,1152]{1,0:T(8,128)(2,1)} %get-tuple-element.251), channel_id=1, source_target_pairs={{0,6},{2,4},{4,2},{6,0},{1,7},{3,5},{5,3},{7,1},{8,14},{10,12},{12... | collective-permute-start | bytes 884744 | tf_op jit(solution)/shard_map/ppermute | solution.py:460
  237.1 29.3 %collective-permute-start.33 = (bf16[512,1152]{1,0:T(8,128)(2,1)S(1)}, bf16[512,1152]{1,0:T(8,128)(2,1)S(1)}, u32[]{:S(2)}, u32[]{:S(2)}) collective-permute-start(bf16[512,1152]{1,0:T(8,128)(2,1)S(1)} %get-tuple-element.209.z.refs_4_), channel_id=1, source_target_pairs={{0,8},{8,0},{16,24},{24,16},{1,9},{9,1},{17,25},{25,17},{2,10},{10... | collective-permute-start | bytes 3538952 | tf_op jit(solution)/shard_map/ppermute | solution.py:457
  238.1 29.5 %collective-permute-start.35 = (bf16[512,1152]{1,0:T(8,128)(2,1)S(1)}, bf16[512,1152]{1,0:T(8,128)(2,1)S(1)}, u32[]{:S(2)}, u32[]{:S(2)}) collective-permute-start(bf16[512,1152]{1,0:T(8,128)(2,1)S(1)} %get-tuple-element.209.z.refs_4_), channel_id=1, source_target_pairs={{0,16},{8,24},{16,0},{24,8},{1,17},{9,25},{17,1},{25,9},{2,18},{10... | collective-permute-start | bytes 3538952 | tf_op jit(solution)/shard_map/ppermute | solution.py:457
  239.3 19.7 %collective-permute-start.27 = (bf16[128,1152]{1,0:T(8,128)(2,1)S(1)}, bf16[128,1152]{1,0:T(8,128)(2,1)S(1)}, u32[]{:S(2)}, u32[]{:S(2)}) collective-permute-start(bf16[128,1152]{1,0:T(8,128)(2,1)S(1)} %get-tuple-element.261), channel_id=1, source_target_pairs={{0,2},{2,0},{4,6},{6,4},{1,3},{3,1},{5,7},{7,5},{8,10},{10,8},{12,... | collective-permute-start | bytes 884744 | tf_op jit(solution)/shard_map/ppermute | solution.py:460
  243.1 21.8 %collective-permute-start.28 = (bf16[128,1152]{1,0:T(8,128)(2,1)S(1)}, bf16[128,1152]{1,0:T(8,128)(2,1)S(1)}, u32[]{:S(2)}, u32[]{:S(2)}) collective-permute-start(bf16[128,1152]{1,0:T(8,128)(2,1)S(1)} %get-tuple-element.260), channel_id=1, source_target_pairs={{0,4},{2,6},{4,0},{6,2},{1,5},{3,7},{5,1},{7,3},{8,12},{10,14},{12... | collective-permute-start | bytes 884744 | tf_op jit(solution)/shard_map/ppermute | solution.py:460
  244.1 20.8 %collective-permute-start.29 = (bf16[128,1152]{1,0:T(8,128)(2,1)S(1)}, bf16[128,1152]{1,0:T(8,128)(2,1)S(1)}, u32[]{:S(2)}, u32[]{:S(2)}) collective-permute-start(bf16[128,1152]{1,0:T(8,128)(2,1)S(1)} %get-tuple-element.259), channel_id=1, source_target_pairs={{0,6},{2,4},{4,2},{6,0},{1,7},{3,5},{5,3},{7,1},{8,14},{10,12},{12... | collective-permute-start | bytes 884744 | tf_op jit(solution)/shard_map/ppermute | solution.py:460
  266.5 17.3 %collective-permute-start.34 = (bf16[256,1152]{1,0:T(8,128)(2,1)S(1)}, bf16[256,1152]{1,0:T(8,128)(2,1)S(1)}, u32[]{:S(2)}, u32[]{:S(2)}) collective-permute-start(bf16[256,1152]{1,0:T(8,128)(2,1)S(1)} %slice.286), channel_id=1, source_target_pairs={{0,16},{8,24},{16,0},{24,8},{1,17},{9,25},{17,1},{25,9},{2,18},{10... | collective-permute-start | bytes 1769480 | tf_op jit(solution)/shard_map/ppermute | solution.py:457
  267.6 16.3 %collective-permute-start.36 = (bf16[256,1152]{1,0:T(8,128)(2,1)S(1)}, bf16[256,1152]{1,0:T(8,128)(2,1)S(1)}, u32[]{:S(2)}, u32[]{:S(2)}) collective-permute-start(bf16[256,1152]{1,0:T(8,128)(2,1)S(1)} %slice.287), channel_id=1, source_target_pairs={{0,8},{8,0},{16,24},{24,16},{1,9},{9,1},{17,25},{25,17},{2,10},{10... | collective-permute-start | bytes 1769480 | tf_op jit(solution)/shard_map/ppermute | solution.py:457
  308.0 188.1 %reduce-scatter.5.cloned.1.call-start = ((), (), s32[]{:S(2)}) async-start(), calls=%async_computation.3 | async-start | bytes 5160960 | tf_op jit(solution)/shard_map/reduce_scatter | solution.py:648
  329.2 15.4 %collective-permute-start.38 = (bf16[256,1152]{1,0:T(8,128)(2,1)S(1)}, bf16[256,1152]{1,0:T(8,128)(2,1)S(1)}, u32[]{:S(2)}, u32[]{:S(2)}) collective-permute-start(bf16[256,1152]{1,0:T(8,128)(2,1)S(1)} %get-tuple-element.242), channel_id=1, source_target_pairs={{0,16},{8,24},{16,0},{24,8},{1,17},{9,25},{17,1},{25,9},{2,18},{10... | collective-permute-start | bytes 1769480 | tf_op jit(solution)/shard_map/ppermute | solution.py:457
  330.1 16.9 %collective-permute-start.39 = (bf16[256,1152]{1,0:T(8,128)(2,1)S(1)}, bf16[256,1152]{1,0:T(8,128)(2,1)S(1)}, u32[]{:S(2)}, u32[]{:S(2)}) collective-permute-start(bf16[256,1152]{1,0:T(8,128)(2,1)S(1)} %get-tuple-element.243), channel_id=1, source_target_pairs={{0,8},{8,0},{16,24},{24,16},{1,9},{9,1},{17,25},{25,17},{2,10},{10... | collective-permute-start | bytes 1769480 | tf_op jit(solution)/shard_map/ppermute | solution.py:457
  346.0 27.7 %collective-permute-start.40 = (bf16[512,1152]{1,0:T(8,128)(2,1)}, bf16[512,1152]{1,0:T(8,128)(2,1)S(1)}, u32[]{:S(2)}, u32[]{:S(2)}) collective-permute-start(bf16[512,1152]{1,0:T(8,128)(2,1)} %pad_maximum_fusion.14), channel_id=1, source_target_pairs={{0,8},{8,0},{16,24},{24,16},{1,9},{9,1},{17,25},{25,17},{2,10},{10... | collective-permute-start | bytes 3538952 | tf_op jit(solution)/shard_map/ppermute | solution.py:457
  348.3 27.5 %collective-permute-start.41 = (bf16[512,1152]{1,0:T(8,128)(2,1)}, bf16[512,1152]{1,0:T(8,128)(2,1)}, u32[]{:S(2)}, u32[]{:S(2)}) collective-permute-start(bf16[512,1152]{1,0:T(8,128)(2,1)} %pad_maximum_fusion.15), channel_id=1, source_target_pairs={{0,16},{8,24},{16,0},{24,8},{1,17},{9,25},{17,1},{25,9},{2,18},{10... | collective-permute-start | bytes 3538952 | tf_op jit(solution)/shard_map/ppermute | solution.py:457
  378.8 16.5 %collective-permute-start.43 = (bf16[4,4,72,896]{3,2,1,0:T(8,128)(2,1)}, bf16[4,4,72,896]{3,2,1,0:T(8,128)(2,1)S(1)}, u32[]{:S(2)}, u32[]{:S(2)}) collective-permute-start(bf16[4,4,72,896]{3,2,1,0:T(8,128)(2,1)} %get-tuple-element.166), channel_id=1, source_target_pairs={{0,1},{1,0},{2,3},{3,2},{4,5},{5,4},{6,7},{7,6},{8,9},{9,8},{10,11... | collective-permute-start | bytes 6193160 | tf_op jit(solution)/shard_map/ppermute | solution.py:463
  402.2 136.0 %all-gather.8.cloned.1.call-start = ((), (), s32[]{:S(2)}) async-start(), calls=%async_computation.5 | async-start | bytes 2488320 | tf_op jit(solution)/shard_map/all_gather | solution.py:659
  439.9 22.7 %collective-permute-start.48 = (bf16[1152,512]{1,0:T(8,128)(2,1)}, bf16[1152,512]{1,0:T(8,128)(2,1)}, u32[]{:S(2)}, u32[]{:S(2)}) collective-permute-start(bf16[1152,512]{1,0:T(8,128)(2,1)} %slice.290), channel_id=1, source_target_pairs={{0,1},{1,0},{2,3},{3,2},{4,5},{5,4},{6,7},{7,6},{8,9},{9,8},{10,11... | collective-permute-start | bytes 3538952 | tf_op jit(solution)/shard_map/ppermute | solution.py:463
  440.8 195.0 %all-gather.6.cloned.1.call-start = ((), (), s32[]{:S(2)}) async-start(), calls=%async_computation.4 | async-start | bytes 5160960 | tf_op jit(solution)/shard_map/all_gather | solution.py:654
  446.5 16.2 %collective-permute-start.47 = (bf16[512,512]{1,0:T(8,128)(2,1)}, bf16[512,512]{1,0:T(8,128)(2,1)}, u32[]{:S(2)}, u32[]{:S(2)}) collective-permute-start(bf16[512,512]{1,0:T(8,128)(2,1)} %bitcast.59), channel_id=1, source_target_pairs={{0,1},{1,0},{2,3},{3,2},{4,5},{5,4},{6,7},{7,6},{8,9},{9,8},{10,11... | collective-permute-start | bytes 1572872 | tf_op jit(solution)/shard_map/ppermute | solution.py:463
  532.0 35.6 %collective-permute-start.64 = (bf16[512,768]{1,0:T(8,128)(2,1)}, bf16[512,768]{1,0:T(8,128)(2,1)}, u32[]{:S(2)}, u32[]{:S(2)}) collective-permute-start(bf16[512,768]{1,0:T(8,128)(2,1)} %pad_maximum_fusion.27), channel_id=1, source_target_pairs={{0,2},{6,4},{1,3},{7,5},{8,10},{14,12},{9,11},{15,13},{16,18},{22,... | collective-permute-start | bytes 2359304 | tf_op jit(solution)/shard_map/ppermute | solution.py:505
  538.2 37.5 %collective-permute-start.69 = (bf16[864,1152]{1,0:T(8,128)(2,1)}, bf16[864,1152]{1,0:T(8,128)(2,1)}, u32[]{:S(2)}, u32[]{:S(2)}) collective-permute-start(bf16[864,1152]{1,0:T(8,128)(2,1)} %all-gather.8.cloned.1.call-done), channel_id=1, source_target_pairs={{0,1},{1,0},{2,3},{3,2},{4,5},{5,4},{6,7},{7,6},{8,9},{9,8},{10,11... | collective-permute-start | bytes 5971976 | tf_op jit(solution)/shard_map/ppermute | solution.py:463
  574.3 61.3 %collective-permute-start.66 = (bf16[512,768]{1,0:T(8,128)(2,1)S(1)}, bf16[512,768]{1,0:T(8,128)(2,1)S(1)}, u32[]{:S(2)}, u32[]{:S(2)}) collective-permute-start(bf16[512,768]{1,0:T(8,128)(2,1)S(1)} %add.381), channel_id=1, source_target_pairs={{2,0},{4,6},{3,1},{5,7},{10,8},{12,14},{11,9},{13,15},{18,16},{20,... | collective-permute-start | bytes 2359304 | tf_op jit(solution)/shard_map/ppermute | solution.py:515
  635.8 34.3 %collective-permute-start.68 = (bf16[4,4,2,72,896]{4,3,2,1,0:T(8,128)(2,1)}, bf16[4,4,2,72,896]{4,3,2,1,0:T(8,128)(2,1)}, u32[]{:S(2)}, u32[]{:S(2)}) collective-permute-start(bf16[4,4,2,72,896]{4,3,2,1,0:T(8,128)(2,1)} %bitcast.240), channel_id=1, source_target_pairs={{0,1},{1,0},{2,3},{3,2},{4,5},{5,4},{6,7},{7,6},{8,9},{9,8},{10,11... | collective-permute-start | bytes 12386312 | tf_op jit(solution)/shard_map/ppermute | solution.py:463
  645.1 23.5 %collective-permute-start.57 = (bf16[128,1152]{1,0:T(8,128)(2,1)S(1)}, bf16[128,1152]{1,0:T(8,128)(2,1)S(1)}, u32[]{:S(2)}, u32[]{:S(2)}) collective-permute-start(bf16[128,1152]{1,0:T(8,128)(2,1)S(1)} %get-tuple-element.238), channel_id=1, source_target_pairs={{0,4},{2,6},{4,0},{6,2},{1,5},{3,7},{5,1},{7,3},{8,12},{10,14},{12... | collective-permute-start | bytes 884744 | tf_op jit(solution)/shard_map/ppermute | solution.py:460
  646.5 22.1 %collective-permute-start.58 = (bf16[128,1152]{1,0:T(8,128)(2,1)S(1)}, bf16[128,1152]{1,0:T(8,128)(2,1)S(1)}, u32[]{:S(2)}, u32[]{:S(2)}) collective-permute-start(bf16[128,1152]{1,0:T(8,128)(2,1)S(1)} %get-tuple-element.237), channel_id=1, source_target_pairs={{0,6},{2,4},{4,2},{6,0},{1,7},{3,5},{5,3},{7,1},{8,14},{10,12},{12... | collective-permute-start | bytes 884744 | tf_op jit(solution)/shard_map/ppermute | solution.py:460
  (147 other events, 1262.3 us)
Sparse Core Ops, SparseCore 0:
  10.5 40.2 all-gather.3
  308.1 43.5 reduce-scatter.6
  402.4 77.3 reduce-scatter.4
  481.2 44.4 all-gather.7
  527.8 94.8 all-gather.5

commit v4 on v3

--- a/solution.py
+++ b/solution.py
@@ -288,18 +288,26 @@
 
 def columns_grad_kernel(n, *refs):
     x, g = refs[:n], refs[n : 2 * n]
-    outs = refs[2 * n : 2 * n + 2]
-    f = outs[0].shape[-1]
-    xt = [x[k][...].T for k in range(n)]
+    outs, xt = refs[2 * n : 2 * n + 2], refs[-1]
+    rows = x[0].shape[0]
+
+    @pl.when(pl.program_id(0) == 0)
+    def _():
+        for k in range(n):
+            xt[:, k * rows : (k + 1) * rows] = x[k][...].T
+
+    total = dot(xt[:, :rows], g[0][0])
+    for k in range(1, n):
+        total += dot(xt[:, k * rows : (k + 1) * rows], g[k][0])
+    n_z, n_s, d, _ = outs[0].shape
     for i, o in enumerate(outs):
-        total = dot(xt[0], g[0][0, :, i * f : (i + 1) * f])
-        for k in range(1, n):
-            total += dot(xt[k], g[k][0, :, i * f : (i + 1) * f])
-        n_z, n_s, d, _ = o.shape
-        for j in range(n_s):
-            for q in range(n_z):
-                first = (j * n_z + q) * d
-                o[q, j] = total[first : first + d].astype(BF)
+
+        @pl.when(pl.program_id(0) == i)
+        def _():
+            for j in range(n_s):
+                for q in range(n_z):
+                    first = (j * n_z + q) * d
+                    o[q, j] = total[first : first + d].astype(BF)
 
 
 def columns_grad(m, xs, gus, form):
@@ -309,24 +317,26 @@
     out = full(form)
     return call(
         functools.partial(columns_grad_kernel, n),
-        (1,),
-        [full((rows, width))] * n + [pl.BlockSpec((1, rows, f), lambda i: (m, 0, 0))] * n,
+        (2,),
+        [full((rows, width))] * n + [pl.BlockSpec((1, rows, f // 2), lambda i: (m, 0, i))] * n,
         [out, out],
         [jax.ShapeDtypeStruct(form, BF)] * 2,
         2 * n * rows * width * f,
         n * rows * (width + f) * 2 + 2 * width * f,
+        scratch=[pltpu.VMEM((width, n * rows), BF)],
     )(*xs, *gus)
 
 
 def down_grad_kernel(n, *refs):
     hid, z = refs[:n], refs[n : 2 * n]
-    outs = refs[2 * n :]
-    f = hid[0].shape[-1] // 2
-    for i, o in enumerate(outs):
-        total = dot_rows(hid[0][:, i * f : (i + 1) * f], z[0][...])
-        for k in range(1, n):
-            total += dot_rows(hid[k][:, i * f : (i + 1) * f], z[k][...])
-        o[...] = total[: o.shape[0]].astype(BF)
+    total = dot_rows(hid[0][...], z[0][...])
+    for k in range(1, n):
+        total += dot_rows(hid[k][...], z[k][...])
+    for i, o in enumerate(refs[2 * n :]):
+
+        @pl.when(pl.program_id(0) == i)
+        def _():
+            o[...] = total[: o.shape[0]].astype(BF)
 
 
 def down_grad(hids, zs, f_own):
@@ -336,8 +346,8 @@
     out = full((f_own, width))
     return call(
         functools.partial(down_grad_kernel, n),
-        (1,),
-        [full((rows, f))] * n + [full((rows, width))] * n,
+        (2,),
+        [pl.BlockSpec((rows, f // 2), lambda i: (0, i))] * n + [full((rows, width))] * n,
         [out, out],
         [jax.ShapeDtypeStruct((f_own, width), BF)] * 2,
         2 * n * rows * width * f,

time: 696 us -> 699 us (level)
  no operation moved by 1% of the time
where the time goes in v4:
time: 699 us; the launch traced here: 690 us
  waiting for transfers between devices  225 us (32%)
  Pallas kernels  204 us (29%)
  other arithmetic  79.6 us (11%)
  local copies, waits for them, and re-layouts  74.6 us (11%)
  starting transfers between devices  72.7 us (10%)
  matrix products  18.2 us (3%)
  between operations  15.8 us (2%)
    ppermute x36, waiting for transfers between devices, px(): return lax.ppermute(v, 'shard', [(i, i ^ k) for i in range(n_s)])  70.4 us
    ppermute x1, waiting for transfers between devices, last(): self.got = lax.ppermute(self.part, 'z', [(1, 0), (2, 3)])  55.9 us
    pallas_call x4, Pallas kernels, ffn_back(): call(ffn_back_kernel, (rows // tile,), [row, keep, keep, act, act], [pl.B...  50.9 us
    pallas_call x4, Pallas kernels, ffn(): call(ffn_kernel, (rows // tile,), [row, keep, keep], [act, act, act, row]...  49 us
    ppermute x12, waiting for transfers between devices, pz(): return lax.ppermute(v, 'z', [(i, i ^ k) for i in range(n_z)])  48.2 us
    ppermute x36, starting transfers between devices, px(): return lax.ppermute(v, 'shard', [(i, i ^ k) for i in range(n_s)])  39.9 us
    pallas_call x2, Pallas kernels, columns_grad(): call(functools.partial(columns_grad_kernel, n), (2,), [full((rows, width)...  35.7 us
    unnamed x243, local copies, waits for them, and re-layouts  31.6 us
  transfers between devices with their start and end apart: 75, of which 29 were waited for; matrix products, arithmetic and copies ran while one was open for 18% of the time, Pallas kernels for 24%

profile of v4, /device:TPU:0, one launch (start us, length us, event | category | flops | bytes accessed | tf_op | source)
XLA Modules:
  0.0 690.2 jit_solution(6792782442789034870)
XLA Ops:
  19.3 7.3 %collective-permute-done = bf16[128,1152]{1,0:T(8,128)(2,1)S(1)} collective-permute-done((bf16[128,1152]{1,0:T(8,128)(2,1)S(1)}, bf16[128,1152]{1,0:T(8,128)(2,1)S(1)}, u32[]{:S(2)}, u32[]{:S(2)}) %collective-permute-start) | collective-permute-done | bytes 294944 | tf_op jit(solution)/shard_map/ppermute | solution.py:470
  30.1 4.7 constant_dynamic-slice_fusion.23
  38.4 3.4 multiply_sine_fusion
  43.1 7.7 %all-gather.4.cloned.1.call-done.w = bf16[1152,1024]{1,0:T(8,128)(2,1)} async-done(((bf16[288,1024]{1,0:T(8,128)(2,1)}), bf16[1152,1024]{1,0:T(8,128)(2,1)}) %all-gather.4.cloned.1.call-update) | async-done | bytes 2359312 | tf_op jit(solution)/shard_map/all_gather | solution.py:545
  56.3 4.5 shard_map.271.wd
  61.6 5.7 collective-permute-done.8
  81.4 9.4 %shard_map.272 = (bf16[1024,1152]{1,0:T(8,128)(2,1)}, f32[1024,768]{1,0:T(8,128)}, bf16[1024,512]{1,0:T(8,128)(2,1)}, bf16[1024,256]{1,0:T(8,128)(2,1)}, bf16[1024,256]{1,0:T(8,128)(2,1)}) custom-call(s32[6]{0:T(128)} %concatenate.62.at, bf16[4,128,1152]{2,1,0:T(8,128)(2,1)} %copy-done.53, bf16[4,128,1152]{2,1,0:T(8,128)(2,1)} %collective-permute-done.3.oth, ...), custom_call_target="tpu_custom_call" | custom-call | flops 2415919104 | bytes 11796480 | tf_op jit(solution)/shard_map/pallas_call | solution.py:108
  90.8 10.6 %shard_map.273 = bf16[1024,512]{1,0:T(8,128)(2,1)} custom-call(s32[6]{0:T(128)} %concatenate.62.at, bf16[1024,512]{1,0:T(8,128)(2,1)} %get-tuple-element.102.q, bf16[1024,256]{1,0:T(8,128)(2,1)} %get-tuple-element.103.k, bf16[1024,256]{1,0:T(8,128)(2,1)} %get-tuple-element.104.v), custom_call_target="tpu_custom_call" | custom-call | flops 2147483648 | bytes 3145728 | tf_op jit(solution)/shard_map/pallas_call | solution.py:162
  102.9 15.4 %collective-permute-done.13.refs_2_ = bf16[2,288,896]{2,1,0:T(8,128)(2,1)} collective-permute-done((bf16[2,288,896]{2,1,0:T(8,128)(2,1)}, bf16[2,288,896]{2,1,0:T(8,128)(2,1)}, u32[]{:S(2)}, u32[]{:S(2)}) %collective-permute-start.13) | collective-permute-done | bytes 1032224 | tf_op jit(solution)/shard_map/ppermute | solution.py:467
  130.3 3.3 copy-done.2
  133.6 12.5 %shard_map.275 = (bf16[512,1792]{1,0:T(8,128)(2,1)S(1)}, bf16[512,1792]{1,0:T(8,128)(2,1)S(1)}, bf16[512,1792]{1,0:T(8,128)(2,1)S(1)}, f32[512,1152]{1,0:T(8,128)S(1)}) custom-call(bf16[512,1152]{1,0:T(8,128)(2,1)S(1)} %multiply_convert_fusion.x.refs_0_, bf16[2,1152,1792]{2,1,0:T(8,128)(2,1)} %copy-done.2, bf16[1792,1152]{1,0:T(8,128)(2,1)S(1)} %copy-done.3), custom_call_target="tpu_custom_call" | custom-call | flops 6341787648 | bytes 20250624 | tf_op jit(solution)/shard_map/pallas_call | solution.py:249
  147.3 6.1 collective-permute-done.19.x.refs_1_
  155.7 12.0 %shard_map.276 = (bf16[512,1792]{1,0:T(8,128)(2,1)S(1)}, bf16[512,1792]{1,0:T(8,128)(2,1)S(1)}, bf16[512,1792]{1,0:T(8,128)(2,1)S(1)}, bf16[512,1152]{1,0:T(8,128)(2,1)S(1)}) custom-call(bf16[512,1152]{1,0:T(8,128)(2,1)S(1)} %collective-permute-done.19.x.refs_1_, bf16[2,1152,1792]{2,1,0:T(8,128)(2,1)} %copy-done.2, bf16[1792,1152]{1,0:T(8,128)(2,1)S(1)} %copy-done.3), custom_call_target="tpu_custom_call" | custom-call | flops 6341787648 | bytes 20250624 | tf_op jit(solution)/shard_map/pallas_call | solution.py:249
  170.2 12.4 %shard_map.277 = (bf16[512,1792]{1,0:T(8,128)(2,1)S(1)}, bf16[512,1792]{1,0:T(8,128)(2,1)S(1)}, bf16[512,1792]{1,0:T(8,128)(2,1)S(1)}, bf16[512,1152]{1,0:T(8,128)(2,1)S(1)}) custom-call(bf16[512,1152]{1,0:T(8,128)(2,1)S(1)} %constant_dynamic-update-slice_fusion.x.refs_3_, bf16[2,1152,1792]{2,1,0:T(8,128)(2,1)} %copy-done.2, bf16[1792,1152]{1,0:T(8,128)(2,1)S(1)} %copy-done.3), custom_call_target="tpu_custom_call" | custom-call | flops 6341787648 | bytes 20250624 | tf_op jit(solution)/shard_map/pallas_call | solution.py:249
  186.6 12.1 %shard_map.278 = (bf16[512,1792]{1,0:T(8,128)(2,1)S(1)}, bf16[512,1792]{1,0:T(8,128)(2,1)S(1)}, bf16[512,1792]{1,0:T(8,128)(2,1)S(1)}, bf16[512,1152]{1,0:T(8,128)(2,1)S(1)}) custom-call(bf16[512,1152]{1,0:T(8,128)(2,1)S(1)} %collective-permute-done.21.x.refs_2_, bf16[2,1152,1792]{2,1,0:T(8,128)(2,1)} %copy-done.2, bf16[1792,1152]{1,0:T(8,128)(2,1)S(1)} %copy-done.3), custom_call_target="tpu_custom_call" | custom-call | flops 6341787648 | bytes 20250624 | tf_op jit(solution)/shard_map/pallas_call | solution.py:249
  212.2 5.6 collective-permute-done.30
  217.8 13.6 %collective-permute-done.31 = bf16[128,1152]{1,0:T(8,128)(2,1)S(1)} collective-permute-done((bf16[128,1152]{1,0:T(8,128)(2,1)}, bf16[128,1152]{1,0:T(8,128)(2,1)S(1)}, u32[]{:S(2)}, u32[]{:S(2)}) %collective-permute-start.31) | collective-permute-done | bytes 294944 | tf_op jit(solution)/shard_map/ppermute | solution.py:470
  239.0 3.8 collective-permute-start.27
  245.3 13.5 %shard_map.279 = (bf16[2,512,1792]{2,1,0:T(8,128)(2,1)S(1)}, f32[512,1152]{1,0:T(8,128)S(1)}) custom-call(bf16[512,1152]{1,0:T(8,128)(2,1)S(1)} %get-tuple-element.209.z.refs_4_, bf16[2,1152,1792]{2,1,0:T(8,128)(2,1)} %copy-done.2, bf16[1792,1152]{1,0:T(8,128)(2,1)} %shard_map.271.wd, bf16[512,1792]{1,0:T(8,128)(2,1)S(1)} %copy-done.34, ...), custom_call_target="tpu_custom_call" | custom-call | flops 6341787648 | bytes 20250624 | tf_op jit(solution)/shard_map/pallas_call | solution.py:277
  258.8 5.9 collective-permute-done.28
  269.3 12.6 %shard_map.280 = (bf16[2,512,1792]{2,1,0:T(8,128)(2,1)S(1)}, bf16[512,1152]{1,0:T(8,128)(2,1)S(1)}) custom-call(bf16[512,1152]{1,0:T(8,128)(2,1)S(1)} %collective-permute-done.33.z.refs_5_, bf16[2,1152,1792]{2,1,0:T(8,128)(2,1)} %copy-done.2, bf16[1792,1152]{1,0:T(8,128)(2,1)S(1)} %copy-done.4, bf16[512,1792]{1,0:T(8,128)(2,1)S(1)} %copy-done.30, ...), custom_call_target="tpu_custom_call" | custom-call | flops 6341787648 | bytes 20250624 | tf_op jit(solution)/shard_map/pallas_call | solution.py:277
  284.9 16.0 %shard_map.281 = (bf16[864,1152]{1,0:T(8,128)(2,1)}, bf16[864,1152]{1,0:T(8,128)(2,1)}) custom-call(bf16[512,1792]{1,0:T(8,128)(2,1)} %copy-done.37, bf16[512,1792]{1,0:T(8,128)(2,1)} %copy-done.38, bf16[512,1792]{1,0:T(8,128)(2,1)} %copy-done.40, bf16[512,1792]{1,0:T(8,128)(2,1)} %copy-done.39, bf16[512,1152]{1,0:T(8,128)(2,1)} %copy-done.6, ...), custom_call_target="tpu_custom_call" | custom-call | flops 8455716864 | bytes 16187392 | tf_op jit(solution)/shard_map/pallas_call | solution.py:347
  300.9 4.2 collective-permute-done.37
  305.1 3.3 add.356
  315.0 12.7 %shard_map.282 = (bf16[2,512,1792]{2,1,0:T(8,128)(2,1)S(1)}, bf16[512,1152]{1,0:T(8,128)(2,1)S(1)}) custom-call(bf16[512,1152]{1,0:T(8,128)(2,1)S(1)} %copy-done.15, bf16[2,1152,1792]{2,1,0:T(8,128)(2,1)} %copy-done.2, bf16[1792,1152]{1,0:T(8,128)(2,1)S(1)} %copy-done.5, bf16[512,1792]{1,0:T(8,128)(2,1)S(1)} %copy-done.26, bf16[512,1792]{1,0:T(8,128)(2,1)S(1)} %copy-done.28), custom_call_target="tpu_custom_call" | custom-call | flops 6341787648 | bytes 20250624 | tf_op jit(solution)/shard_map/pallas_call | solution.py:277
  331.7 12.2 %shard_map.283 = (bf16[2,512,1792]{2,1,0:T(8,128)(2,1)S(1)}, bf16[512,1152]{1,0:T(8,128)(2,1)S(1)}) custom-call(bf16[512,1152]{1,0:T(8,128)(2,1)S(1)} %copy-done.11, bf16[2,1152,1792]{2,1,0:T(8,128)(2,1)} %copy-done.2, bf16[1792,1152]{1,0:T(8,128)(2,1)S(1)} %copy-done.5, bf16[512,1792]{1,0:T(8,128)(2,1)S(1)} %copy-done.22, bf16[512,1792]{1,0:T(8,128)(2,1)S(1)} %copy-done.24), custom_call_target="tpu_custom_call" | custom-call | flops 6341787648 | bytes 20250624 | tf_op jit(solution)/shard_map/pallas_call | solution.py:277
  352.3 17.8 %shard_map.284 = (bf16[4,4,72,896]{3,2,1,0:T(8,128)(2,1)}, bf16[4,4,72,896]{3,2,1,0:T(8,128)(2,1)}) custom-call(bf16[512,1152]{1,0:T(8,128)(2,1)} %copy-done.7, bf16[512,1152]{1,0:T(8,128)(2,1)} %copy-done.8, bf16[512,1152]{1,0:T(8,128)(2,1)} %copy-done.9, bf16[512,1152]{1,0:T(8,128)(2,1)} %copy-done.13, bf16[2,512,1792]{2,1,0:T(8,128)(2,1)} %copy-done.17, ...), custom_call_target="tpu_custom_call" | custom-call | flops 8455716864 | bytes 16187392 | tf_op jit(solution)/shard_map/pallas_call | solution.py:318
  370.1 3.8 collective-permute-done.40
  378.9 17.9 %shard_map.285 = (bf16[4,4,72,896]{3,2,1,0:T(8,128)(2,1)}, bf16[4,4,72,896]{3,2,1,0:T(8,128)(2,1)}) custom-call(bf16[512,1152]{1,0:T(8,128)(2,1)} %copy-done.7, bf16[512,1152]{1,0:T(8,128)(2,1)} %copy-done.8, bf16[512,1152]{1,0:T(8,128)(2,1)} %copy-done.9, bf16[512,1152]{1,0:T(8,128)(2,1)} %copy-done.13, bf16[2,512,1792]{2,1,0:T(8,128)(2,1)} %copy-done.17, ...), custom_call_target="tpu_custom_call" | custom-call | flops 8455716864 | bytes 16187392 | tf_op jit(solution)/shard_map/pallas_call | solution.py:318
  397.5 3.7 collective-permute-done.42
  420.0 14.8 %shard_map.286 = (bf16[1024,512]{1,0:T(8,128)(2,1)}, f32[1024,256]{1,0:T(8,128)}, f32[1024,256]{1,0:T(8,128)}, f32[1,256]{1,0:T(1,128)}) custom-call(s32[6]{0:T(128)} %concatenate.62.at, bf16[1024,512]{1,0:T(8,128)(2,1)} %get-tuple-element.102.q, bf16[1024,256]{1,0:T(8,128)(2,1)} %get-tuple-element.103.k, bf16[1024,256]{1,0:T(8,128)(2,1)} %get-tuple-element.104.v, ...), custom_call_target="tpu_custom_call" | custom-call | flops 5368709120 | bytes 9437184 | tf_op jit(solution)/shard_map/pallas_call | solution.py:213
  461.3 3.5 fusion.18
  464.8 4.6 fusion.13
  471.1 4.1 convolution_convert_fusion
  477.6 6.1 collective-permute-done.49
  487.6 8.9 %collective-permute-done.50 = bf16[320,768]{1,0:T(8,128)(2,1)S(1)} collective-permute-done((bf16[320,768]{1,0:T(8,128)(2,1)S(1)}, bf16[320,768]{1,0:T(8,128)(2,1)S(1)}, u32[]{:S(2)}, u32[]{:S(2)}) %collective-permute-start.50) | collective-permute-done | bytes 491552 | tf_op jit(solution)/shard_map/ppermute | solution.py:467
  503.3 5.6 collective-permute-done.53
  508.9 3.8 collective-permute-done.54
  525.3 4.5 collective-permute-done.61
  534.3 6.0 collective-permute-start.64
  540.3 29.7 %collective-permute-done.64 = bf16[512,768]{1,0:T(8,128)(2,1)} collective-permute-done((bf16[512,768]{1,0:T(8,128)(2,1)}, bf16[512,768]{1,0:T(8,128)(2,1)}, u32[]{:S(2)}, u32[]{:S(2)}) %collective-permute-start.64) | collective-permute-done | bytes 786464 | tf_op jit(solution)/shard_map/ppermute | solution.py:515
  573.1 3.3 fusion.11
  582.5 55.9 %collective-permute-done.66 = bf16[512,768]{1,0:T(8,128)(2,1)S(1)} collective-permute-done((bf16[512,768]{1,0:T(8,128)(2,1)S(1)}, bf16[512,768]{1,0:T(8,128)(2,1)S(1)}, u32[]{:S(2)}, u32[]{:S(2)}) %collective-permute-start.66) | collective-permute-done | bytes 786464 | tf_op jit(solution)/shard_map/ppermute | solution.py:525
  639.1 5.9 bitcast_convert_fusion
  648.8 3.4 collective-permute-start.58
  655.5 5.4 collective-permute-done.56
  660.9 10.5 %collective-permute-done.57 = bf16[128,1152]{1,0:T(8,128)(2,1)S(1)} collective-permute-done((bf16[128,1152]{1,0:T(8,128)(2,1)S(1)}, bf16[128,1152]{1,0:T(8,128)(2,1)S(1)}, u32[]{:S(2)}, u32[]{:S(2)}) %collective-permute-start.57) | collective-permute-done | bytes 294944 | tf_op jit(solution)/shard_map/ppermute | solution.py:470
  672.9 10.7 %shard_map.287 = (f32[288,6912]{1,0:T(8,128)}, f32[288,6912]{1,0:T(8,128)}) custom-call(s32[6]{0:T(128)} %concatenate.62.at, bf16[4,4,2,72,896]{4,3,2,1,0:T(8,128)(2,1)} %bitcast.241, bf16[4,4,2,72,896]{4,3,2,1,0:T(8,128)(2,1)} %collective-permute-done.68.oth), custom_call_target="tpu_custom_call" | custom-call | bytes 23887872 | tf_op jit(solution)/shard_map/pallas_call | solution.py:419
  (545 shorter events, 214.2 us)
Async XLA Ops:
  7.2 43.5 %all-gather.4.cloned.1.call-start = ((), (), s32[]{:S(2)}) async-start(), calls=%async_computation.2 | async-start | bytes 2949120 | tf_op jit(solution)/shard_map/all_gather | solution.py:545
  10.2 342.0 %reduce-scatter.7.cloned.1.call-start = ((), (), s32[]{:S(2)}) async-start(), calls=%async_computation.6 | async-start | bytes 2488320
  11.1 15.5 %collective-permute-start = (bf16[128,1152]{1,0:T(8,128)(2,1)S(1)}, bf16[128,1152]{1,0:T(8,128)(2,1)S(1)}, u32[]{:S(2)}, u32[]{:S(2)}) collective-permute-start(bf16[128,1152]{1,0:T(8,128)(2,1)S(1)} %get-tuple-element.277), channel_id=1, source_target_pairs={{0,2},{2,0},{4,6},{6,4},{1,3},{3,1},{5,7},{7,5},{8,10},{10,8},{12,... | collective-permute-start | bytes 884744 | tf_op jit(solution)/shard_map/ppermute | solution.py:470
  14.2 27.6 %collective-permute-start.1 = (bf16[128,1152]{1,0:T(8,128)(2,1)}, bf16[128,1152]{1,0:T(8,128)(2,1)S(1)}, u32[]{:S(2)}, u32[]{:S(2)}) collective-permute-start(bf16[128,1152]{1,0:T(8,128)(2,1)} %get-tuple-element.279), channel_id=1, source_target_pairs={{0,4},{2,6},{4,0},{6,2},{1,5},{3,7},{5,1},{7,3},{8,12},{10,14},{12... | collective-permute-start | bytes 884744 | tf_op jit(solution)/shard_map/ppermute | solution.py:470
  16.7 25.0 %collective-permute-start.2 = (bf16[128,1152]{1,0:T(8,128)(2,1)S(1)}, bf16[128,1152]{1,0:T(8,128)(2,1)S(1)}, u32[]{:S(2)}, u32[]{:S(2)}) collective-permute-start(bf16[128,1152]{1,0:T(8,128)(2,1)S(1)} %get-tuple-element.278), channel_id=1, source_target_pairs={{0,6},{2,4},{4,2},{6,0},{1,7},{3,5},{5,3},{7,1},{8,14},{10,12},{12... | collective-permute-start | bytes 884744 | tf_op jit(solution)/shard_map/ppermute | solution.py:470
  26.6 26.2 %collective-permute-start.4 = (f32[1280]{0:T(1024)S(1)}, f32[1280]{0:T(1024)S(1)}, u32[]{:S(2)}, u32[]{:S(2)}) collective-permute-start(f32[1280]{0:T(1024)S(1)} %concatenate.61), channel_id=1, source_target_pairs={{0,8},{8,0},{16,24},{24,16},{1,9},{9,1},{17,25},{25,17},{2,10},{10... | collective-permute-start | bytes 15368 | tf_op jit(solution)/shard_map/ppermute | solution.py:467
  28.3 32.5 %collective-permute-start.5 = (f32[1280]{0:T(1024)S(1)}, f32[1280]{0:T(1024)}, u32[]{:S(2)}, u32[]{:S(2)}) collective-permute-start(f32[1280]{0:T(1024)S(1)} %concatenate.61), channel_id=1, source_target_pairs={{0,16},{8,24},{16,0},{24,8},{1,17},{9,25},{17,1},{25,9},{2,18},{10... | collective-permute-start | bytes 15368 | tf_op jit(solution)/shard_map/ppermute | solution.py:467
  29.8 31.8 %collective-permute-start.6 = (f32[1280]{0:T(1024)S(1)}, f32[1280]{0:T(1024)S(1)}, u32[]{:S(2)}, u32[]{:S(2)}) collective-permute-start(f32[1280]{0:T(1024)S(1)} %concatenate.61), channel_id=1, source_target_pairs={{0,24},{8,16},{16,8},{24,0},{1,25},{9,17},{17,9},{25,1},{2,26},{10... | collective-permute-start | bytes 15368 | tf_op jit(solution)/shard_map/ppermute | solution.py:467
  52.2 15.1 %collective-permute-start.8 = (bf16[128,1152]{1,0:T(8,128)(2,1)}, bf16[128,1152]{1,0:T(8,128)(2,1)}, u32[]{:S(2)}, u32[]{:S(2)}) collective-permute-start(bf16[128,1152]{1,0:T(8,128)(2,1)} %constant_dynamic-slice_fusion.36), channel_id=1, source_target_pairs={{0,16},{8,24},{16,0},{24,8},{1,17},{9,25},{17,1},{25,9},{2,18},{10... | collective-permute-start | bytes 884744 | tf_op jit(solution)/shard_map/ppermute | solution.py:467
  60.8 20.6 %collective-permute-start.3 = (bf16[4,128,1152]{2,1,0:T(8,128)(2,1)S(1)}, bf16[4,128,1152]{2,1,0:T(8,128)(2,1)}, u32[]{:S(2)}, u32[]{:S(2)}) collective-permute-start(bf16[4,128,1152]{2,1,0:T(8,128)(2,1)S(1)} %pad_maximum_fusion.4.own), channel_id=1, source_target_pairs={{0,1},{1,0},{2,3},{3,2},{4,5},{5,4},{6,7},{7,6},{8,9},{9,8},{10,11... | collective-permute-start | bytes 3538952 | tf_op jit(solution)/shard_map/ppermute | solution.py:473
  70.2 48.6 %collective-permute-start.10 = (bf16[4,128,1152]{2,1,0:T(8,128)(2,1)}, bf16[4,128,1152]{2,1,0:T(8,128)(2,1)}, u32[]{:S(2)}, u32[]{:S(2)}) collective-permute-start(bf16[4,128,1152]{2,1,0:T(8,128)(2,1)} %pad_maximum_fusion.7), channel_id=1, source_target_pairs={{0,1},{1,0},{2,3},{3,2},{4,5},{5,4},{6,7},{7,6},{8,9},{9,8},{10,11... | collective-permute-start | bytes 3538952 | tf_op jit(solution)/shard_map/ppermute | solution.py:473
  70.3 32.5 %collective-permute-start.12 = (bf16[2,288,896]{2,1,0:T(8,128)(2,1)}, bf16[2,288,896]{2,1,0:T(8,128)(2,1)S(1)}, u32[]{:S(2)}, u32[]{:S(2)}) collective-permute-start(bf16[2,288,896]{2,1,0:T(8,128)(2,1)} %pad_maximum_fusion.22), channel_id=1, source_target_pairs={{0,8},{8,0},{16,24},{24,16},{1,9},{9,1},{17,25},{25,17},{2,10},{10... | collective-permute-start | bytes 3096584 | tf_op jit(solution)/shard_map/ppermute | solution.py:467
  71.0 47.4 %collective-permute-start.13 = (bf16[2,288,896]{2,1,0:T(8,128)(2,1)}, bf16[2,288,896]{2,1,0:T(8,128)(2,1)}, u32[]{:S(2)}, u32[]{:S(2)}) collective-permute-start(bf16[2,288,896]{2,1,0:T(8,128)(2,1)} %pad_maximum_fusion.23), channel_id=1, source_target_pairs={{0,16},{8,24},{16,0},{24,8},{1,17},{9,25},{17,1},{25,9},{2,18},{10... | collective-permute-start | bytes 3096584 | tf_op jit(solution)/shard_map/ppermute | solution.py:467
  72.4 45.9 %collective-permute-start.14 = (bf16[2,288,896]{2,1,0:T(8,128)(2,1)}, bf16[2,288,896]{2,1,0:T(8,128)(2,1)}, u32[]{:S(2)}, u32[]{:S(2)}) collective-permute-start(bf16[2,288,896]{2,1,0:T(8,128)(2,1)} %pad_maximum_fusion.24), channel_id=1, source_target_pairs={{0,24},{8,16},{16,8},{24,0},{1,25},{9,17},{17,9},{25,1},{2,26},{10... | collective-permute-start | bytes 3096584 | tf_op jit(solution)/shard_map/ppermute | solution.py:467
  102.8 19.3 %collective-permute-start.11 = (bf16[512,512]{1,0:T(8,128)(2,1)S(1)}, bf16[512,512]{1,0:T(8,128)(2,1)S(1)}, u32[]{:S(2)}, u32[]{:S(2)}) collective-permute-start(bf16[512,512]{1,0:T(8,128)(2,1)S(1)} %bitcast.253), channel_id=1, source_target_pairs={{0,1},{1,0},{2,3},{3,2},{4,5},{5,4},{6,7},{7,6},{8,9},{9,8},{10,11... | collective-permute-start | bytes 1572872 | tf_op jit(solution)/shard_map/ppermute | solution.py:473
  125.5 28.0 %collective-permute-start.19 = (bf16[512,1152]{1,0:T(8,128)(2,1)S(1)}, bf16[512,1152]{1,0:T(8,128)(2,1)S(1)}, u32[]{:S(2)}, u32[]{:S(2)}) collective-permute-start(bf16[512,1152]{1,0:T(8,128)(2,1)S(1)} %multiply_convert_fusion.x.refs_0_), channel_id=1, source_target_pairs={{0,8},{8,0},{16,24},{24,16},{1,9},{9,1},{17,25},{25,17},{2,10},{10... | collective-permute-start | bytes 3538952 | tf_op jit(solution)/shard_map/ppermute | solution.py:467
  127.0 28.0 %collective-permute-start.21 = (bf16[512,1152]{1,0:T(8,128)(2,1)S(1)}, bf16[512,1152]{1,0:T(8,128)(2,1)S(1)}, u32[]{:S(2)}, u32[]{:S(2)}) collective-permute-start(bf16[512,1152]{1,0:T(8,128)(2,1)S(1)} %multiply_convert_fusion.x.refs_0_), channel_id=1, source_target_pairs={{0,16},{8,24},{16,0},{24,8},{1,17},{9,25},{17,1},{25,9},{2,18},{10... | collective-permute-start | bytes 3538952 | tf_op jit(solution)/shard_map/ppermute | solution.py:467
  153.5 15.6 %collective-permute-start.20 = (bf16[256,1152]{1,0:T(8,128)(2,1)S(1)}, bf16[256,1152]{1,0:T(8,128)(2,1)S(1)}, u32[]{:S(2)}, u32[]{:S(2)}) collective-permute-start(bf16[256,1152]{1,0:T(8,128)(2,1)S(1)} %slice.283), channel_id=1, source_target_pairs={{0,16},{8,24},{16,0},{24,8},{1,17},{9,25},{17,1},{25,9},{2,18},{10... | collective-permute-start | bytes 1769480 | tf_op jit(solution)/shard_map/ppermute | solution.py:467
  155.1 14.2 %collective-permute-start.22 = (bf16[256,1152]{1,0:T(8,128)(2,1)S(1)}, bf16[256,1152]{1,0:T(8,128)(2,1)S(1)}, u32[]{:S(2)}, u32[]{:S(2)}) collective-permute-start(bf16[256,1152]{1,0:T(8,128)(2,1)S(1)} %slice.284), channel_id=1, source_target_pairs={{0,8},{8,0},{16,24},{24,16},{1,9},{9,1},{17,25},{25,17},{2,10},{10... | collective-permute-start | bytes 1769480 | tf_op jit(solution)/shard_map/ppermute | solution.py:467
  184.0 16.0 %collective-permute-start.23 = (bf16[256,1152]{1,0:T(8,128)(2,1)S(1)}, bf16[256,1152]{1,0:T(8,128)(2,1)S(1)}, u32[]{:S(2)}, u32[]{:S(2)}) collective-permute-start(bf16[256,1152]{1,0:T(8,128)(2,1)S(1)} %get-tuple-element.264), channel_id=1, source_target_pairs={{0,16},{8,24},{16,0},{24,8},{1,17},{9,25},{17,1},{25,9},{2,18},{10... | collective-permute-start | bytes 1769480 | tf_op jit(solution)/shard_map/ppermute | solution.py:467
  185.5 17.7 %collective-permute-start.25 = (bf16[256,1152]{1,0:T(8,128)(2,1)S(1)}, bf16[256,1152]{1,0:T(8,128)(2,1)S(1)}, u32[]{:S(2)}, u32[]{:S(2)}) collective-permute-start(bf16[256,1152]{1,0:T(8,128)(2,1)S(1)} %get-tuple-element.265), channel_id=1, source_target_pairs={{0,8},{8,0},{16,24},{24,16},{1,9},{9,1},{17,25},{25,17},{2,10},{10... | collective-permute-start | bytes 1769480 | tf_op jit(solution)/shard_map/ppermute | solution.py:467
  202.3 29.6 %collective-permute-start.24 = (bf16[512,1152]{1,0:T(8,128)(2,1)}, bf16[512,1152]{1,0:T(8,128)(2,1)}, u32[]{:S(2)}, u32[]{:S(2)}) collective-permute-start(bf16[512,1152]{1,0:T(8,128)(2,1)} %pad_maximum_fusion.8), channel_id=1, source_target_pairs={{0,8},{8,0},{16,24},{24,16},{1,9},{9,1},{17,25},{25,17},{2,10},{10... | collective-permute-start | bytes 3538952 | tf_op jit(solution)/shard_map/ppermute | solution.py:467
  204.4 27.4 %collective-permute-start.26 = (bf16[512,1152]{1,0:T(8,128)(2,1)}, bf16[512,1152]{1,0:T(8,128)(2,1)}, u32[]{:S(2)}, u32[]{:S(2)}) collective-permute-start(bf16[512,1152]{1,0:T(8,128)(2,1)} %pad_maximum_fusion.9), channel_id=1, source_target_pairs={{0,16},{8,24},{16,0},{24,8},{1,17},{9,25},{17,1},{25,9},{2,18},{10... | collective-permute-start | bytes 3538952 | tf_op jit(solution)/shard_map/ppermute | solution.py:467
  207.9 23.4 %collective-permute-start.31 = (bf16[128,1152]{1,0:T(8,128)(2,1)}, bf16[128,1152]{1,0:T(8,128)(2,1)S(1)}, u32[]{:S(2)}, u32[]{:S(2)}) collective-permute-start(bf16[128,1152]{1,0:T(8,128)(2,1)} %get-tuple-element.252), channel_id=1, source_target_pairs={{0,4},{2,6},{4,0},{6,2},{1,5},{3,7},{5,1},{7,3},{8,12},{10,14},{12... | collective-permute-start | bytes 884744 | tf_op jit(solution)/shard_map/ppermute | solution.py:470
  210.3 21.0 %collective-permute-start.32 = (bf16[128,1152]{1,0:T(8,128)(2,1)}, bf16[128,1152]{1,0:T(8,128)(2,1)S(1)}, u32[]{:S(2)}, u32[]{:S(2)}) collective-permute-start(bf16[128,1152]{1,0:T(8,128)(2,1)} %get-tuple-element.251), channel_id=1, source_target_pairs={{0,6},{2,4},{4,2},{6,0},{1,7},{3,5},{5,3},{7,1},{8,14},{10,12},{12... | collective-permute-start | bytes 884744 | tf_op jit(solution)/shard_map/ppermute | solution.py:470
  236.9 29.3 %collective-permute-start.33 = (bf16[512,1152]{1,0:T(8,128)(2,1)S(1)}, bf16[512,1152]{1,0:T(8,128)(2,1)S(1)}, u32[]{:S(2)}, u32[]{:S(2)}) collective-permute-start(bf16[512,1152]{1,0:T(8,128)(2,1)S(1)} %get-tuple-element.209.z.refs_4_), channel_id=1, source_target_pairs={{0,8},{8,0},{16,24},{24,16},{1,9},{9,1},{17,25},{25,17},{2,10},{10... | collective-permute-start | bytes 3538952 | tf_op jit(solution)/shard_map/ppermute | solution.py:467
  237.7 29.5 %collective-permute-start.35 = (bf16[512,1152]{1,0:T(8,128)(2,1)S(1)}, bf16[512,1152]{1,0:T(8,128)(2,1)S(1)}, u32[]{:S(2)}, u32[]{:S(2)}) collective-permute-start(bf16[512,1152]{1,0:T(8,128)(2,1)S(1)} %get-tuple-element.209.z.refs_4_), channel_id=1, source_target_pairs={{0,16},{8,24},{16,0},{24,8},{1,17},{9,25},{17,1},{25,9},{2,18},{10... | collective-permute-start | bytes 3538952 | tf_op jit(solution)/shard_map/ppermute | solution.py:467
  239.0 19.7 %collective-permute-start.27 = (bf16[128,1152]{1,0:T(8,128)(2,1)S(1)}, bf16[128,1152]{1,0:T(8,128)(2,1)S(1)}, u32[]{:S(2)}, u32[]{:S(2)}) collective-permute-start(bf16[128,1152]{1,0:T(8,128)(2,1)S(1)} %get-tuple-element.261), channel_id=1, source_target_pairs={{0,2},{2,0},{4,6},{6,4},{1,3},{3,1},{5,7},{7,5},{8,10},{10,8},{12,... | collective-permute-start | bytes 884744 | tf_op jit(solution)/shard_map/ppermute | solution.py:470
  242.8 21.8 %collective-permute-start.28 = (bf16[128,1152]{1,0:T(8,128)(2,1)S(1)}, bf16[128,1152]{1,0:T(8,128)(2,1)S(1)}, u32[]{:S(2)}, u32[]{:S(2)}) collective-permute-start(bf16[128,1152]{1,0:T(8,128)(2,1)S(1)} %get-tuple-element.260), channel_id=1, source_target_pairs={{0,4},{2,6},{4,0},{6,2},{1,5},{3,7},{5,1},{7,3},{8,12},{10,14},{12... | collective-permute-start | bytes 884744 | tf_op jit(solution)/shard_map/ppermute | solution.py:470
  243.8 20.8 %collective-permute-start.29 = (bf16[128,1152]{1,0:T(8,128)(2,1)S(1)}, bf16[128,1152]{1,0:T(8,128)(2,1)S(1)}, u32[]{:S(2)}, u32[]{:S(2)}) collective-permute-start(bf16[128,1152]{1,0:T(8,128)(2,1)S(1)} %get-tuple-element.259), channel_id=1, source_target_pairs={{0,6},{2,4},{4,2},{6,0},{1,7},{3,5},{5,3},{7,1},{8,14},{10,12},{12... | collective-permute-start | bytes 884744 | tf_op jit(solution)/shard_map/ppermute | solution.py:470
  266.2 17.5 %collective-permute-start.34 = (bf16[256,1152]{1,0:T(8,128)(2,1)S(1)}, bf16[256,1152]{1,0:T(8,128)(2,1)S(1)}, u32[]{:S(2)}, u32[]{:S(2)}) collective-permute-start(bf16[256,1152]{1,0:T(8,128)(2,1)S(1)} %slice.286), channel_id=1, source_target_pairs={{0,16},{8,24},{16,0},{24,8},{1,17},{9,25},{17,1},{25,9},{2,18},{10... | collective-permute-start | bytes 1769480 | tf_op jit(solution)/shard_map/ppermute | solution.py:467
  267.3 16.5 %collective-permute-start.36 = (bf16[256,1152]{1,0:T(8,128)(2,1)S(1)}, bf16[256,1152]{1,0:T(8,128)(2,1)S(1)}, u32[]{:S(2)}, u32[]{:S(2)}) collective-permute-start(bf16[256,1152]{1,0:T(8,128)(2,1)S(1)} %slice.287), channel_id=1, source_target_pairs={{0,8},{8,0},{16,24},{24,16},{1,9},{9,1},{17,25},{25,17},{2,10},{10... | collective-permute-start | bytes 1769480 | tf_op jit(solution)/shard_map/ppermute | solution.py:467
  308.5 189.7 %reduce-scatter.5.cloned.1.call-start = ((), (), s32[]{:S(2)}) async-start(), calls=%async_computation.3 | async-start | bytes 5160960 | tf_op jit(solution)/shard_map/reduce_scatter | solution.py:658
  329.7 15.4 %collective-permute-start.38 = (bf16[256,1152]{1,0:T(8,128)(2,1)S(1)}, bf16[256,1152]{1,0:T(8,128)(2,1)S(1)}, u32[]{:S(2)}, u32[]{:S(2)}) collective-permute-start(bf16[256,1152]{1,0:T(8,128)(2,1)S(1)} %get-tuple-element.242), channel_id=1, source_target_pairs={{0,16},{8,24},{16,0},{24,8},{1,17},{9,25},{17,1},{25,9},{2,18},{10... | collective-permute-start | bytes 1769480 | tf_op jit(solution)/shard_map/ppermute | solution.py:467
  330.6 16.6 %collective-permute-start.39 = (bf16[256,1152]{1,0:T(8,128)(2,1)S(1)}, bf16[256,1152]{1,0:T(8,128)(2,1)S(1)}, u32[]{:S(2)}, u32[]{:S(2)}) collective-permute-start(bf16[256,1152]{1,0:T(8,128)(2,1)S(1)} %get-tuple-element.243), channel_id=1, source_target_pairs={{0,8},{8,0},{16,24},{24,16},{1,9},{9,1},{17,25},{25,17},{2,10},{10... | collective-permute-start | bytes 1769480 | tf_op jit(solution)/shard_map/ppermute | solution.py:467
  346.3 27.5 %collective-permute-start.40 = (bf16[512,1152]{1,0:T(8,128)(2,1)}, bf16[512,1152]{1,0:T(8,128)(2,1)S(1)}, u32[]{:S(2)}, u32[]{:S(2)}) collective-permute-start(bf16[512,1152]{1,0:T(8,128)(2,1)} %pad_maximum_fusion.14), channel_id=1, source_target_pairs={{0,8},{8,0},{16,24},{24,16},{1,9},{9,1},{17,25},{25,17},{2,10},{10... | collective-permute-start | bytes 3538952 | tf_op jit(solution)/shard_map/ppermute | solution.py:467
  348.5 27.3 %collective-permute-start.41 = (bf16[512,1152]{1,0:T(8,128)(2,1)}, bf16[512,1152]{1,0:T(8,128)(2,1)}, u32[]{:S(2)}, u32[]{:S(2)}) collective-permute-start(bf16[512,1152]{1,0:T(8,128)(2,1)} %pad_maximum_fusion.15), channel_id=1, source_target_pairs={{0,16},{8,24},{16,0},{24,8},{1,17},{9,25},{17,1},{25,9},{2,18},{10... | collective-permute-start | bytes 3538952 | tf_op jit(solution)/shard_map/ppermute | solution.py:467
  378.9 18.4 %collective-permute-start.43 = (bf16[4,4,72,896]{3,2,1,0:T(8,128)(2,1)}, bf16[4,4,72,896]{3,2,1,0:T(8,128)(2,1)S(1)}, u32[]{:S(2)}, u32[]{:S(2)}) collective-permute-start(bf16[4,4,72,896]{3,2,1,0:T(8,128)(2,1)} %get-tuple-element.166), channel_id=1, source_target_pairs={{0,1},{1,0},{2,3},{3,2},{4,5},{5,4},{6,7},{7,6},{8,9},{9,8},{10,11... | collective-permute-start | bytes 6193160 | tf_op jit(solution)/shard_map/ppermute | solution.py:473
  404.2 136.1 %all-gather.8.cloned.1.call-start = ((), (), s32[]{:S(2)}) async-start(), calls=%async_computation.5 | async-start | bytes 2488320 | tf_op jit(solution)/shard_map/all_gather | solution.py:669
  441.9 22.9 %collective-permute-start.48 = (bf16[1152,512]{1,0:T(8,128)(2,1)}, bf16[1152,512]{1,0:T(8,128)(2,1)}, u32[]{:S(2)}, u32[]{:S(2)}) collective-permute-start(bf16[1152,512]{1,0:T(8,128)(2,1)} %slice.290), channel_id=1, source_target_pairs={{0,1},{1,0},{2,3},{3,2},{4,5},{5,4},{6,7},{7,6},{8,9},{9,8},{10,11... | collective-permute-start | bytes 3538952 | tf_op jit(solution)/shard_map/ppermute | solution.py:473
  442.7 195.9 %all-gather.6.cloned.1.call-start = ((), (), s32[]{:S(2)}) async-start(), calls=%async_computation.4 | async-start | bytes 5160960 | tf_op jit(solution)/shard_map/all_gather | solution.py:664
  448.4 16.4 %collective-permute-start.47 = (bf16[512,512]{1,0:T(8,128)(2,1)}, bf16[512,512]{1,0:T(8,128)(2,1)}, u32[]{:S(2)}, u32[]{:S(2)}) collective-permute-start(bf16[512,512]{1,0:T(8,128)(2,1)} %bitcast.59), channel_id=1, source_target_pairs={{0,1},{1,0},{2,3},{3,2},{4,5},{5,4},{6,7},{7,6},{8,9},{9,8},{10,11... | collective-permute-start | bytes 1572872 | tf_op jit(solution)/shard_map/ppermute | solution.py:473
  534.3 35.7 %collective-permute-start.64 = (bf16[512,768]{1,0:T(8,128)(2,1)}, bf16[512,768]{1,0:T(8,128)(2,1)}, u32[]{:S(2)}, u32[]{:S(2)}) collective-permute-start(bf16[512,768]{1,0:T(8,128)(2,1)} %pad_maximum_fusion.27), channel_id=1, source_target_pairs={{0,2},{6,4},{1,3},{7,5},{8,10},{14,12},{9,11},{15,13},{16,18},{22,... | collective-permute-start | bytes 2359304 | tf_op jit(solution)/shard_map/ppermute | solution.py:515
  540.3 37.7 %collective-permute-start.69 = (bf16[864,1152]{1,0:T(8,128)(2,1)}, bf16[864,1152]{1,0:T(8,128)(2,1)}, u32[]{:S(2)}, u32[]{:S(2)}) collective-permute-start(bf16[864,1152]{1,0:T(8,128)(2,1)} %all-gather.8.cloned.1.call-done), channel_id=1, source_target_pairs={{0,1},{1,0},{2,3},{3,2},{4,5},{5,4},{6,7},{7,6},{8,9},{9,8},{10,11... | collective-permute-start | bytes 5971976 | tf_op jit(solution)/shard_map/ppermute | solution.py:473
  576.6 61.8 %collective-permute-start.66 = (bf16[512,768]{1,0:T(8,128)(2,1)S(1)}, bf16[512,768]{1,0:T(8,128)(2,1)S(1)}, u32[]{:S(2)}, u32[]{:S(2)}) collective-permute-start(bf16[512,768]{1,0:T(8,128)(2,1)S(1)} %add.381), channel_id=1, source_target_pairs={{2,0},{4,6},{3,1},{5,7},{10,8},{12,14},{11,9},{13,15},{18,16},{20,... | collective-permute-start | bytes 2359304 | tf_op jit(solution)/shard_map/ppermute | solution.py:525
  638.6 34.3 %collective-permute-start.68 = (bf16[4,4,2,72,896]{4,3,2,1,0:T(8,128)(2,1)}, bf16[4,4,2,72,896]{4,3,2,1,0:T(8,128)(2,1)}, u32[]{:S(2)}, u32[]{:S(2)}) collective-permute-start(bf16[4,4,2,72,896]{4,3,2,1,0:T(8,128)(2,1)} %bitcast.240), channel_id=1, source_target_pairs={{0,1},{1,0},{2,3},{3,2},{4,5},{5,4},{6,7},{7,6},{8,9},{9,8},{10,11... | collective-permute-start | bytes 12386312 | tf_op jit(solution)/shard_map/ppermute | solution.py:473
  647.9 23.5 %collective-permute-start.57 = (bf16[128,1152]{1,0:T(8,128)(2,1)S(1)}, bf16[128,1152]{1,0:T(8,128)(2,1)S(1)}, u32[]{:S(2)}, u32[]{:S(2)}) collective-permute-start(bf16[128,1152]{1,0:T(8,128)(2,1)S(1)} %get-tuple-element.238), channel_id=1, source_target_pairs={{0,4},{2,6},{4,0},{6,2},{1,5},{3,7},{5,1},{7,3},{8,12},{10,14},{12... | collective-permute-start | bytes 884744 | tf_op jit(solution)/shard_map/ppermute | solution.py:470
  648.8 22.6 %collective-permute-start.58 = (bf16[128,1152]{1,0:T(8,128)(2,1)S(1)}, bf16[128,1152]{1,0:T(8,128)(2,1)S(1)}, u32[]{:S(2)}, u32[]{:S(2)}) collective-permute-start(bf16[128,1152]{1,0:T(8,128)(2,1)S(1)} %get-tuple-element.237), channel_id=1, source_target_pairs={{0,6},{2,4},{4,2},{6,0},{1,7},{3,5},{5,3},{7,1},{8,14},{10,12},{12... | collective-permute-start | bytes 884744 | tf_op jit(solution)/shard_map/ppermute | solution.py:470
  (147 other events, 1263.9 us)
Sparse Core Ops, SparseCore 0:
  10.5 40.2 all-gather.3
  308.6 43.6 reduce-scatter.6
  404.3 77.3 reduce-scatter.4
  483.3 44.4 all-gather.7
  529.8 95.4 all-gather.5
